TPU v7x, 32 devices: a whole 2x2x4 slice. The times are simulated.
32 devices in a mesh: row: 8 (over y, x, core), col: 4 (over z).
Axes of the slice: x: 2, y: 2, z: 4, core: 2. Of those that a mesh axis runs over, the one named last changes fastest.
Arguments:
- tokens: bfloat16 [4, 4096, 1792], P(None, ('row', 'col')), may hold values from -12 to 12
- lengths: int32 [4, 8], replicated, may hold values from 1 to 1024, 4096 in all within a row
- permutation: int32 [4, 32], replicated, may hold values from 0 to 31, each once within a row
- cotangent: bfloat16 [4, 4096, 1792], P(None, ('row', 'col')), may hold values from -12 to 12
- norm1_gain: float32 [1792], replicated, may hold values from 0.5 to 1.5
- mixer_in: bfloat16 [1792, 1792], P('row', 'col'), may hold values from -0.125 to 0.125
- mixer_gate: bfloat16 [1792, 1792], P('row', 'col'), may hold values from -0.125 to 0.125
- conv_kernel: float32 [3, 1792], P(None, 'col'), may hold values from -2.5 to 2.5
- mixer_out: bfloat16 [1792, 1792], P('row', 'col'), may hold values from -0.125 to 0.125
- norm2_gain: float32 [1792], replicated, may hold values from 0.5 to 1.5
- ffn_gate: bfloat16 [1792, 4864], P('row', 'col'), may hold values from -0.125 to 0.125
- ffn_up: bfloat16 [1792, 4864], P('row', 'col'), may hold values from -0.125 to 0.125
- ffn_down: bfloat16 [1792, 4864], P('row', 'col'), may hold values from -0.078125 to 0.078125
Outputs:
- output: bfloat16 [4, 4096, 1792], P(None, ('row', 'col'))
- input_grad: float32 [4, 4096, 1792], P(None, ('row', 'col'))
- norm1_gain_grad: float32 [1792], P(('row', 'col'))
- mixer_in_grad: float32 [1792, 1792], P('row', 'col')
- mixer_gate_grad: float32 [1792, 1792], P('row', 'col')
- conv_kernel_grad: float32 [3, 1792], P(None, ('col', 'row'))
- mixer_out_grad: float32 [1792, 1792], P('row', 'col')
- norm2_gain_grad: float32 [1792], P(('row', 'col'))
- ffn_gate_grad: float32 [1792, 4864], P('row', 'col')
- ffn_up_grad: float32 [1792, 4864], P('row', 'col')
- ffn_down_grad: float32 [1792, 4864], P('row', 'col')
Inputs may be any that keep to these rules, and one draw needn't show every extreme that they name: Each row of lengths sums to 4096, and its largest entry is exactly 1024. `permutation`: each row holds every number of 0 to 31 once.
All inputs are finite; a program needn't handle non-finite values.
Results may differ from a plain program's by a relative error of at most 0.0083.
Values may be sent and summed in bfloat16 or wider, within the bound.
No kernel may reach another device: no remote copies, remote signals or barrier semaphores. Data moves between devices by JAX's collectives and lax.ppermute only.
A program may use at most 160 MiB of HBM per device.

v0:
```python
import jax
import jax.numpy as jnp
from jax import lax
from jax.sharding import PartitionSpec as P

BLOCK = 128


EPSILON = 1e-05


def contract_last(left, right):
    return lax.dot_general(
        left, right, (((1,), (1,)), ((), ())), preferred_element_type=jnp.float32
    )


def contract_first(left, right):
    return lax.dot_general(
        left, right, (((0,), (0,)), ((), ())), preferred_element_type=jnp.float32
    )


def spread(shard):
    return lax.all_gather(shard, "col", axis=0, tiled=True)


def spread_grad(shard):
    return lax.all_gather(shard, "col", axis=0, tiled=True)


def collect(partial_sum):
    return lax.psum_scatter(partial_sum, "col", scatter_dimension=0, tiled=True)


def collect_grad(partial_sum):
    return lax.psum_scatter(partial_sum, "col", scatter_dimension=0, tiled=True)


def per_device(
    tokens,
    lengths,
    permutation,
    cotangent,
    norm1_gain,
    mixer_in,
    mixer_gate,
    conv_kernel,
    mixer_out,
    norm2_gain,
    ffn_gate,
    ffn_up,
    ffn_down,
):
    micro_count, rows_local, full_width = tokens.shape
    group_rows = rows_local * lax.axis_size("col")
    block_size = BLOCK
    blocks_local = group_rows // block_size
    blocks_all = permutation.shape[1]
    row_index = lax.axis_index("row")
    width_local = conv_kernel.shape[1]
    within = jnp.arange(block_size, dtype=jnp.int32)
    blocks_range = jnp.arange(blocks_all, dtype=jnp.int32)
    outputs = []
    input_grads = []
    totals = None
    for micro_index in range(micro_count):
        gathered = (
            lax.all_gather(mixer_in, "row", axis=0, tiled=True),
            lax.all_gather(mixer_gate, "row", axis=0, tiled=True),
            lax.all_gather(ffn_gate, "row", axis=0, tiled=True),
            lax.all_gather(ffn_up, "row", axis=0, tiled=True),
            lax.all_gather(mixer_out, "row", axis=0, tiled=True),
            lax.all_gather(ffn_down, "row", axis=0, tiled=True),
        )
        w_in, w_gate, w_ffg, w_ffu, w_out, w_down = gathered
        local_in = tokens[micro_index].astype(jnp.float32)
        local_cot = cotangent[micro_index]
        dealt_order = permutation[micro_index]
        seq_len = lengths[micro_index]
        offsets = jnp.cumsum(seq_len) - seq_len
        own_blocks = lax.dynamic_slice_in_dim(dealt_order, row_index * blocks_local, blocks_local)
        inverse = jnp.sum(
            jnp.where(dealt_order[None, :] == blocks_range[:, None], blocks_range[None, :], 0),
            axis=1,
        )
        source = jnp.take(inverse, jnp.maximum(own_blocks - 1, 0))
        position = (own_blocks[:, None] * block_size + within[None, :]).reshape(-1)
        is_start = jnp.any(position[:, None] == offsets[None, :], axis=1)
        was_start = jnp.any(position[:, None] - 1 == offsets[None, :], axis=1)
        keep_one = jnp.where(is_start, 0.0, 1.0).astype(jnp.float32)[:, None]
        keep_two = jnp.where(is_start | was_start, 0.0, 1.0).astype(jnp.float32)[:, None]
        scale_one = lax.rsqrt(jnp.mean(local_in * local_in, axis=1, keepdims=True) + EPSILON)
        normed_one = local_in * scale_one
        hidden_one = spread((normed_one * norm1_gain).astype(jnp.bfloat16))
        signal = jnp.dot(hidden_one, w_in, preferred_element_type=jnp.float32)
        gating = jnp.dot(hidden_one, w_gate, preferred_element_type=jnp.float32)
        signal_blocks = signal.reshape(blocks_local, block_size, width_local)
        tails_all = lax.all_gather(signal_blocks[:, block_size - 2 :, :], "row", axis=0, tiled=True)
        before = jnp.take(tails_all, source, axis=0)
        extended = jnp.concatenate([before, signal_blocks], axis=1)
        shift_one = keep_one * extended[:, 1 : block_size + 1, :].reshape(group_rows, width_local)
        shift_two = keep_two * extended[:, 0:block_size, :].reshape(group_rows, width_local)
        mixed_sig = (
            conv_kernel[0] * signal + conv_kernel[1] * shift_one + conv_kernel[2] * shift_two
        )
        product = (mixed_sig * gating).astype(jnp.bfloat16)
        branch = collect(contract_last(product, w_out))
        residual = local_in + branch
        scale_two = lax.rsqrt(jnp.mean(residual * residual, axis=1, keepdims=True) + EPSILON)
        normed_two = residual * scale_two
        hidden_two = spread((normed_two * norm2_gain).astype(jnp.bfloat16))
        gate_val = jnp.dot(hidden_two, w_ffg, preferred_element_type=jnp.float32)
        up_val = jnp.dot(hidden_two, w_ffu, preferred_element_type=jnp.float32)
        sigmoid_gate = jax.nn.sigmoid(gate_val)
        activated = (gate_val * sigmoid_gate * up_val).astype(jnp.bfloat16)
        ffn_result = collect(contract_last(activated, w_down))
        outputs.append((residual + ffn_result).astype(jnp.bfloat16))
        grad_full = spread_grad(local_cot)
        grad_act = jnp.dot(grad_full, w_down, preferred_element_type=jnp.float32)
        grad_down = contract_first(grad_full, activated)
        silu_slope = sigmoid_gate * (1.0 + gate_val * (1.0 - sigmoid_gate))
        grad_gate = (grad_act * up_val * silu_slope).astype(jnp.bfloat16)
        grad_up = (grad_act * gate_val * sigmoid_gate).astype(jnp.bfloat16)
        grad_ffg = contract_first(hidden_two, grad_gate)
        grad_ffu = contract_first(hidden_two, grad_up)
        grad_hidden_two = collect_grad(
            contract_last(grad_gate, w_ffg) + contract_last(grad_up, w_ffu)
        )
        grad_gain_two = jnp.sum(grad_hidden_two * normed_two, axis=0)
        grad_norm_two = grad_hidden_two * norm2_gain
        inner_two = jnp.mean(grad_norm_two * normed_two, axis=1, keepdims=True)
        grad_residual = local_cot.astype(jnp.float32) + scale_two * (
            grad_norm_two - normed_two * inner_two
        )
        grad_branch = spread_grad(grad_residual.astype(jnp.bfloat16))
        grad_product = jnp.dot(grad_branch, w_out, preferred_element_type=jnp.float32)
        grad_out_w = contract_first(grad_branch, product)
        grad_mixed = grad_product * gating
        grad_gating = (grad_product * mixed_sig).astype(jnp.bfloat16)
        grad_kernel = jnp.stack(
            [
                jnp.sum(grad_mixed * signal, axis=0),
                jnp.sum(grad_mixed * shift_one, axis=0),
                jnp.sum(grad_mixed * shift_two, axis=0),
            ]
        )
        into_one = (conv_kernel[1] * keep_one * grad_mixed).reshape(
            blocks_local, block_size, width_local
        )
        into_two = (conv_kernel[2] * keep_two * grad_mixed).reshape(
            blocks_local, block_size, width_local
        )
        grad_extended = jnp.pad(into_one, ((0, 0), (1, 1), (0, 0))) + jnp.pad(
            into_two, ((0, 0), (0, 2), (0, 0))
        )
        grad_before = grad_extended[:, :2, :]
        grad_blocks = grad_extended[:, 2:, :] + (conv_kernel[0] * grad_mixed).reshape(
            blocks_local, block_size, width_local
        )
        chooser = (source[:, None] == blocks_range[None, :]).astype(jnp.float32)
        tail_terms = jnp.einsum("jn,jtd->ntd", chooser, grad_before)
        returned = lax.psum_scatter(
            tail_terms.astype(jnp.bfloat16), "row", scatter_dimension=0, tiled=True
        ).astype(jnp.float32)
        grad_blocks = jnp.concatenate(
            [grad_blocks[:, : block_size - 2, :], grad_blocks[:, block_size - 2 :, :] + returned],
            axis=1,
        )
        grad_signal = grad_blocks.reshape(group_rows, width_local).astype(jnp.bfloat16)
        grad_in_w = contract_first(hidden_one, grad_signal)
        grad_gate_w = contract_first(hidden_one, grad_gating)
        grad_hidden_one = collect_grad(
            contract_last(grad_signal, w_in) + contract_last(grad_gating, w_gate)
        )
        grad_gain_one = jnp.sum(grad_hidden_one * normed_one, axis=0)
        grad_norm_one = grad_hidden_one * norm1_gain
        inner_one = jnp.mean(grad_norm_one * normed_one, axis=1, keepdims=True)
        input_grads.append(grad_residual + scale_one * (grad_norm_one - normed_one * inner_one))
        partials = (
            grad_gain_one,
            grad_in_w,
            grad_gate_w,
            grad_kernel,
            grad_out_w,
            grad_gain_two,
            grad_ffg,
            grad_ffu,
            grad_down,
        )
        partials = (
            lax.psum_scatter(partials[0], "row", scatter_dimension=0, tiled=True),
            lax.psum_scatter(partials[1], "row", scatter_dimension=0, tiled=True),
            lax.psum_scatter(partials[2], "row", scatter_dimension=0, tiled=True),
            lax.psum_scatter(partials[3], "row", scatter_dimension=1, tiled=True),
            lax.psum_scatter(partials[4], "row", scatter_dimension=0, tiled=True),
            lax.psum_scatter(partials[5], "row", scatter_dimension=0, tiled=True),
            lax.psum_scatter(partials[6], "row", scatter_dimension=0, tiled=True),
            lax.psum_scatter(partials[7], "row", scatter_dimension=0, tiled=True),
            lax.psum_scatter(partials[8], "row", scatter_dimension=0, tiled=True),
        )
        if totals is None:
            totals = tuple(partials)
        else:
            totals = tuple((left_val + right_val for left_val, right_val in zip(totals, partials)))
    gain_one_total, gain_two_total = (
        lax.psum_scatter(totals[0], "col", scatter_dimension=0, tiled=True),
        lax.psum_scatter(totals[5], "col", scatter_dimension=0, tiled=True),
    )
    return (
        jnp.stack(outputs),
        jnp.stack(input_grads),
        gain_one_total,
        totals[1],
        totals[2],
        totals[3],
        totals[4],
        gain_two_total,
        totals[6],
        totals[7],
        totals[8],
    )


def solution(mesh):
    placed = (
        P(None, ("row", "col"), None),
        P(),
        P(),
        P(None, ("row", "col"), None),
        P(),
        P("row", "col"),
        P("row", "col"),
        P(None, "col"),
        P("row", "col"),
        P(),
        P("row", "col"),
        P("row", "col"),
        P("row", "col"),
    )
    return jax.shard_map(
        per_device,
        mesh=mesh,
        in_specs=placed,
        out_specs=(
            P(None, ("row", "col"), None),
            P(None, ("row", "col"), None),
            P(("row", "col")),
            P("row", "col"),
            P("row", "col"),
            P(None, ("col", "row")),
            P("row", "col"),
            P(("row", "col")),
            P("row", "col"),
            P("row", "col"),
            P("row", "col"),
        ),
        check_vma=False,
    )
```

profile of v0, /device:TPU:30, one launch (start us, length us, event | category | flops | bytes accessed | tf_op | source)
XLA Modules:
  0.0 2549.4 jit_solution(138353777836643099)
XLA Ops:
  18.1 33.3 %all-gather.27.cloned.1.call-done = bf16[512,1792]{1,0:T(8,128)(2,1)} async-done(((bf16[128,1792]{1,0:T(8,128)(2,1)}), bf16[512,1792]{1,0:T(8,128)(2,1)}) %all-gather.27.cloned.1.call-update) | async-done | bytes 1835024 | tf_op jit(solution)/shard_map/all_gather | solution.py:25
  51.3 28.8 %all-gather.29.cloned.1.call-done = bf16[1792,448]{1,0:T(8,128)(2,1)} async-done(((bf16[224,448]{1,0:T(8,128)(2,1)}), bf16[1792,448]{1,0:T(8,128)(2,1)}) %all-gather.29.cloned.1.call-update) | async-done | bytes 1605648 | tf_op jit(solution)/shard_map/all_gather | solution.py:69
  88.7 9.2 all_gather.98
  99.8 22.7 all-gather.43.cloned.1.call-done
  130.4 8.7 all_gather.106
  160.5 19.6 all-gather.33.cloned.1.call-done
  187.4 34.9 %all-gather.47.cloned.1.call-done = bf16[512,1792]{1,0:T(8,128)(2,1)} async-done(((bf16[128,1792]{1,0:T(8,128)(2,1)}), bf16[512,1792]{1,0:T(8,128)(2,1)}) %all-gather.47.cloned.1.call-update) | async-done | bytes 1835024 | tf_op jit(solution)/shard_map/all_gather | solution.py:25
  230.8 8.4 all_gather.109
  241.2 23.0 all-gather.51.cloned.1.call-done
  275.0 8.3 all_gather.112
  309.1 26.7 %reduce-scatter.30.cloned.1.call-done = f32[128,1792]{1,0:T(8,128)} async-done(((f32[512,1792]{1,0:T(8,128)}), f32[128,1792]{1,0:T(8,128)}) %reduce-scatter.30.cloned.1.call-update) | async-done | bytes 917520 | tf_op jit(solution)/shard_map/reduce_scatter | solution.py:33
  335.8 71.1 %reduce-scatter.38.cloned.1.call-done = f32[128,1792]{1,0:T(8,128)} async-done(((f32[512,1792]{1,0:T(8,128)}), f32[128,1792]{1,0:T(8,128)}) %reduce-scatter.38.cloned.1.call-update) | async-done | bytes 917520 | tf_op jit(solution)/shard_map/reduce_scatter | solution.py:33
  406.9 71.0 %reduce-scatter.42.cloned.1.call-done = f32[128,1792]{1,0:T(8,128)} async-done(((f32[512,1792]{1,0:T(8,128)}), f32[128,1792]{1,0:T(8,128)}) %reduce-scatter.42.cloned.1.call-update) | async-done | bytes 917520 | tf_op jit(solution)/shard_map/reduce_scatter | solution.py:33
  477.9 71.1 %reduce-scatter.34.cloned.1.call-done = f32[128,1792]{1,0:T(8,128)} async-done(((f32[512,1792]{1,0:T(8,128)}), f32[128,1792]{1,0:T(8,128)}) %reduce-scatter.34.cloned.1.call-update) | async-done | bytes 917520 | tf_op jit(solution)/shard_map/reduce_scatter | solution.py:33
  561.0 28.3 %all-gather.37.cloned.1.call-done = bf16[1792,1216]{1,0:T(8,128)(2,1)} async-done(((bf16[224,1216]{1,0:T(8,128)(2,1)}), bf16[1792,1216]{1,0:T(8,128)(2,1)}) %all-gather.37.cloned.1.call-update) | async-done | bytes 4358160 | tf_op jit(solution)/shard_map/all_gather | solution.py:71
  589.3 42.4 %all-gather.49.cloned.1.call-done = bf16[512,1792]{1,0:T(8,128)(2,1)} async-done(((bf16[128,1792]{1,0:T(8,128)(2,1)}), bf16[512,1792]{1,0:T(8,128)(2,1)}) %all-gather.49.cloned.1.call-update) | async-done | bytes 1835024 | tf_op jit(solution)/shard_map/all_gather | solution.py:25
  638.4 33.4 %all-gather.39.cloned.1.call-done = bf16[1792,1216]{1,0:T(8,128)(2,1)} async-done(((bf16[224,1216]{1,0:T(8,128)(2,1)}), bf16[1792,1216]{1,0:T(8,128)(2,1)}) %all-gather.39.cloned.1.call-update) | async-done | bytes 4358160 | tf_op jit(solution)/shard_map/all_gather | solution.py:72
  671.9 6.8 fusion.149
  678.6 34.9 %all-gather.67.cloned.1.call-done = bf16[1,512,1792]{2,1,0:T(8,128)(2,1)} async-done(((bf16[1,128,1792]{2,1,0:T(8,128)(2,1)}), bf16[1,512,1792]{2,1,0:T(8,128)(2,1)}) %all-gather.67.cloned.1.call-update) | async-done | bytes 1835024 | tf_op jit(solution)/shard_map/all_gather | solution.py:29
  713.5 40.2 %all-gather.41.cloned.1.call-done = bf16[1792,1216]{1,0:T(8,128)(2,1)} async-done(((bf16[224,1216]{1,0:T(8,128)(2,1)}), bf16[1792,1216]{1,0:T(8,128)(2,1)}) %all-gather.41.cloned.1.call-update) | async-done | bytes 4358160 | tf_op jit(solution)/shard_map/all_gather | solution.py:74
  753.7 8.9 multiply_convert_fusion.2
  773.5 22.5 all-gather.35.cloned.1.call-done
  796.0 6.9 fusion.137
  809.1 28.6 %all-gather.63.cloned.1.call-done = bf16[1,512,1792]{2,1,0:T(8,128)(2,1)} async-done(((bf16[1,128,1792]{2,1,0:T(8,128)(2,1)}), bf16[1,512,1792]{2,1,0:T(8,128)(2,1)}) %all-gather.63.cloned.1.call-update) | async-done | bytes 1835024 | tf_op jit(solution)/shard_map/all_gather | solution.py:29
  837.7 8.9 multiply_convert_fusion.6
  852.7 7.2 convolution_add_fusion.10
  860.0 49.3 %reduce-scatter.54.cloned.1.call-done = f32[128,1792]{1,0:T(8,128)} async-done(((f32[512,1792]{1,0:T(8,128)}), f32[128,1792]{1,0:T(8,128)}) %reduce-scatter.54.cloned.1.call-update) | async-done | bytes 917520 | tf_op jit(solution)/shard_map/reduce_scatter | solution.py:37
  909.3 71.0 %reduce-scatter.46.cloned.1.call-done = f32[128,1792]{1,0:T(8,128)} async-done(((f32[512,1792]{1,0:T(8,128)}), f32[128,1792]{1,0:T(8,128)}) %reduce-scatter.46.cloned.1.call-update) | async-done | bytes 917520 | tf_op jit(solution)/shard_map/reduce_scatter | solution.py:37
  986.8 38.4 %all-gather.45.cloned.1.call-done = bf16[512,1792]{1,0:T(8,128)(2,1)} async-done(((bf16[128,1792]{1,0:T(8,128)(2,1)}), bf16[512,1792]{1,0:T(8,128)(2,1)}) %all-gather.45.cloned.1.call-update) | async-done | bytes 1835024 | tf_op jit(solution)/shard_map/all_gather | solution.py:25
  1025.1 6.9 fusion.143
  1038.3 28.7 %all-gather.65.cloned.1.call-done = bf16[1,512,1792]{2,1,0:T(8,128)(2,1)} async-done(((bf16[1,128,1792]{2,1,0:T(8,128)(2,1)}), bf16[1,512,1792]{2,1,0:T(8,128)(2,1)}) %all-gather.65.cloned.1.call-update) | async-done | bytes 1835024 | tf_op jit(solution)/shard_map/all_gather | solution.py:29
  1067.0 8.9 multiply_convert_fusion.4
  1081.9 7.0 convolution_add_fusion.9
  1089.0 19.9 all-gather.53.cloned.1.call-done
  1108.9 6.9 fusion.154
  1122.0 28.6 %all-gather.69.cloned.1.call-done = bf16[1,512,1792]{2,1,0:T(8,128)(2,1)} async-done(((bf16[1,128,1792]{2,1,0:T(8,128)(2,1)}), bf16[1,512,1792]{2,1,0:T(8,128)(2,1)}) %all-gather.69.cloned.1.call-update) | async-done | bytes 1835024 | tf_op jit(solution)/shard_map/all_gather | solution.py:29
  1150.6 8.9 multiply_convert_fusion
  1165.6 7.0 convolution_add_fusion.7
  1172.7 7.2 fusion.145
  1180.0 7.2 fusion.156
  1187.3 35.0 %reduce-scatter.50.cloned.1.call-done = f32[128,1792]{1,0:T(8,128)} async-done(((f32[512,1792]{1,0:T(8,128)}), f32[128,1792]{1,0:T(8,128)}) %reduce-scatter.50.cloned.1.call-update) | async-done | bytes 917520 | tf_op jit(solution)/shard_map/reduce_scatter | solution.py:37
  1222.2 71.0 %reduce-scatter.58.cloned.1.call-done = f32[128,1792]{1,0:T(8,128)} async-done(((f32[512,1792]{1,0:T(8,128)}), f32[128,1792]{1,0:T(8,128)}) %reduce-scatter.58.cloned.1.call-update) | async-done | bytes 917520 | tf_op jit(solution)/shard_map/reduce_scatter | solution.py:37
  1297.7 66.5 %reduce-scatter.36.cloned.1.call-done = f32[128,1792]{1,0:T(8,128)} async-done(((f32[512,1792]{1,0:T(8,128)}), f32[128,1792]{1,0:T(8,128)}) %reduce-scatter.36.cloned.1.call-update) | async-done | bytes 917520 | tf_op jit(solution)/shard_map/reduce_scatter | solution.py:33
  1364.2 71.1 %reduce-scatter.44.cloned.1.call-done = f32[128,1792]{1,0:T(8,128)} async-done(((f32[512,1792]{1,0:T(8,128)}), f32[128,1792]{1,0:T(8,128)}) %reduce-scatter.44.cloned.1.call-update) | async-done | bytes 917520 | tf_op jit(solution)/shard_map/reduce_scatter | solution.py:33
  1444.8 36.7 %all-gather.61.cloned.1.call-done = bf16[512,1792]{1,0:T(8,128)(2,1)} async-done(((bf16[128,1792]{1,0:T(8,128)(2,1)}), bf16[512,1792]{1,0:T(8,128)(2,1)}) %all-gather.61.cloned.1.call-update) | async-done | bytes 1835024 | tf_op jit(solution)/shard_map/all_gather | solution.py:29
  1487.2 35.9 %all-gather.57.cloned.1.call-done = bf16[512,1792]{1,0:T(8,128)(2,1)} async-done(((bf16[128,1792]{1,0:T(8,128)(2,1)}), bf16[512,1792]{1,0:T(8,128)(2,1)}) %all-gather.57.cloned.1.call-update) | async-done | bytes 1835024 | tf_op jit(solution)/shard_map/all_gather | solution.py:29
  1528.6 36.5 %all-gather.59.cloned.1.call-done = bf16[512,1792]{1,0:T(8,128)(2,1)} async-done(((bf16[128,1792]{1,0:T(8,128)(2,1)}), bf16[512,1792]{1,0:T(8,128)(2,1)}) %all-gather.59.cloned.1.call-update) | async-done | bytes 1835024 | tf_op jit(solution)/shard_map/all_gather | solution.py:29
  1570.9 36.6 %all-gather.55.cloned.1.call-done = bf16[512,1792]{1,0:T(8,128)(2,1)} async-done(((bf16[128,1792]{1,0:T(8,128)(2,1)}), bf16[512,1792]{1,0:T(8,128)(2,1)}) %all-gather.55.cloned.1.call-update) | async-done | bytes 1835024 | tf_op jit(solution)/shard_map/all_gather | solution.py:29
  1662.6 50.2 %all-reduce.22.cloned.1.call-done = (bf16[32,2,448]{2,0,1:T(8,128)(2,1)}, bf16[32,2,448]{2,0,1:T(8,128)(2,1)}, bf16[32,2,448]{2,0,1:T(8,128)(2,1)}, bf16[32,2,448]{2,0,1:T(8,128)(2,1)}) async-done(((bf16[32,2,448]{2,0,1:T(8,128)(2,1)}, bf16[32,2,448]{2,0,1:T(8,128)(2,1)}, bf16[32,2,448]{2,0,1:T(8,128)(2,1)}, bf16[32,2,448]{2,0,1:T(8,128)(2,1)}), (bf16[32,2,448]{2,0,1:T(8,128)(2,1)}, ...) | async-done | bytes 229392
  1802.8 12.7 add_add_fusion.1
  1832.9 12.9 add_add_fusion
  1862.2 10.8 copy.122
  1906.0 25.8 %reduce-scatter.52.cloned.1.call-done = f32[128,1792]{1,0:T(8,128)} async-done(((f32[512,1792]{1,0:T(8,128)}), f32[128,1792]{1,0:T(8,128)}) %reduce-scatter.52.cloned.1.call-update) | async-done | bytes 917520 | tf_op jit(solution)/shard_map/reduce_scatter | solution.py:37
  1931.8 71.1 %reduce-scatter.48.cloned.1.call-done = f32[128,1792]{1,0:T(8,128)} async-done(((f32[512,1792]{1,0:T(8,128)}), f32[128,1792]{1,0:T(8,128)}) %reduce-scatter.48.cloned.1.call-update) | async-done | bytes 917520 | tf_op jit(solution)/shard_map/reduce_scatter | solution.py:37
  2006.0 21.8 all-reduce.17
  2027.9 8.6 all-reduce.18
  2038.3 36.0 %reduce-scatter.40.cloned.1.call-done = f32[128,1792]{1,0:T(8,128)} async-done(((f32[512,1792]{1,0:T(8,128)}), f32[128,1792]{1,0:T(8,128)}) %reduce-scatter.40.cloned.1.call-update) | async-done | bytes 917520 | tf_op jit(solution)/shard_map/reduce_scatter | solution.py:33
  2077.9 67.5 %reduce-scatter.32.cloned.1.call-done = f32[128,1792]{1,0:T(8,128)} async-done(((f32[512,1792]{1,0:T(8,128)}), f32[128,1792]{1,0:T(8,128)}) %reduce-scatter.32.cloned.1.call-update) | async-done | bytes 917520 | tf_op jit(solution)/shard_map/reduce_scatter | solution.py:33
  2155.8 69.4 %reduce-scatter.68.cloned.1.call-done = f32[224,1216]{1,0:T(8,128)} async-done(((f32[1792,1216]{1,0:T(8,128)}), f32[224,1216]{1,0:T(8,128)}) %reduce-scatter.68.cloned.1.call-update) | async-done | bytes 1089552 | tf_op jit(solution)/shard_map/reduce_scatter | solution.py:198
  2225.3 79.3 %reduce-scatter.70.cloned.1.call-done = f32[224,1216]{1,0:T(8,128)} async-done(((f32[1792,1216]{1,0:T(8,128)}), f32[224,1216]{1,0:T(8,128)}) %reduce-scatter.70.cloned.1.call-update) | async-done | bytes 1089552 | tf_op jit(solution)/shard_map/reduce_scatter | solution.py:199
  2304.6 79.7 %reduce-scatter.72.cloned.1.call-done = f32[224,1216]{1,0:T(8,128)} async-done(((f32[1792,1216]{1,0:T(8,128)}), f32[224,1216]{1,0:T(8,128)}) %reduce-scatter.72.cloned.1.call-update) | async-done | bytes 1089552
  2384.3 52.6 %reduce-scatter.64.cloned.1.call-done = f32[224,448]{1,0:T(8,128)} async-done(((f32[1792,448]{1,0:T(8,128)}), f32[224,448]{1,0:T(8,128)}) %reduce-scatter.64.cloned.1.call-update) | async-done | bytes 401424 | tf_op jit(solution)/shard_map/reduce_scatter | solution.py:194
  2436.9 53.2 %reduce-scatter.66.cloned.1.call-done = f32[224,448]{1,0:T(8,128)} async-done(((f32[1792,448]{1,0:T(8,128)}), f32[224,448]{1,0:T(8,128)}) %reduce-scatter.66.cloned.1.call-update) | async-done | bytes 401424 | tf_op jit(solution)/shard_map/reduce_scatter | solution.py:196
  2490.0 52.6 %reduce-scatter.62.cloned.1.call-done = f32[224,448]{1,0:T(8,128)} async-done(((f32[1792,448]{1,0:T(8,128)}), f32[224,448]{1,0:T(8,128)}) %reduce-scatter.62.cloned.1.call-update) | async-done | bytes 401424 | tf_op jit(solution)/shard_map/reduce_scatter | solution.py:193
  (684 shorter events, 435.3 us)
Async XLA Ops:
  7.2 44.1 %all-gather.27.cloned.1.call-start = ((), (), s32[]{:S(2)}) async-start(), calls=%async_computation.22 | async-start | bytes 2293760 | tf_op jit(solution)/shard_map/all_gather | solution.py:25
  11.0 69.1 %all-gather.29.cloned.1.call-start = ((), (), s32[]{:S(2)}) async-start(), calls=%async_computation.23 | async-start | bytes 2064384 | tf_op jit(solution)/shard_map/all_gather | solution.py:69
  11.7 110.8 %all-gather.43.cloned.1.call-start = ((), (), s32[]{:S(2)}) async-start(), calls=%async_computation.32 | async-start | bytes 2293760 | tf_op jit(solution)/shard_map/all_gather | solution.py:25
  12.5 139.0 %all-gather.31.cloned.1.call-start = ((), (), s32[]{:S(2)}) async-start(), calls=%async_computation.24 | async-start | bytes 2064384 | tf_op jit(solution)/shard_map/all_gather | solution.py:70
  13.0 167.0 %all-gather.33.cloned.1.call-start = ((), (), s32[]{:S(2)}) async-start(), calls=%async_computation.25 | async-start | bytes 2064384 | tf_op jit(solution)/shard_map/all_gather | solution.py:73
  13.6 208.6 %all-gather.47.cloned.1.call-start = ((), (), s32[]{:S(2)}) async-start(), calls=%async_computation.36 | async-start | bytes 2293760 | tf_op jit(solution)/shard_map/all_gather | solution.py:25
  14.2 249.9 %all-gather.51.cloned.1.call-start = ((), (), s32[]{:S(2)}) async-start(), calls=%async_computation.40 | async-start | bytes 2293760 | tf_op jit(solution)/shard_map/all_gather | solution.py:25
  15.0 320.8 %reduce-scatter.30.cloned.1.call-start = ((), (), s32[]{:S(2)}) async-start(), calls=%async_computation.26 | async-start | bytes 4587520 | tf_op jit(solution)/shard_map/reduce_scatter | solution.py:33
  17.1 275.1 %copy-start.105 = (f32[1,448]{1,0:T(1,128)}, f32[1,448]{1,0:T(1,128)S(1)}, u32[]{:S(2)}) copy-start(f32[1,448]{1,0:T(1,128)S(1)} %get-tuple-element.208) | copy-start | bytes 5380
  17.1 275.1 %copy-start.107 = (f32[1,448]{1,0:T(1,128)}, f32[1,448]{1,0:T(1,128)S(1)}, u32[]{:S(2)}) copy-start(f32[1,448]{1,0:T(1,128)S(1)} %get-tuple-element.209) | copy-start | bytes 5380
  17.1 275.1 %copy-start.109 = (f32[1,448]{1,0:T(1,128)}, f32[1,448]{1,0:T(1,128)S(1)}, u32[]{:S(2)}) copy-start(f32[1,448]{1,0:T(1,128)S(1)} %get-tuple-element.210) | copy-start | bytes 5380
  17.9 136.8 %copy-start.97 = (f32[512]{0:T(512)}, f32[512]{0:T(512)S(1)}, u32[]{:S(2)}) copy-start(f32[512]{0:T(512)S(1)} %get-tuple-element.240) | copy-start | bytes 6148
  17.9 136.8 %copy-start.99 = (f32[512]{0:T(512)}, f32[512]{0:T(512)S(1)}, u32[]{:S(2)}) copy-start(f32[512]{0:T(512)S(1)} %get-tuple-element.241) | copy-start | bytes 6148
  18.0 136.7 %copy-start.101 = (f32[512]{0:T(512)}, f32[512]{0:T(512)S(1)}, u32[]{:S(2)}) copy-start(f32[512]{0:T(512)S(1)} %get-tuple-element.242) | copy-start | bytes 6148
  160.5 145.0 %copy-start.47 = (bf16[512,448]{0,1:T(8,128)(2,1)}, bf16[512,448]{0,1:T(8,128)(2,1)S(1)}, u32[]{:S(2)}) copy-start(bf16[512,448]{0,1:T(8,128)(2,1)S(1)} %get-tuple-element.220) | copy-start | bytes 1376260
  184.7 222.2 %reduce-scatter.38.cloned.1.call-start = ((), (), s32[]{:S(2)}) async-start(), calls=%async_computation.37 | async-start | bytes 4587520 | tf_op jit(solution)/shard_map/reduce_scatter | solution.py:33
  301.3 176.6 %reduce-scatter.42.cloned.1.call-start = ((), (), s32[]{:S(2)}) async-start(), calls=%async_computation.41 | async-start | bytes 4587520 | tf_op jit(solution)/shard_map/reduce_scatter | solution.py:33
  305.4 243.7 %reduce-scatter.34.cloned.1.call-start = ((), (), s32[]{:S(2)}) async-start(), calls=%async_computation.33 | async-start | bytes 4587520 | tf_op jit(solution)/shard_map/reduce_scatter | solution.py:33
  308.5 280.8 %all-gather.37.cloned.1.call-start = ((), (), s32[]{:S(2)}) async-start(), calls=%async_computation.28 | async-start | bytes 5160960 | tf_op jit(solution)/shard_map/all_gather | solution.py:71
  309.0 245.2 %copy-start.93 = (f32[1792]{0:T(1024)S(1)}, f32[1792]{0:T(1024)}, u32[]{:S(2)}) copy-start(f32[1792]{0:T(1024)} %param.26) | copy-start | bytes 21508
  309.1 322.6 %all-gather.49.cloned.1.call-start = ((), (), s32[]{:S(2)}) async-start(), calls=%async_computation.38 | async-start | bytes 2293760 | tf_op jit(solution)/shard_map/all_gather | solution.py:25
  553.3 739.9 %copy-start.10 = (f32[128,1792]{1,0:T(8,128)}, f32[128,1792]{1,0:T(8,128)S(1)}, u32[]{:S(2)}) copy-start(f32[128,1792]{1,0:T(8,128)S(1)} %get-tuple-element.117) | copy-start | bytes 2752516
  553.3 739.9 %copy-start.115 = (f32[128]{0:T(128)}, f32[128]{0:T(128)S(1)}, u32[]{:S(2)}) copy-start(f32[128]{0:T(128)S(1)} %add_rsqrt_fusion.6) | copy-start | bytes 1540
  553.4 882.0 %copy-start.117 = (f32[128]{0:T(128)}, f32[128]{0:T(128)S(1)}, u32[]{:S(2)}) copy-start(f32[128]{0:T(128)S(1)} %add_rsqrt_fusion.2) | copy-start | bytes 1540
  555.5 116.4 %all-gather.39.cloned.1.call-start = ((), (), s32[]{:S(2)}) async-start(), calls=%async_computation.29 | async-start | bytes 5160960 | tf_op jit(solution)/shard_map/all_gather | solution.py:72
  556.0 157.5 %all-gather.67.cloned.1.call-start = ((), (), s32[]{:S(2)}) async-start(), calls=%async_computation.58 | async-start | bytes 2293760 | tf_op jit(solution)/shard_map/all_gather | solution.py:29
  558.8 194.9 %all-gather.41.cloned.1.call-start = ((), (), s32[]{:S(2)}) async-start(), calls=%async_computation.30 | async-start | bytes 5160960 | tf_op jit(solution)/shard_map/all_gather | solution.py:74
  559.4 236.6 %all-gather.35.cloned.1.call-start = ((), (), s32[]{:S(2)}) async-start(), calls=%async_computation.27 | async-start | bytes 2293760 | tf_op jit(solution)/shard_map/all_gather | solution.py:25
  560.0 277.7 %all-gather.63.cloned.1.call-start = ((), (), s32[]{:S(2)}) async-start(), calls=%async_computation.56 | async-start | bytes 2293760 | tf_op jit(solution)/shard_map/all_gather | solution.py:29
  560.6 348.8 %reduce-scatter.54.cloned.1.call-start = ((), (), s32[]{:S(2)}) async-start(), calls=%async_computation.50 | async-start | bytes 4587520 | tf_op jit(solution)/shard_map/reduce_scatter | solution.py:37
  773.4 206.9 %reduce-scatter.46.cloned.1.call-start = ((), (), s32[]{:S(2)}) async-start(), calls=%async_computation.44 | async-start | bytes 4587520 | tf_op jit(solution)/shard_map/reduce_scatter | solution.py:37
  859.9 165.3 %all-gather.45.cloned.1.call-start = ((), (), s32[]{:S(2)}) async-start(), calls=%async_computation.34 | async-start | bytes 2293760 | tf_op jit(solution)/shard_map/all_gather | solution.py:25
  859.9 575.4 %copy-start.119 = (f32[128]{0:T(128)}, f32[128]{0:T(128)S(1)}, u32[]{:S(2)}) copy-start(f32[128]{0:T(128)S(1)} %add_rsqrt_fusion.4) | copy-start | bytes 1540
  860.0 575.4 %copy-start.121 = (f32[128]{0:T(128)}, f32[128]{0:T(128)S(1)}, u32[]{:S(2)}) copy-start(f32[128]{0:T(128)S(1)} %add_rsqrt_fusion) | copy-start | bytes 1540
  984.7 82.3 %all-gather.65.cloned.1.call-start = ((), (), s32[]{:S(2)}) async-start(), calls=%async_computation.57 | async-start | bytes 2293760 | tf_op jit(solution)/shard_map/all_gather | solution.py:29
  985.4 123.5 %all-gather.53.cloned.1.call-start = ((), (), s32[]{:S(2)}) async-start(), calls=%async_computation.42 | async-start | bytes 2293760 | tf_op jit(solution)/shard_map/all_gather | solution.py:25
  986.2 164.5 %all-gather.69.cloned.1.call-start = ((), (), s32[]{:S(2)}) async-start(), calls=%async_computation.59 | async-start | bytes 2293760 | tf_op jit(solution)/shard_map/all_gather | solution.py:29
  986.7 235.5 %reduce-scatter.50.cloned.1.call-start = ((), (), s32[]{:S(2)}) async-start(), calls=%async_computation.47 | async-start | bytes 4587520 | tf_op jit(solution)/shard_map/reduce_scatter | solution.py:37
  1089.0 204.3 %reduce-scatter.58.cloned.1.call-start = ((), (), s32[]{:S(2)}) async-start(), calls=%async_computation.53 | async-start | bytes 4587520 | tf_op jit(solution)/shard_map/reduce_scatter | solution.py:37
  1172.6 191.6 %reduce-scatter.36.cloned.1.call-start = ((), (), s32[]{:S(2)}) async-start(), calls=%async_computation.35 | async-start | bytes 4587520 | tf_op jit(solution)/shard_map/reduce_scatter | solution.py:33
  1179.9 255.4 %reduce-scatter.44.cloned.1.call-start = ((), (), s32[]{:S(2)}) async-start(), calls=%async_computation.43 | async-start | bytes 4587520 | tf_op jit(solution)/shard_map/reduce_scatter | solution.py:33
  1187.2 294.2 %all-gather.61.cloned.1.call-start = ((), (), s32[]{:S(2)}) async-start(), calls=%async_computation.54 | async-start | bytes 2293760 | tf_op jit(solution)/shard_map/all_gather | solution.py:29
  1187.2 248.1 %copy-start.151 = (f32[128]{0:T(128)}, f32[128]{0:T(128)S(1)}, u32[]{:S(2)}) copy-start(f32[128]{0:T(128)S(1)} %broadcast_multiply_fusion.7) | copy-start | bytes 1540
  1297.7 143.2 %copy-start.149 = (f32[128]{0:T(128)}, f32[128]{0:T(128)S(1)}, u32[]{:S(2)}) copy-start(f32[128]{0:T(128)S(1)} %broadcast_multiply_fusion.5) | copy-start | bytes 1540
  1297.7 143.2 %copy-start.145 = (f32[128]{0:T(128)}, f32[128]{0:T(128)S(1)}, u32[]{:S(2)}) copy-start(f32[128]{0:T(128)S(1)} %broadcast_multiply_fusion.9) | copy-start | bytes 1540
  1441.0 82.2 %all-gather.57.cloned.1.call-start = ((), (), s32[]{:S(2)}) async-start(), calls=%async_computation.48 | async-start | bytes 2293760 | tf_op jit(solution)/shard_map/all_gather | solution.py:29
  1441.5 123.5 %all-gather.59.cloned.1.call-start = ((), (), s32[]{:S(2)}) async-start(), calls=%async_computation.51 | async-start | bytes 2293760 | tf_op jit(solution)/shard_map/all_gather | solution.py:29
  1442.3 165.2 %all-gather.55.cloned.1.call-start = ((), (), s32[]{:S(2)}) async-start(), calls=%async_computation.45 | async-start | bytes 2293760 | tf_op jit(solution)/shard_map/all_gather | solution.py:29
  1443.0 269.7 %all-reduce.22.cloned.1.call-start = ((), (), s32[]{:S(2)}) async-start(), calls=%async_computation.66 | async-start | bytes 524288
  1659.2 246.8 %reduce-scatter.56.cloned.1.call-start = ((), (), s32[]{:S(2)}) async-start(), calls=%async_computation.52 | async-start | bytes 4587520 | tf_op jit(solution)/shard_map/reduce_scatter | solution.py:37
  1720.7 185.3 %reduce-scatter.60.cloned.1.call-start = ((), (), s32[]{:S(2)}) async-start(), calls=%async_computation.55 | async-start | bytes 4587520 | tf_op jit(solution)/shard_map/reduce_scatter | solution.py:37
  1737.4 194.4 %reduce-scatter.52.cloned.1.call-start = ((), (), s32[]{:S(2)}) async-start(), calls=%async_computation.49 | async-start | bytes 4587520 | tf_op jit(solution)/shard_map/reduce_scatter | solution.py:37
  1754.0 248.9 %reduce-scatter.48.cloned.1.call-start = ((), (), s32[]{:S(2)}) async-start(), calls=%async_computation.46 | async-start | bytes 4587520 | tf_op jit(solution)/shard_map/reduce_scatter | solution.py:37
  1768.9 305.4 %reduce-scatter.40.cloned.1.call-start = ((), (), s32[]{:S(2)}) async-start(), calls=%async_computation.39 | async-start | bytes 4587520 | tf_op jit(solution)/shard_map/reduce_scatter | solution.py:33
  1776.9 368.6 %reduce-scatter.32.cloned.1.call-start = ((), (), s32[]{:S(2)}) async-start(), calls=%async_computation.31 | async-start | bytes 4587520 | tf_op jit(solution)/shard_map/reduce_scatter | solution.py:33
  1784.9 440.4 %reduce-scatter.68.cloned.1.call-start = ((), (), s32[]{:S(2)}) async-start(), calls=%async_computation.63 | async-start | bytes 10321920 | tf_op jit(solution)/shard_map/reduce_scatter | solution.py:198
  1815.6 489.0 %reduce-scatter.70.cloned.1.call-start = ((), (), s32[]{:S(2)}) async-start(), calls=%async_computation.64 | async-start | bytes 10321920 | tf_op jit(solution)/shard_map/reduce_scatter | solution.py:199
  1845.8 538.4 %reduce-scatter.72.cloned.1.call-start = ((), (), s32[]{:S(2)}) async-start(), calls=%async_computation.65 | async-start | bytes 10321920
  1873.0 563.8 %reduce-scatter.64.cloned.1.call-start = ((), (), s32[]{:S(2)}) async-start(), calls=%async_computation.61 | async-start | bytes 4128768 | tf_op jit(solution)/shard_map/reduce_scatter | solution.py:194
  1883.1 606.9 %reduce-scatter.66.cloned.1.call-start = ((), (), s32[]{:S(2)}) async-start(), calls=%async_computation.62 | async-start | bytes 4128768 | tf_op jit(solution)/shard_map/reduce_scatter | solution.py:196
  1893.3 649.4 %reduce-scatter.62.cloned.1.call-start = ((), (), s32[]{:S(2)}) async-start(), calls=%async_computation.60 | async-start | bytes 4128768 | tf_op jit(solution)/shard_map/reduce_scatter | solution.py:193
  1905.9 168.4 %copy-start.94 = (f32[1792]{0:T(1024)S(1)}, f32[1792]{0:T(1024)}, u32[]{:S(2)}) copy-start(f32[1792]{0:T(1024)} %param.26) | copy-start | bytes 21508
  1905.9 168.4 %copy-start.118 = (f32[128]{0:T(128)S(1)}, f32[128]{0:T(128)}, u32[]{:S(2)}) copy-start(f32[128]{0:T(128)} %copy-done.117) | copy-start | bytes 1540
  1905.9 168.4 %copy-start.152 = (f32[128]{0:T(128)S(1)}, f32[128]{0:T(128)}, u32[]{:S(2)}) copy-start(f32[128]{0:T(128)} %copy-done.151) | copy-start | bytes 1540
  (165 other events, 2187.6 us)
Sparse Core Ops, SparseCore 0:
  11.1 40.1 all-gather.26
  53.2 26.8 all-gather.28
  82.2 40.1 all-gather.42
  124.2 27.1 all-gather.30
  153.2 26.7 all-gather.32
  182.0 40.2 all-gather.46
  223.8 40.2 all-gather.50
  267.0 68.7 reduce-scatter.29
  338.1 68.7 reduce-scatter.37
  409.1 68.7 reduce-scatter.41
  480.2 68.7 reduce-scatter.33
  550.8 38.4 all-gather.36
  591.4 40.1 all-gather.48
  633.4 38.4 all-gather.38
  673.3 40.1 all-gather.66
  715.3 38.4 all-gather.40
  755.7 40.1 all-gather.34
  797.4 40.2 all-gather.62
  840.5 68.7 reduce-scatter.53
  911.5 68.7 reduce-scatter.45
  984.8 40.3 all-gather.44
  1026.7 40.2 all-gather.64
  1068.6 40.2 all-gather.52
  1110.3 40.2 all-gather.68
  1153.5 68.7 reduce-scatter.49
  1224.4 68.7 reduce-scatter.57
  1295.4 68.7 reduce-scatter.35
  1366.5 68.7 reduce-scatter.43
  1441.1 40.3 all-gather.60
  1482.8 40.2 all-gather.56
  1524.7 40.2 all-gather.58
  1567.2 40.2 all-gather.54
  1659.3 53.4 all-reduce.21
  1720.8 68.6 reduce-scatter.55
  1791.9 68.7 reduce-scatter.59
  1863.0 68.7 reduce-scatter.51
  1934.1 68.7 reduce-scatter.47
  2005.3 68.9 reduce-scatter.39
  2076.6 68.8 reduce-scatter.31
  2150.1 75.1 reduce-scatter.67
  2229.5 75.0 reduce-scatter.69
  2309.2 75.0 reduce-scatter.71
  2388.1 48.6 reduce-scatter.63
  2441.3 48.6 reduce-scatter.65
  2493.9 48.6 reduce-scatter.61
where the time goes:
time: 2560 us; the launch traced here: 2550 us
  waiting for transfers between devices  1910 us (75%)
  matrix products  355 us (14%)
  local copies, waits for them, and re-layouts  126 us (5%)
  other arithmetic  70.9 us (3%)
  blocking collectives  64.9 us (3%)
    reduce_scatter x8, waiting for transfers between devices, collect(): return lax.psum_scatter(partial_sum, 'col', scatter_dimension=0, tiled=True)  481 us
    reduce_scatter x8, waiting for transfers between devices, collect_grad(): return lax.psum_scatter(partial_sum, 'col', scatter_dimension=0, tiled=True)  323 us
    all_gather x8, waiting for transfers between devices, spread_grad(): return lax.all_gather(shard, 'col', axis=0, tiled=True)  266 us
    all_gather x8, waiting for transfers between devices, spread(): return lax.all_gather(shard, 'col', axis=0, tiled=True)  237 us
    unnamed x47, waiting for transfers between devices  140 us
    dot_general x24, matrix products, contract_last(): lax.dot_general(left, right, (((1,), (1,)), ((), ())), preferred_element_...  115 us
    dot_general x24, matrix products, contract_first(): lax.dot_general(left, right, (((0,), (0,)), ((), ())), preferred_element_...  98.7 us
    reduce_scatter x1, waiting for transfers between devices, per_device(): lax.psum_scatter(partials[7], 'row', scatter_dimension=0, tiled=True)  79.3 us
  transfers between devices with their start and end apart: 45, of which 43 were waited for; matrix products, arithmetic and copies ran while one was open for 18% of the time, Pallas kernels for 0%

commit v1 on v0

v1 whole, which is shorter than its diff:
```python
import jax
import jax.numpy as jnp
from jax import lax
from jax.sharding import Mesh
from jax.sharding import PartitionSpec as P

BLOCK = 128
EPSILON = 1e-05
F32 = jnp.float32
BF16 = jnp.bfloat16
EVERY = ("a", "b", "c", "z")


def dot_nn(left, right):
    return lax.dot_general(left, right, (((1,), (0,)), ((), ())), preferred_element_type=F32)


def dot_nt(left, right):
    return lax.dot_general(left, right, (((1,), (1,)), ((), ())), preferred_element_type=F32)


def dot_tn(left, right):
    return lax.dot_general(left, right, (((0,), (0,)), ((), ())), preferred_element_type=F32)


def shift_by(value, axis, amount):
    size = lax.axis_size(axis)
    return lax.ppermute(value, axis, [(i, (i + amount) % size) for i in range(size)])


def pieces_of(value, axis):
    return [value] + [shift_by(value, axis, s) for s in range(1, lax.axis_size(axis))]


def in_order(pieces, axis, dim):
    size, index = len(pieces), lax.axis_index(axis)
    if size == 2:
        first = index == 0
        return jnp.stack(
            [jnp.where(first, pieces[0], pieces[1]), jnp.where(first, pieces[1], pieces[0])], axis=dim
        )
    return jnp.stack(
        [lax.select_n((index - j) % size, *pieces) for j in range(size)], axis=dim
    )


def scatter_sum(value, axis, dim):
    size, index = lax.axis_size(axis), lax.axis_index(axis)
    total = lax.dynamic_index_in_dim(value, index, dim, keepdims=False).astype(F32)
    for s in range(1, size):
        leaving = lax.dynamic_index_in_dim(value, (index - s) % size, dim, keepdims=False)
        total = total + shift_by(leaving.astype(BF16), axis, -s).astype(F32)
    return total


def rows_gathered(block):
    value = in_order(pieces_of(block, "a"), "a", 0)
    value = in_order(pieces_of(value, "b"), "b", 1)
    value = in_order(pieces_of(value, "c"), "c", 2)
    return value.reshape(-1, block.shape[-1])


def rows_scattered(partial):
    sizes = tuple(lax.axis_size(n) for n in ("a", "b", "c"))
    width = partial.shape[1]
    value = partial.reshape(*sizes, -1, width)
    value = scatter_sum(value, "c", 2)
    value = scatter_sum(value, "b", 1)
    value = scatter_sum(value, "a", 0)
    count = lax.axis_size("z")
    local = width // count
    total = value[:, :local]
    for s in range(1, count):
        total = total + shift_by(value[:, s * local : (s + 1) * local].astype(BF16), "z", -s).astype(F32)
    return total


def swapped(block):
    count = lax.axis_size("z")
    return lax.ppermute(
        block,
        ("b", "c", "z"),
        [(t * count + z, z * count + t) for t in range(count) for z in range(count)],
    )


def team_gathered(value):
    near = pieces_of(value, "b")
    far = shift_by(jnp.concatenate(near, axis=0), "c", 1)
    return jnp.concatenate([*near, far], axis=0)


def team_scattered(partial):
    half = partial.shape[0] // 2
    value = partial[:half] + shift_by(partial[half:].astype(BF16), "c", 1).astype(F32)
    count = lax.axis_size("b")
    size = half // count
    total = value[:size]
    for s in range(1, count):
        total = total + shift_by(value[s * size : (s + 1) * size].astype(BF16), "b", -s).astype(F32)
    return total


def per_device(
    tokens,
    lengths,
    permutation,
    cotangent,
    norm1_gain,
    mixer_in,
    mixer_gate,
    conv_kernel,
    mixer_out,
    norm2_gain,
    ffn_gate,
    ffn_up,
    ffn_down,
):
    micro, length, width = tokens.shape
    count_b, count_z = lax.axis_size("b"), lax.axis_size("z")
    ia, ib, ic, iz = (lax.axis_index(n) for n in EVERY)
    place = ((ia * count_b + ib) * 2 + ic) * count_z + iz
    per_block = BLOCK // length
    blocks = permutation.shape[1]
    local = conv_kernel.shape[1]
    rows = micro * length

    ffn_g, ffn_u, ffn_d = (
        lax.all_gather(swapped(w), ("a", "z"), axis=0, tiled=True) for w in (ffn_gate, ffn_up, ffn_down)
    )
    both = jnp.concatenate(
        [*pieces_of(mixer_in, "z"), *pieces_of(mixer_gate, "z")], axis=1
    )
    both = rows_gathered(both)
    w_out = rows_gathered(jnp.concatenate(pieces_of(mixer_out, "z"), axis=1))
    kernel = jnp.concatenate(pieces_of(conv_kernel, "z"), axis=1)
    cot_team = team_gathered(cotangent.reshape(rows, width))

    dealt = lax.dynamic_slice_in_dim(permutation, place // per_block, 1, axis=1)[:, 0]
    own = dealt * per_block + place % per_block
    spots = jnp.arange(blocks, dtype=jnp.int32)

    def holder(piece):
        at = jnp.sum(jnp.where(permutation == (piece // per_block)[:, None], spots[None, :], 0), axis=1)
        return at * per_block + piece % per_block

    before = holder(jnp.maximum(own - 1, 0))
    last = blocks * per_block - 1
    after = holder(jnp.minimum(own + 1, last))
    order = jnp.arange(lengths.shape[1], dtype=jnp.int32)
    offsets = jnp.sum(jnp.where(order[None, None, :] < order[None, :, None], lengths[:, None, :], 0), axis=2)
    position = own[:, None] * length + jnp.arange(length, dtype=jnp.int32)[None, :]
    is_start = jnp.any(position[:, :, None] == offsets[:, None, :], axis=2)
    was_start = jnp.any(position[:, :, None] - 1 == offsets[:, None, :], axis=2)
    keep_one = jnp.where(is_start, 0.0, 1.0).astype(F32)[:, :, None]
    keep_two = jnp.where(is_start | was_start, 0.0, 1.0).astype(F32)[:, :, None]

    def pick(everyone, source):
        return jnp.stack(
            [
                lax.dynamic_slice(everyone, (source[m], m, 0, 0), (1, 1, 2, everyone.shape[3]))[0, 0]
                for m in range(micro)
            ]
        )

    tails = pick(lax.all_gather(tokens[:, length - 2 :, :], EVERY, axis=0), before)
    local_in = tokens.reshape(rows, width).astype(F32)
    local_cot = cotangent.reshape(rows, width).astype(F32)
    scale_one = lax.rsqrt(jnp.mean(local_in * local_in, axis=1, keepdims=True) + EPSILON)
    normed_one = local_in * scale_one
    hidden_one = (normed_one * norm1_gain).astype(BF16)
    tail_in = tails.reshape(micro * 2, width).astype(F32)
    tail_scale = lax.rsqrt(jnp.mean(tail_in * tail_in, axis=1, keepdims=True) + EPSILON)
    tail_hidden = (tail_in * tail_scale * norm1_gain).astype(BF16)
    channels = kernel.shape[1]
    signal_gating = dot_nn(hidden_one, both)
    signal = signal_gating[:, :channels].reshape(micro, length, channels)
    gating = signal_gating[:, channels:].reshape(micro, length, channels)
    tail_signal = dot_nn(tail_hidden, both[:, :channels]).reshape(micro, 2, channels)
    extended = jnp.concatenate([tail_signal, signal], axis=1)
    shift_one = keep_one * extended[:, 1 : length + 1, :]
    shift_two = keep_two * extended[:, 0:length, :]
    mixed = kernel[0] * signal + kernel[1] * shift_one + kernel[2] * shift_two
    product = (mixed * gating).astype(BF16).reshape(rows, channels)
    residual = local_in + dot_nt(product, w_out)

    scale_two = lax.rsqrt(jnp.mean(residual * residual, axis=1, keepdims=True) + EPSILON)
    normed_two = residual * scale_two
    hidden_two = team_gathered((normed_two * norm2_gain).astype(BF16))
    gate_val = dot_nn(hidden_two, ffn_g)
    up_val = dot_nn(hidden_two, ffn_u)
    sigmoid_gate = jax.nn.sigmoid(gate_val)
    activated = (gate_val * sigmoid_gate * up_val).astype(BF16)
    output = (residual + team_scattered(dot_nt(activated, ffn_d))).astype(BF16)

    def ffn_scattered(partial):
        value = partial.reshape(2, count_z, -1, partial.shape[1])
        value = scatter_sum(value, "a", 0)
        value = scatter_sum(value, "z", 0)
        return swapped(value.astype(BF16)).astype(F32)

    grad_down = ffn_scattered(dot_tn(cot_team, activated).astype(BF16))
    grad_act = dot_nn(cot_team, ffn_d)
    slope = sigmoid_gate * (1.0 + gate_val * (1.0 - sigmoid_gate))
    grad_gate = (grad_act * up_val * slope).astype(BF16)
    grad_up = (grad_act * gate_val * sigmoid_gate).astype(BF16)
    grad_hidden_two = team_scattered(dot_nt(grad_gate, ffn_g) + dot_nt(grad_up, ffn_u))
    grad_ffg = ffn_scattered(dot_tn(hidden_two, grad_gate).astype(BF16))
    grad_ffu = ffn_scattered(dot_tn(hidden_two, grad_up).astype(BF16))

    grad_gain_two = jnp.sum(grad_hidden_two * normed_two, axis=0)
    grad_norm_two = grad_hidden_two * norm2_gain
    inner_two = jnp.mean(grad_norm_two * normed_two, axis=1, keepdims=True)
    grad_residual = local_cot + scale_two * (grad_norm_two - normed_two * inner_two)
    grad_branch = grad_residual.astype(BF16)
    grad_product = dot_nn(grad_branch, w_out).reshape(micro, length, channels)
    grad_out = rows_scattered(dot_tn(grad_branch, product).astype(BF16))
    grad_mixed = grad_product * gating
    grad_gating = (grad_product * mixed).astype(BF16).reshape(rows, channels)
    grad_kernel = jnp.stack(
        [
            jnp.sum(grad_mixed * signal, axis=(0, 1)),
            jnp.sum(grad_mixed * shift_one, axis=(0, 1)),
            jnp.sum(grad_mixed * shift_two, axis=(0, 1)),
        ]
    )
    into_one = kernel[1] * (keep_one * grad_mixed)
    into_two = kernel[2] * (keep_two * grad_mixed)
    leaving = jnp.stack([into_two[:, 0], into_one[:, 0] + into_two[:, 1]], axis=1)
    blocked = leaving.reshape(micro, 2, count_z, local)

    def turned(value, dim):
        picks = [
            lax.dynamic_index_in_dim(value, (iz - j) % count_z, dim, keepdims=False) for j in range(count_z)
        ]
        return jnp.concatenate(picks, axis=-1)

    everyone = lax.all_gather(turned(blocked, 2).astype(BF16), EVERY, axis=0)
    arrived = turned(pick(everyone, after).reshape(micro, 2, count_z, local), 2).astype(F32)
    arrived = jnp.where((own == last)[:, None, None], 0.0, arrived)
    from_one = jnp.concatenate([into_one[:, 1:], arrived[:, 1:]], axis=1)
    from_two = jnp.concatenate([into_two[:, 2:], arrived[:, :1], jnp.zeros_like(arrived[:, :1])], axis=1)
    grad_signal = (kernel[0] * grad_mixed + from_one + from_two).astype(BF16).reshape(rows, channels)
    grad_gate_w = rows_scattered(dot_tn(hidden_one, grad_gating).astype(BF16))
    grad_in_w = rows_scattered(dot_tn(hidden_one, grad_signal).astype(BF16))
    grad_hidden_one = dot_nt(jnp.concatenate([grad_signal, grad_gating], axis=1), both)
    grad_gain_one = jnp.sum(grad_hidden_one * normed_one, axis=0)
    grad_norm_one = grad_hidden_one * norm1_gain
    inner_one = jnp.mean(grad_norm_one * normed_one, axis=1, keepdims=True)
    input_grad = grad_residual + scale_one * (grad_norm_one - normed_one * inner_one)

    row_count = 4 * count_b
    kernel_parts = turned(grad_kernel.reshape(3, count_z, local), 1).reshape(3, count_z, row_count, -1)
    small = jnp.concatenate(
        [
            grad_gain_one.reshape(row_count, count_z, 1, -1),
            grad_gain_two.reshape(row_count, count_z, 1, -1),
            kernel_parts.transpose(2, 1, 0, 3),
        ],
        axis=2,
    ).reshape(row_count * count_z, 5, -1)
    small = lax.psum_scatter(small, EVERY, scatter_dimension=0, tiled=True)[0]
    return (
        output.reshape(micro, length, width),
        input_grad.reshape(micro, length, width),
        small[0],
        grad_in_w,
        grad_gate_w,
        small[2:5],
        grad_out,
        small[1],
        grad_ffg,
        grad_ffu,
        grad_down,
    )


def solution(mesh):
    row, col = mesh.shape["row"], mesh.shape["col"]
    fine = Mesh(mesh.devices.reshape(2, row // 4, 2, col), EVERY)
    by_rows = ("a", "b", "c")
    matrix = P(by_rows, "z")
    token = P(None, EVERY, None)
    return jax.shard_map(
        per_device,
        mesh=fine,
        in_specs=(
            token,
            P(),
            P(),
            token,
            P(),
            matrix,
            matrix,
            P(None, "z"),
            matrix,
            P(),
            matrix,
            matrix,
            matrix,
        ),
        out_specs=(
            token,
            token,
            P(EVERY),
            matrix,
            matrix,
            P(None, ("z", *by_rows)),
            matrix,
            P(EVERY),
            matrix,
            matrix,
            matrix,
        ),
        check_vma=False,
    )
```

time: 2560 us -> 1300 us (0.51)
  waiting for transfers between devices: 1910 us -> 514 us
  starting transfers between devices: 4.37 us -> 161 us
  matrix products: 355 us -> 199 us
  blocking collectives: 64.9 us -> 188 us
  local copies, waits for them, and re-layouts: 126 us -> 96.9 us
    reduce_scatter x21 -> x0, waiting for transfers between devices: 1110 us -> none  [the longest x8 481 us: collect(): return lax.psum_scatter(partial_sum, 'col', scatter_dimension=0, tiled=True)]
    all_gather x22 -> x3, waiting for transfers between devices: 657 us -> 0.01 us  [per_device(): lax.all_gather(swapped(w), ('a', 'z'), axis=0, tiled=True)]
    ppermute x0 -> x62, waiting for transfers between devices: none -> 514 us  [the longest x56 483 us: shift_by(): lax.ppermute(value, axis, [(i, (i + amount) % size) for i in range(size)])]
    ppermute x0 -> x62, starting transfers between devices: none -> 161 us  [the longest x56 114 us: shift_by(): lax.ppermute(value, axis, [(i, (i + amount) % size) for i in range(size)])]
    dot_general x76 -> x17, matrix products: 355 us -> 199 us  [the longest x6 73.5 us: dot_nn(): lax.dot_general(left, right, (((1,), (0,)), ((), ())), preferred_element_...]
    unnamed x47 -> x3, waiting for transfers between devices: 140 us -> 0.05 us
    all_gather x4 -> x2, blocking collectives: 34.6 us -> 145 us  [the longest x1 76 us: per_device(): lax.all_gather(tokens[:, length - 2:, :], EVERY, axis=0)]
    reshape x28 -> x0, local copies, waits for them, and re-layouts: 57.5 us -> none  [the longest x8 18.6 us: per_device(): (conv_kernel[0] * grad_mixed).reshape(blocks_local, block_size, width_local)]
  transfers between devices with their start and end apart: 45 -> 65, of which waited for: 43 -> 28; matrix products, arithmetic and copies ran while one was open for 18% -> 23% of each run, Pallas kernels for 0% -> 0%
where the time goes in v1:
time: 1300 us; the launch traced here: 1280 us
  waiting for transfers between devices  514 us (40%)
  matrix products  199 us (15%)
  blocking collectives  188 us (14%)
  starting transfers between devices  161 us (12%)
  local copies, waits for them, and re-layouts  96.9 us (7%)
  other arithmetic  95 us (7%)
  between operations  31 us (2%)
    ppermute x56, waiting for transfers between devices, shift_by(): lax.ppermute(value, axis, [(i, (i + amount) % size) for i in range(size)])  483 us
    ppermute x56, starting transfers between devices, shift_by(): lax.ppermute(value, axis, [(i, (i + amount) % size) for i in range(size)])  114 us
    all_gather x1, blocking collectives, per_device(): lax.all_gather(tokens[:, length - 2:, :], EVERY, axis=0)  76 us
    dot_general x6, matrix products, dot_nn(): lax.dot_general(left, right, (((1,), (0,)), ((), ())), preferred_element_...  73.5 us
    dot_general x5, matrix products, dot_nt(): lax.dot_general(left, right, (((1,), (1,)), ((), ())), preferred_element_...  69.2 us
    all_gather x1, blocking collectives, per_device(): everyone = lax.all_gather(turned(blocked, 2).astype(BF16), EVERY, axis=0)  68.5 us
    dot_general x6, matrix products, dot_tn(): lax.dot_general(left, right, (((0,), (0,)), ((), ())), preferred_element_...  55.8 us
    ppermute x6, starting transfers between devices, swapped(): lax.ppermute(block, ('b', 'c', 'z'), [(t * count + z, z * count + t) for...  47.5 us
  transfers between devices with their start and end apart: 65, of which 28 were waited for; matrix products, arithmetic and copies ran while one was open for 23% of the time, Pallas kernels for 0%

profile of v1, /device:TPU:30, one launch (start us, length us, event | category | flops | bytes accessed | tf_op | source)
XLA Modules:
  0.0 1284.7 jit_solution(5016543920830570994)
XLA Ops:
  9.2 14.9 %collective-permute-done.22 = bf16[224,1216]{1,0:T(8,128)(2,1)S(1)} collective-permute-done((bf16[224,1216]{1,0:T(8,128)(2,1)}, bf16[224,1216]{1,0:T(8,128)(2,1)S(1)}, u32[]{:S(2)}, u32[]{:S(2)}) %collective-permute-start.22) | collective-permute-done | bytes 544800 | tf_op jit(solution)/shard_map/ppermute | solution.py:80
  24.9 17.5 %collective-permute-start.3 = (bf16[224,448]{1,0:T(8,128)(2,1)}, bf16[224,448]{1,0:T(8,128)(2,1)S(1)}, u32[]{:S(2)}, u32[]{:S(2)}) collective-permute-start(bf16[224,448]{1,0:T(8,128)(2,1)} %param.18), channel_id=1, source_target_pairs={{0,1},{1,2},{2,3},{3,0},{4,5},{5,6},{6,7},{7,4},{8,9},{9,10},{10,1... | collective-permute-start | bytes 602120 | tf_op jit(solution)/shard_map/ppermute | solution.py:28
  48.8 11.2 collective-permute-start.8
  60.1 28.0 %collective-permute-done.4 = bf16[224,448]{1,0:T(8,128)(2,1)S(1)} collective-permute-done((bf16[224,448]{1,0:T(8,128)(2,1)}, bf16[224,448]{1,0:T(8,128)(2,1)S(1)}, u32[]{:S(2)}, u32[]{:S(2)}) %collective-permute-start.4) | collective-permute-done | bytes 200736 | tf_op jit(solution)/shard_map/ppermute | solution.py:28
  88.1 8.2 collective-permute-done.7
  99.2 57.5 %collective-permute-done.9 = bf16[224,3584]{1,0:T(8,128)(2,1)S(1)} collective-permute-done((bf16[224,3584]{1,0:T(8,128)(2,1)S(1)}, bf16[224,3584]{1,0:T(8,128)(2,1)S(1)}, u32[]{:S(2)}, u32[]{:S(2)}) %collective-permute-start.9) | collective-permute-done | bytes 1605664 | tf_op jit(solution)/shard_map/ppermute | solution.py:28
  164.2 4.4 collective-permute-done.12
  168.6 14.8 %collective-permute-done.13 = bf16[224,448]{1,0:T(8,128)(2,1)S(1)} collective-permute-done((bf16[224,448]{1,0:T(8,128)(2,1)S(1)}, bf16[224,448]{1,0:T(8,128)(2,1)S(1)}, u32[]{:S(2)}, u32[]{:S(2)}) %collective-permute-start.13) | collective-permute-done | bytes 200736 | tf_op jit(solution)/shard_map/ppermute | solution.py:28
  188.6 14.3 %collective-permute-done.21 = bf16[224,1216]{1,0:T(8,128)(2,1)} collective-permute-done((bf16[224,1216]{1,0:T(8,128)(2,1)}, bf16[224,1216]{1,0:T(8,128)(2,1)}, u32[]{:S(2)}, u32[]{:S(2)}) %collective-permute-start.21) | collective-permute-done | bytes 544800 | tf_op jit(solution)/shard_map/ppermute | solution.py:80
  207.7 36.2 %collective-permute-done.10 = bf16[2,224,3584]{2,1,0:T(8,128)(2,1)} collective-permute-done((bf16[2,224,3584]{2,1,0:T(8,128)(2,1)S(1)}, bf16[2,224,3584]{2,1,0:T(8,128)(2,1)}, u32[]{:S(2)}, u32[]{:S(2)}) %collective-permute-start.10) | collective-permute-done | bytes 3211296 | tf_op jit(solution)/shard_map/ppermute | solution.py:28
  250.8 26.0 %collective-permute-done.16 = bf16[2,224,1792]{2,1,0:T(8,128)(2,1)S(1)} collective-permute-done((bf16[2,224,1792]{2,1,0:T(8,128)(2,1)S(1)}, bf16[2,224,1792]{2,1,0:T(8,128)(2,1)S(1)}, u32[]{:S(2)}, u32[]{:S(2)}) %collective-permute-start.16) | collective-permute-done | bytes 1605664 | tf_op jit(solution)/shard_map/ppermute | solution.py:28
  297.6 76.0 %all-gather = bf16[128,2,1792]{2,1,0:T(2,128)(2,1)S(1)} all-gather(bf16[4,2,1792]{2,1,0:T(2,128)(2,1)S(1)} %slice.165), channel_id=2, replica_groups=mesh['a'=2,'b'=2,'c'=2,'z'=4] {'a','b','c','z'}, dimensions={0}, use_global_device_ids=true | all-gather | bytes 946176 | tf_op jit(solution)/shard_map/all_gather | solution.py:166
  375.8 8.1 collective-permute-start.25
  391.0 3.9 select_bitcast_fusion.1
  401.0 8.9 fusion.104
  417.8 7.2 multiply_reduce_fusion.5
  425.8 6.5 collective-permute-start.18
  435.9 35.0 %collective-permute-done.18 = bf16[512,1792]{1,0:T(8,128)(2,1)S(1)} collective-permute-done((bf16[512,1792]{1,0:T(8,128)(2,1)S(1)}, bf16[512,1792]{1,0:T(8,128)(2,1)S(1)}, u32[]{:S(2)}, u32[]{:S(2)}) %collective-permute-start.18) | collective-permute-done | bytes 1835040 | tf_op jit(solution)/shard_map/ppermute | solution.py:28
  473.4 15.6 %fusion.23 = f32[2048,1216]{0,1:T(8,128)} fusion(bf16[1792,1216]{1,0:T(8,128)(2,1)} %all-gather.9.cloned.1.call-done, bf16[1024,1792]{1,0:T(8,128)(2,1)} %collective-permute-done.26, bf16[512,1792]{1,0:T(8,128)(2,1)} %collective-permute-done.25, bf16[512,1792]{1,0:T(8,128)(2,1)S(1)} %bitcast.279), kind=kOutput, calls=%fused_computation.97 | convolution fusion | flops 8947499008 | bytes 21659648 | tf_op jit(solution)/shard_map/dot_general | solution.py:15
  488.9 15.6 %fusion.91 = f32[2048,1216]{0,1:T(8,128)} fusion(bf16[1792,1216]{1,0:T(8,128)(2,1)} %all-gather.7.cloned.1.call-done, bf16[1024,1792]{1,0:T(8,128)(2,1)} %collective-permute-done.19, bf16[512,1792]{1,0:T(8,128)(2,1)} %copy-done.28, bf16[512,1792]{1,0:T(8,128)(2,1)} %copy-done.25), kind=kOutput, calls=%fused_computation.271 | convolution fusion | flops 8947499008 | bytes 21659648 | tf_op jit(solution)/shard_map/dot_general | solution.py:15
  504.6 23.0 %multiply_convert_fusion.1 = (bf16[2048,1216]{0,1:T(8,128)(2,1)}, bf16[2048,1216]{0,1:T(8,128)(2,1)}, bf16[2048,1216]{0,1:T(8,128)(2,1)}) fusion(f32[2048,1216]{0,1:T(8,128)} %fusion.23, f32[2048,1216]{0,1:T(8,128)} %fusion.91, bf16[1792,1216]{1,0:T(8,128)(2,1)} %all-gather.5.cloned.1.call-done, bf16[1024,1792]{1,0:T(8,128)(2,1)} %collective-permute-done.19, ...), kind=kOutput, calls=%fused_computation.4 | convolution fusion | flops 8987344896 | bytes 46563328 | tf_op jit(solution)/shard_map/dot_general | solution.py:15
  527.6 15.5 %convolution_convert_fusion = bf16[1792,1216]{0,1:T(8,128)(2,1)} fusion(bf16[2048,1216]{0,1:T(8,128)(2,1)} %get-tuple-element.50, bf16[1024,1792]{1,0:T(8,128)(2,1)} %collective-permute-done.26, bf16[512,1792]{1,0:T(8,128)(2,1)} %collective-permute-done.25, bf16[512,1792]{1,0:T(8,128)(2,1)S(1)} %bitcast.280), kind=kOutput, calls=%fused_computation.8 | convolution fusion | flops 8949678080 | bytes 16678912 | tf_op jit(solution)/shard_map/dot_general | solution.py:23
  543.0 7.2 copy.116
  553.8 13.7 %convolution_convert_fusion.1 = bf16[1792,1216]{0,1:T(8,128)(2,1)} fusion(bf16[2048,1216]{0,1:T(8,128)(2,1)} %get-tuple-element.51, bf16[1024,1792]{1,0:T(8,128)(2,1)} %collective-permute-done.19, bf16[512,1792]{1,0:T(8,128)(2,1)S(1)} %copy-done.29, bf16[512,1792]{1,0:T(8,128)(2,1)S(1)} %copy-done.26), kind=kOutput, calls=%fused_computation.9 | convolution fusion | flops 8949678080 | bytes 16678912 | tf_op jit(solution)/shard_map/dot_general | solution.py:23
  567.5 7.2 copy.115
  579.8 13.6 %convolution_convert_fusion.2 = bf16[1792,1216]{0,1:T(8,128)(2,1)} fusion(bf16[2048,1216]{0,1:T(8,128)(2,1)} %get-tuple-element.49, bf16[1024,1792]{1,0:T(8,128)(2,1)} %collective-permute-done.19, bf16[512,1792]{1,0:T(8,128)(2,1)S(1)} %copy-done.30, bf16[512,1792]{1,0:T(8,128)(2,1)S(1)} %copy-done.26), kind=kOutput, calls=%fused_computation.10 | convolution fusion | flops 8949678080 | bytes 16678912 | tf_op jit(solution)/shard_map/dot_general | solution.py:23
  593.4 7.2 copy.114
  603.9 13.4 %fusion.105 = f32[2048,1792]{1,0:T(8,128)S(1)} fusion(bf16[2048,1216]{0,1:T(8,128)(2,1)} %get-tuple-element.50, bf16[1792,1216]{1,0:T(8,128)(2,1)} %all-gather.9.cloned.1.call-done), kind=kOutput, calls=%fused_computation.285 | convolution fusion | flops 8925478912 | bytes 24018944 | tf_op jit(solution)/shard_map/dot_general | solution.py:19
  623.5 16.3 %fusion.106 = f32[2048,1792]{1,0:T(8,128)} fusion(bf16[2048,1216]{0,1:T(8,128)(2,1)} %get-tuple-element.51, bf16[1792,1216]{1,0:T(8,128)(2,1)} %all-gather.7.cloned.1.call-done), kind=kOutput, calls=%fused_computation.286 | convolution fusion | flops 8925478912 | bytes 24018944 | tf_op jit(solution)/shard_map/dot_general | solution.py:19
  639.8 18.7 %convolution_add_fusion = f32[2048,1792]{1,0:T(8,128)} fusion(f32[2048,1792]{1,0:T(8,128)} %fusion.106, bf16[2048,1216]{0,1:T(8,128)(2,1)} %get-tuple-element.49, bf16[1792,1216]{1,0:T(8,128)(2,1)} %all-gather.5.cloned.1.call-done), kind=kOutput, calls=%fused_computation.7 | convolution fusion | flops 8929148928 | bytes 38699008 | tf_op jit(solution)/shard_map/dot_general | solution.py:19
  668.4 35.9 %collective-permute-done.47 = bf16[4,224,1216]{2,1,0:T(8,128)(2,1)S(1)} collective-permute-done((bf16[4,224,1216]{2,1,0:T(8,128)(2,1)}, bf16[4,224,1216]{2,1,0:T(8,128)(2,1)S(1)}, u32[]{:S(2)}, u32[]{:S(2)}) %collective-permute-start.47) | collective-permute-done | bytes 2179104 | tf_op jit(solution)/shard_map/ppermute | solution.py:28
  710.0 23.6 %collective-permute-done.60 = bf16[224,1216]{1,0:T(8,128)(2,1)S(1)} collective-permute-done((bf16[224,1216]{1,0:T(8,128)(2,1)S(1)}, bf16[224,1216]{1,0:T(8,128)(2,1)S(1)}, u32[]{:S(2)}, u32[]{:S(2)}) %collective-permute-start.60) | collective-permute-done | bytes 544800 | tf_op jit(solution)/shard_map/ppermute | solution.py:28
  735.9 10.9 collective-permute-start.48
  746.8 21.8 %collective-permute-done.54 = bf16[224,1216]{1,0:T(8,128)(2,1)S(1)} collective-permute-done((bf16[224,1216]{1,0:T(8,128)(2,1)S(1)}, bf16[224,1216]{1,0:T(8,128)(2,1)S(1)}, u32[]{:S(2)}, u32[]{:S(2)}) %collective-permute-start.54) | collective-permute-done | bytes 544800 | tf_op jit(solution)/shard_map/ppermute | solution.py:28
  768.6 4.8 collective-permute-done.55
  774.6 19.4 %collective-permute-start.61 = (bf16[224,1216]{1,0:T(8,128)(2,1)}, bf16[224,1216]{1,0:T(8,128)(2,1)}, u32[]{:S(2)}, u32[]{:S(2)}) collective-permute-start(bf16[224,1216]{1,0:T(8,128)(2,1)} %fusion.29), channel_id=1, source_target_pairs={{0,0},{1,4},{2,8},{3,12},{4,1},{5,5},{6,9},{7,13},{8,2},{9,6},{10,... | collective-permute-start | bytes 1634312 | tf_op jit(solution)/shard_map/ppermute | solution.py:80
  794.0 4.1 slice_add_fusion
  801.3 4.8 slice_add_fusion.1
  809.7 6.2 collective-permute-start.56
  815.9 8.2 collective-permute-done.49
  824.1 4.9 collective-permute-done.50
  831.6 15.8 %collective-permute-start.51 = (bf16[224,1216]{1,0:T(8,128)(2,1)}, bf16[224,1216]{1,0:T(8,128)(2,1)S(1)}, u32[]{:S(2)}, u32[]{:S(2)}) collective-permute-start(bf16[224,1216]{1,0:T(8,128)(2,1)} %fusion.35), channel_id=1, source_target_pairs={{0,0},{1,4},{2,8},{3,12},{4,1},{5,5},{6,9},{7,13},{8,2},{9,6},{10,... | collective-permute-start | bytes 1634312 | tf_op jit(solution)/shard_map/ppermute | solution.py:80
  863.0 3.7 collective-permute-done.28
  866.8 3.9 multiply_reduce_fusion.3
  870.7 46.3 %collective-permute-done.24 = bf16[512,1792]{1,0:T(8,128)(2,1)} collective-permute-done((bf16[512,1792]{1,0:T(8,128)(2,1)}, bf16[512,1792]{1,0:T(8,128)(2,1)}, u32[]{:S(2)}, u32[]{:S(2)}) %collective-permute-start.24) | collective-permute-done | bytes 1835040 | tf_op jit(solution)/shard_map/ppermute | solution.py:28
  917.1 6.2 fusion.96
  923.3 5.5 convolution_convert_fusion.3
  928.8 9.4 multiply_reduce_fusion
  949.9 3.8 bitcast_convert_fusion
  958.5 68.5 %all_gather.24 = bf16[32,4,2,1792]{3,1,2,0:T(4,128)(2,1)S(1)} all-gather(bf16[1,4,2,1792]{3,1,2,0:T(4,128)(2,1)S(1)} %copy.104), channel_id=1, replica_groups=mesh['a'=2,'b'=2,'c'=2,'z'=4] {'a','b','c','z'}, dimensions={0}, use_global_device_ids=true | all-gather | bytes 946176 | tf_op jit(solution)/shard_map/all_gather | solution.py:238
  1028.1 5.0 fusion.7
  1033.1 3.8 bitcast_convert_fusion.1
  1041.0 3.8 collective-permute-start.29
  1044.8 13.7 %fusion.19 = (f32[1792]{0:T(1024)S(1)}, f32[512]{0:T(512)S(1)}, f32[512,1792]{1,0:T(8,128)}) fusion(bf16[4,128,1792]{2,1,0:T(8,128)(2,1)S(1)} %copy-done.8, f32[512]{0:T(512)S(1)} %copy-done.60, f32[1792]{0:T(1024)S(1)} %copy-done.51, bf16[1792,3584]{1,0:T(8,128)(2,1)} %bitcast.276, bf16[512,1792]{1,0:T(8,128)(2,1)} %bitcast.304, ...), kind=kOutput, calls=%fused_computation.62 | convolution fusion | flops 6590428672 | bytes 22038528 | tf_op jit(solution)/shard_map/dot_general | solution.py:19
  1059.4 43.7 %all-reduce = f32[32,5,56]{2,0,1:T(8,128)S(1)} all-reduce(f32[32,5,56]{2,0,1:T(8,128)S(1)} %pad_maximum_fusion.13), channel_id=3, replica_groups=mesh['a'=2,'b'=2,'c'=2,'z'=4] {'a','b','c','z'}, use_global_device_ids=true, to_apply=%region_15.16.clone | all-reduce | flops 8960 | bytes 71680
  1104.2 6.0 fusion.18
  1122.8 28.3 %collective-permute-done.42 = bf16[2,224,1792]{2,1,0:T(8,128)(2,1)S(1)} collective-permute-done((bf16[2,224,1792]{2,1,0:T(8,128)(2,1)S(1)}, bf16[2,224,1792]{2,1,0:T(8,128)(2,1)S(1)}, u32[]{:S(2)}, u32[]{:S(2)}) %collective-permute-start.42) | collective-permute-done | bytes 1605664 | tf_op jit(solution)/shard_map/ppermute | solution.py:28
  1152.5 33.0 %collective-permute-done.36 = bf16[2,224,1792]{2,1,0:T(8,128)(2,1)S(1)} collective-permute-done((bf16[2,224,1792]{2,1,0:T(8,128)(2,1)S(1)}, bf16[2,224,1792]{2,1,0:T(8,128)(2,1)S(1)}, u32[]{:S(2)}, u32[]{:S(2)}) %collective-permute-start.36) | collective-permute-done | bytes 1605664 | tf_op jit(solution)/shard_map/ppermute | solution.py:28
  1186.9 30.5 %collective-permute-done.30 = bf16[2,224,1792]{2,1,0:T(8,128)(2,1)S(1)} collective-permute-done((bf16[2,224,1792]{2,1,0:T(8,128)(2,1)S(1)}, bf16[2,224,1792]{2,1,0:T(8,128)(2,1)S(1)}, u32[]{:S(2)}, u32[]{:S(2)}) %collective-permute-start.30) | collective-permute-done | bytes 1605664 | tf_op jit(solution)/shard_map/ppermute | solution.py:28
  1225.7 9.5 collective-permute-done.31
  1240.4 12.2 collective-permute-start.32
  1252.6 4.1 collective-permute-start.33
  1257.6 6.0 collective-permute-done.39
  1264.5 11.0 collective-permute-done.33
  (392 shorter events, 189.6 us)
Async XLA Ops:
  7.2 466.2 %all-gather.9.cloned.1.call-start = ((), (), s32[]{:S(2)}) async-start(), calls=%async_computation.2 | async-start | bytes 5160960 | tf_op jit(solution)/shard_map/all_gather | solution.py:129
  7.2 16.8 %collective-permute-start.22 = (bf16[224,1216]{1,0:T(8,128)(2,1)}, bf16[224,1216]{1,0:T(8,128)(2,1)S(1)}, u32[]{:S(2)}, u32[]{:S(2)}) collective-permute-start(bf16[224,1216]{1,0:T(8,128)(2,1)} %param.25), channel_id=1, source_target_pairs={{0,0},{1,4},{2,8},{3,12},{4,1},{5,5},{6,9},{7,13},{8,2},{9,6},{10,... | collective-permute-start | bytes 1634312 | tf_op jit(solution)/shard_map/ppermute | solution.py:80
  24.9 464.1 %all-gather.7.cloned.1.call-start = ((), (), s32[]{:S(2)}) async-start(), calls=%async_computation.1 | async-start | bytes 5160960 | tf_op jit(solution)/shard_map/all_gather | solution.py:129
  24.9 23.9 %collective-permute-start.3 = (bf16[224,448]{1,0:T(8,128)(2,1)}, bf16[224,448]{1,0:T(8,128)(2,1)S(1)}, u32[]{:S(2)}, u32[]{:S(2)}) collective-permute-start(bf16[224,448]{1,0:T(8,128)(2,1)} %param.18), channel_id=1, source_target_pairs={{0,1},{1,2},{2,3},{3,0},{4,5},{5,6},{6,7},{7,4},{8,9},{9,10},{10,1... | collective-permute-start | bytes 602120 | tf_op jit(solution)/shard_map/ppermute | solution.py:28
  42.4 45.7 %collective-permute-start.4 = (bf16[224,448]{1,0:T(8,128)(2,1)}, bf16[224,448]{1,0:T(8,128)(2,1)S(1)}, u32[]{:S(2)}, u32[]{:S(2)}) collective-permute-start(bf16[224,448]{1,0:T(8,128)(2,1)} %param.18), channel_id=1, source_target_pairs={{0,2},{1,3},{2,0},{3,1},{4,6},{5,7},{6,4},{7,5},{8,10},{9,11},{10,... | collective-permute-start | bytes 602120 | tf_op jit(solution)/shard_map/ppermute | solution.py:28
  42.4 45.7 %collective-permute-start.5 = (bf16[224,448]{1,0:T(8,128)(2,1)}, bf16[224,448]{1,0:T(8,128)(2,1)S(1)}, u32[]{:S(2)}, u32[]{:S(2)}) collective-permute-start(bf16[224,448]{1,0:T(8,128)(2,1)} %param.18), channel_id=1, source_target_pairs={{0,3},{1,0},{2,1},{3,2},{4,7},{5,4},{6,5},{7,6},{8,11},{9,8},{10,9... | collective-permute-start | bytes 602120 | tf_op jit(solution)/shard_map/ppermute | solution.py:28
  43.2 44.9 %collective-permute-start.6 = (bf16[224,448]{1,0:T(8,128)(2,1)}, bf16[224,448]{1,0:T(8,128)(2,1)S(1)}, u32[]{:S(2)}, u32[]{:S(2)}) collective-permute-start(bf16[224,448]{1,0:T(8,128)(2,1)} %param.19), channel_id=1, source_target_pairs={{0,1},{1,2},{2,3},{3,0},{4,5},{5,6},{6,7},{7,4},{8,9},{9,10},{10,1... | collective-permute-start | bytes 602120 | tf_op jit(solution)/shard_map/ppermute | solution.py:28
  46.2 50.0 %collective-permute-start.7 = (bf16[224,448]{1,0:T(8,128)(2,1)}, bf16[224,448]{1,0:T(8,128)(2,1)S(1)}, u32[]{:S(2)}, u32[]{:S(2)}) collective-permute-start(bf16[224,448]{1,0:T(8,128)(2,1)} %param.19), channel_id=1, source_target_pairs={{0,2},{1,3},{2,0},{3,1},{4,6},{5,7},{6,4},{7,5},{8,10},{9,11},{10,... | collective-permute-start | bytes 602120 | tf_op jit(solution)/shard_map/ppermute | solution.py:28
  48.8 47.4 %collective-permute-start.8 = (bf16[224,448]{1,0:T(8,128)(2,1)}, bf16[224,448]{1,0:T(8,128)(2,1)S(1)}, u32[]{:S(2)}, u32[]{:S(2)}) collective-permute-start(bf16[224,448]{1,0:T(8,128)(2,1)} %param.19), channel_id=1, source_target_pairs={{0,3},{1,0},{2,1},{3,2},{4,7},{5,4},{6,5},{7,6},{8,11},{9,8},{10,9... | collective-permute-start | bytes 602120 | tf_op jit(solution)/shard_map/ppermute | solution.py:28
  98.6 58.1 %collective-permute-start.9 = (bf16[224,3584]{1,0:T(8,128)(2,1)S(1)}, bf16[224,3584]{1,0:T(8,128)(2,1)S(1)}, u32[]{:S(2)}, u32[]{:S(2)}) collective-permute-start(bf16[224,3584]{1,0:T(8,128)(2,1)S(1)} %concatenate.81), channel_id=1, source_target_pairs={{0,16},{16,0},{1,17},{17,1},{2,18},{18,2},{3,19},{19,3},{4,20},{20... | collective-permute-start | bytes 4816904 | tf_op jit(solution)/shard_map/ppermute | solution.py:28
  158.6 85.3 %collective-permute-start.10 = (bf16[2,224,3584]{2,1,0:T(8,128)(2,1)S(1)}, bf16[2,224,3584]{2,1,0:T(8,128)(2,1)}, u32[]{:S(2)}, u32[]{:S(2)}) collective-permute-start(bf16[2,224,3584]{2,1,0:T(8,128)(2,1)S(1)} %pad_maximum_fusion.8), channel_id=1, source_target_pairs={{0,8},{8,0},{1,9},{9,1},{2,10},{10,2},{3,11},{11,3},{4,12},{12,4},... | collective-permute-start | bytes 9633800 | tf_op jit(solution)/shard_map/ppermute | solution.py:28
  161.7 21.7 %collective-permute-start.13 = (bf16[224,448]{1,0:T(8,128)(2,1)S(1)}, bf16[224,448]{1,0:T(8,128)(2,1)S(1)}, u32[]{:S(2)}, u32[]{:S(2)}) collective-permute-start(bf16[224,448]{1,0:T(8,128)(2,1)S(1)} %copy-done.37), channel_id=1, source_target_pairs={{0,2},{1,3},{2,0},{3,1},{4,6},{5,7},{6,4},{7,5},{8,10},{9,11},{10,... | collective-permute-start | bytes 602120 | tf_op jit(solution)/shard_map/ppermute | solution.py:28
  163.7 20.4 %collective-permute-start.14 = (bf16[224,448]{1,0:T(8,128)(2,1)S(1)}, bf16[224,448]{1,0:T(8,128)(2,1)}, u32[]{:S(2)}, u32[]{:S(2)}) collective-permute-start(bf16[224,448]{1,0:T(8,128)(2,1)S(1)} %copy-done.37), channel_id=1, source_target_pairs={{0,3},{1,0},{2,1},{3,2},{4,7},{5,4},{6,5},{7,6},{8,11},{9,8},{10,9... | collective-permute-start | bytes 602120 | tf_op jit(solution)/shard_map/ppermute | solution.py:28
  186.2 18.7 %collective-permute-start.15 = (bf16[224,1792]{1,0:T(8,128)(2,1)}, bf16[224,1792]{1,0:T(8,128)(2,1)}, u32[]{:S(2)}, u32[]{:S(2)}) collective-permute-start(bf16[224,1792]{1,0:T(8,128)(2,1)} %concatenate.83), channel_id=1, source_target_pairs={{0,16},{16,0},{1,17},{17,1},{2,18},{18,2},{3,19},{19,3},{4,20},{20... | collective-permute-start | bytes 2408456 | tf_op jit(solution)/shard_map/ppermute | solution.py:28
  186.6 16.2 %collective-permute-start.21 = (bf16[224,1216]{1,0:T(8,128)(2,1)}, bf16[224,1216]{1,0:T(8,128)(2,1)}, u32[]{:S(2)}, u32[]{:S(2)}) collective-permute-start(bf16[224,1216]{1,0:T(8,128)(2,1)} %param.24), channel_id=1, source_target_pairs={{0,0},{1,4},{2,8},{3,12},{4,1},{5,5},{6,9},{7,13},{8,2},{9,6},{10,... | collective-permute-start | bytes 1634312 | tf_op jit(solution)/shard_map/ppermute | solution.py:80
  202.9 301.7 %all-gather.5.cloned.1.call-start = ((), (), s32[]{:S(2)}) async-start(), calls=%async_computation | async-start | bytes 5160960 | tf_op jit(solution)/shard_map/all_gather | solution.py:129
  206.6 70.2 %collective-permute-start.16 = (bf16[2,224,1792]{2,1,0:T(8,128)(2,1)S(1)}, bf16[2,224,1792]{2,1,0:T(8,128)(2,1)S(1)}, u32[]{:S(2)}, u32[]{:S(2)}) collective-permute-start(bf16[2,224,1792]{2,1,0:T(8,128)(2,1)S(1)} %pad_maximum_fusion.12), channel_id=1, source_target_pairs={{0,8},{8,0},{1,9},{9,1},{2,10},{10,2},{3,11},{11,3},{4,12},{12,4},... | collective-permute-start | bytes 4816904 | tf_op jit(solution)/shard_map/ppermute | solution.py:28
  250.8 140.2 %collective-permute-start.11 = (bf16[2,2,224,3584]{3,2,0,1:T(8,128)(2,1)}, bf16[2,2,224,3584]{3,2,0,1:T(8,128)(2,1)}, u32[]{:S(2)}, u32[]{:S(2)}) collective-permute-start(bf16[2,2,224,3584]{3,2,0,1:T(8,128)(2,1)} %pad_maximum_fusion.3), channel_id=1, source_target_pairs={{0,4},{4,0},{1,5},{5,1},{2,6},{6,2},{3,7},{7,3},{8,12},{12,8},{9,1... | collective-permute-start | bytes 19267592 | tf_op jit(solution)/shard_map/ppermute | solution.py:28
  280.1 104.0 %collective-permute-start.17 = (bf16[2,2,224,1792]{3,2,0,1:T(8,128)(2,1)}, bf16[2,2,224,1792]{3,2,0,1:T(8,128)(2,1)}, u32[]{:S(2)}, u32[]{:S(2)}) collective-permute-start(bf16[2,2,224,1792]{3,2,0,1:T(8,128)(2,1)} %pad_maximum_fusion.9), channel_id=1, source_target_pairs={{0,4},{4,0},{1,5},{5,1},{2,6},{6,2},{3,7},{7,3},{8,12},{12,8},{9,1... | collective-permute-start | bytes 9633800 | tf_op jit(solution)/shard_map/ppermute | solution.py:28
  280.1 95.4 %collective-permute-start = (f32[3,448]{1,0:T(4,128)S(1)}, f32[3,448]{1,0:T(4,128)S(1)}, u32[]{:S(2)}, u32[]{:S(2)}) collective-permute-start(f32[3,448]{1,0:T(4,128)S(1)} %copy-done.61), channel_id=1, source_target_pairs={{0,1},{1,2},{2,3},{3,0},{4,5},{5,6},{6,7},{7,4},{8,9},{9,10},{10,1... | collective-permute-start | bytes 16136 | tf_op jit(solution)/shard_map/ppermute | solution.py:28
  280.1 95.6 %collective-permute-start.1 = (f32[3,448]{1,0:T(4,128)S(1)}, f32[3,448]{1,0:T(4,128)S(1)}, u32[]{:S(2)}, u32[]{:S(2)}) collective-permute-start(f32[3,448]{1,0:T(4,128)S(1)} %copy-done.61), channel_id=1, source_target_pairs={{0,2},{1,3},{2,0},{3,1},{4,6},{5,7},{6,4},{7,5},{8,10},{9,11},{10,... | collective-permute-start | bytes 16136 | tf_op jit(solution)/shard_map/ppermute | solution.py:28
  282.4 101.7 %collective-permute-start.20 = (bf16[224,1216]{1,0:T(8,128)(2,1)}, bf16[224,1216]{1,0:T(8,128)(2,1)}, u32[]{:S(2)}, u32[]{:S(2)}) collective-permute-start(bf16[224,1216]{1,0:T(8,128)(2,1)} %param.23), channel_id=1, source_target_pairs={{0,0},{1,4},{2,8},{3,12},{4,1},{5,5},{6,9},{7,13},{8,2},{9,6},{10,... | collective-permute-start | bytes 1634312 | tf_op jit(solution)/shard_map/ppermute | solution.py:80
  375.5 8.4 collective-permute-start.2
  375.8 56.6 %collective-permute-start.25 = (bf16[512,1792]{1,0:T(8,128)(2,1)}, bf16[512,1792]{1,0:T(8,128)(2,1)}, u32[]{:S(2)}, u32[]{:S(2)}) collective-permute-start(bf16[512,1792]{1,0:T(8,128)(2,1)} %bitcast.277), channel_id=1, source_target_pairs={{0,8},{8,0},{1,9},{9,1},{2,10},{10,2},{3,11},{11,3},{4,12},{12,4},... | collective-permute-start | bytes 5505032 | tf_op jit(solution)/shard_map/ppermute | solution.py:28
  425.8 45.1 %collective-permute-start.18 = (bf16[512,1792]{1,0:T(8,128)(2,1)S(1)}, bf16[512,1792]{1,0:T(8,128)(2,1)S(1)}, u32[]{:S(2)}, u32[]{:S(2)}) collective-permute-start(bf16[512,1792]{1,0:T(8,128)(2,1)S(1)} %multiply_convert_fusion.4), channel_id=1, source_target_pairs={{0,8},{8,0},{1,9},{9,1},{2,10},{10,2},{3,11},{11,3},{4,12},{12,4},... | collective-permute-start | bytes 5505032 | tf_op jit(solution)/shard_map/ppermute | solution.py:28
  435.9 37.4 %collective-permute-start.26 = (bf16[1024,1792]{1,0:T(8,128)(2,1)}, bf16[1024,1792]{1,0:T(8,128)(2,1)}, u32[]{:S(2)}, u32[]{:S(2)}) collective-permute-start(bf16[1024,1792]{1,0:T(8,128)(2,1)} %pad_maximum_fusion.7), channel_id=1, source_target_pairs={{0,4},{4,0},{1,5},{5,1},{2,6},{6,2},{3,7},{7,3},{8,12},{12,8},{9,1... | collective-permute-start | bytes 11010056 | tf_op jit(solution)/shard_map/ppermute | solution.py:28
  473.3 15.6 %collective-permute-start.19 = (bf16[1024,1792]{1,0:T(8,128)(2,1)}, bf16[1024,1792]{1,0:T(8,128)(2,1)}, u32[]{:S(2)}, u32[]{:S(2)}) collective-permute-start(bf16[1024,1792]{1,0:T(8,128)(2,1)} %pad_maximum_fusion.6), channel_id=1, source_target_pairs={{0,4},{4,0},{1,5},{5,1},{2,6},{6,2},{3,7},{7,3},{8,12},{12,8},{9,1... | collective-permute-start | bytes 11010056 | tf_op jit(solution)/shard_map/ppermute | solution.py:28
  553.6 109.0 %collective-permute-start.57 = (bf16[4,224,1216]{2,1,0:T(8,128)(2,1)}, bf16[4,224,1216]{2,1,0:T(8,128)(2,1)}, u32[]{:S(2)}, u32[]{:S(2)}) collective-permute-start(bf16[4,224,1216]{2,1,0:T(8,128)(2,1)} %dynamic-slice_bitcast_fusion), channel_id=1, source_target_pairs={{0,16},{16,0},{1,17},{17,1},{2,18},{18,2},{3,19},{19,3},{4,20},{20... | collective-permute-start | bytes 6537224 | tf_op jit(solution)/shard_map/ppermute | solution.py:28
  578.0 87.3 %collective-permute-start.52 = (bf16[4,224,1216]{2,1,0:T(8,128)(2,1)}, bf16[4,224,1216]{2,1,0:T(8,128)(2,1)}, u32[]{:S(2)}, u32[]{:S(2)}) collective-permute-start(bf16[4,224,1216]{2,1,0:T(8,128)(2,1)} %dynamic-slice_bitcast_fusion.1), channel_id=1, source_target_pairs={{0,16},{16,0},{1,17},{17,1},{2,18},{18,2},{3,19},{19,3},{4,20},{20... | collective-permute-start | bytes 6537224 | tf_op jit(solution)/shard_map/ppermute | solution.py:28
  603.7 100.7 %collective-permute-start.47 = (bf16[4,224,1216]{2,1,0:T(8,128)(2,1)}, bf16[4,224,1216]{2,1,0:T(8,128)(2,1)S(1)}, u32[]{:S(2)}, u32[]{:S(2)}) collective-permute-start(bf16[4,224,1216]{2,1,0:T(8,128)(2,1)} %dynamic-slice_bitcast_fusion.2), channel_id=1, source_target_pairs={{0,16},{16,0},{1,17},{17,1},{2,18},{18,2},{3,19},{19,3},{4,20},{20... | collective-permute-start | bytes 6537224 | tf_op jit(solution)/shard_map/ppermute | solution.py:28
  623.5 176.2 %collective-permute-start.23 = (bf16[1024,1792]{1,0:T(8,128)(2,1)}, bf16[1024,1792]{1,0:T(8,128)(2,1)}, u32[]{:S(2)}, u32[]{:S(2)}) collective-permute-start(bf16[1024,1792]{1,0:T(8,128)(2,1)} %slice.306), channel_id=1, source_target_pairs={{0,4},{4,0},{1,5},{5,1},{2,6},{6,2},{3,7},{7,3},{8,12},{12,8},{9,1... | collective-permute-start | bytes 11010056 | tf_op jit(solution)/shard_map/ppermute | solution.py:28
  662.0 112.6 %collective-permute-start.27 = (bf16[1024,1792]{1,0:T(8,128)(2,1)S(1)}, bf16[1024,1792]{1,0:T(8,128)(2,1)S(1)}, u32[]{:S(2)}, u32[]{:S(2)}) collective-permute-start(bf16[1024,1792]{1,0:T(8,128)(2,1)S(1)} %slice.305), channel_id=1, source_target_pairs={{0,4},{4,0},{1,5},{5,1},{2,6},{6,2},{3,7},{7,3},{8,12},{12,8},{9,1... | collective-permute-start | bytes 11010056 | tf_op jit(solution)/shard_map/ppermute | solution.py:28
  665.2 42.7 %collective-permute-start.58 = (bf16[224,1216]{1,0:T(8,128)(2,1)S(1)}, bf16[224,1216]{1,0:T(8,128)(2,1)S(1)}, u32[]{:S(2)}, u32[]{:S(2)}) collective-permute-start(bf16[224,1216]{1,0:T(8,128)(2,1)S(1)} %get-tuple-element.66), channel_id=1, source_target_pairs={{0,3},{1,0},{2,1},{3,2},{4,7},{5,4},{6,5},{7,6},{8,11},{9,8},{10,9... | collective-permute-start | bytes 1634312 | tf_op jit(solution)/shard_map/ppermute | solution.py:28
  665.3 44.7 %collective-permute-start.59 = (bf16[224,1216]{1,0:T(8,128)(2,1)S(1)}, bf16[224,1216]{1,0:T(8,128)(2,1)S(1)}, u32[]{:S(2)}, u32[]{:S(2)}) collective-permute-start(bf16[224,1216]{1,0:T(8,128)(2,1)S(1)} %get-tuple-element.68), channel_id=1, source_target_pairs={{0,2},{1,3},{2,0},{3,1},{4,6},{5,7},{6,4},{7,5},{8,10},{9,11},{10,... | collective-permute-start | bytes 1634312 | tf_op jit(solution)/shard_map/ppermute | solution.py:28
  705.8 27.8 %collective-permute-start.60 = (bf16[224,1216]{1,0:T(8,128)(2,1)S(1)}, bf16[224,1216]{1,0:T(8,128)(2,1)S(1)}, u32[]{:S(2)}, u32[]{:S(2)}) collective-permute-start(bf16[224,1216]{1,0:T(8,128)(2,1)S(1)} %get-tuple-element.67), channel_id=1, source_target_pairs={{0,1},{1,2},{2,3},{3,0},{4,5},{5,6},{6,7},{7,4},{8,9},{9,10},{10,1... | collective-permute-start | bytes 1634312 | tf_op jit(solution)/shard_map/ppermute | solution.py:28
  707.9 28.0 %collective-permute-start.53 = (bf16[224,1216]{1,0:T(8,128)(2,1)S(1)}, bf16[224,1216]{1,0:T(8,128)(2,1)S(1)}, u32[]{:S(2)}, u32[]{:S(2)}) collective-permute-start(bf16[224,1216]{1,0:T(8,128)(2,1)S(1)} %get-tuple-element.69), channel_id=1, source_target_pairs={{0,3},{1,0},{2,1},{3,2},{4,7},{5,4},{6,5},{7,6},{8,11},{9,8},{10,9... | collective-permute-start | bytes 1634312 | tf_op jit(solution)/shard_map/ppermute | solution.py:28
  710.0 58.7 %collective-permute-start.54 = (bf16[224,1216]{1,0:T(8,128)(2,1)S(1)}, bf16[224,1216]{1,0:T(8,128)(2,1)S(1)}, u32[]{:S(2)}, u32[]{:S(2)}) collective-permute-start(bf16[224,1216]{1,0:T(8,128)(2,1)S(1)} %get-tuple-element.71), channel_id=1, source_target_pairs={{0,2},{1,3},{2,0},{3,1},{4,6},{5,7},{6,4},{7,5},{8,10},{9,11},{10,... | collective-permute-start | bytes 1634312 | tf_op jit(solution)/shard_map/ppermute | solution.py:28
  733.5 39.9 %collective-permute-start.55 = (bf16[224,1216]{1,0:T(8,128)(2,1)S(1)}, bf16[224,1216]{1,0:T(8,128)(2,1)S(1)}, u32[]{:S(2)}, u32[]{:S(2)}) collective-permute-start(bf16[224,1216]{1,0:T(8,128)(2,1)S(1)} %get-tuple-element.70), channel_id=1, source_target_pairs={{0,1},{1,2},{2,3},{3,0},{4,5},{5,6},{6,7},{7,4},{8,9},{9,10},{10,1... | collective-permute-start | bytes 1634312 | tf_op jit(solution)/shard_map/ppermute | solution.py:28
  735.9 73.8 %collective-permute-start.48 = (bf16[224,1216]{1,0:T(8,128)(2,1)}, bf16[224,1216]{1,0:T(8,128)(2,1)}, u32[]{:S(2)}, u32[]{:S(2)}) collective-permute-start(bf16[224,1216]{1,0:T(8,128)(2,1)} %get-tuple-element.72), channel_id=1, source_target_pairs={{0,3},{1,0},{2,1},{3,2},{4,7},{5,4},{6,5},{7,6},{8,11},{9,8},{10,9... | collective-permute-start | bytes 1634312 | tf_op jit(solution)/shard_map/ppermute | solution.py:28
  768.6 55.5 %collective-permute-start.49 = (bf16[224,1216]{1,0:T(8,128)(2,1)}, bf16[224,1216]{1,0:T(8,128)(2,1)}, u32[]{:S(2)}, u32[]{:S(2)}) collective-permute-start(bf16[224,1216]{1,0:T(8,128)(2,1)} %get-tuple-element.74), channel_id=1, source_target_pairs={{0,2},{1,3},{2,0},{3,1},{4,6},{5,7},{6,4},{7,5},{8,10},{9,11},{10,... | collective-permute-start | bytes 1634312 | tf_op jit(solution)/shard_map/ppermute | solution.py:28
  773.5 55.6 %collective-permute-start.50 = (bf16[224,1216]{1,0:T(8,128)(2,1)}, bf16[224,1216]{1,0:T(8,128)(2,1)}, u32[]{:S(2)}, u32[]{:S(2)}) collective-permute-start(bf16[224,1216]{1,0:T(8,128)(2,1)} %get-tuple-element.73), channel_id=1, source_target_pairs={{0,1},{1,2},{2,3},{3,0},{4,5},{5,6},{6,7},{7,4},{8,9},{9,10},{10,1... | collective-permute-start | bytes 1634312 | tf_op jit(solution)/shard_map/ppermute | solution.py:28
  774.6 81.0 %collective-permute-start.61 = (bf16[224,1216]{1,0:T(8,128)(2,1)}, bf16[224,1216]{1,0:T(8,128)(2,1)}, u32[]{:S(2)}, u32[]{:S(2)}) collective-permute-start(bf16[224,1216]{1,0:T(8,128)(2,1)} %fusion.29), channel_id=1, source_target_pairs={{0,0},{1,4},{2,8},{3,12},{4,1},{5,5},{6,9},{7,13},{8,2},{9,6},{10,... | collective-permute-start | bytes 1634312 | tf_op jit(solution)/shard_map/ppermute | solution.py:80
  799.7 67.1 %collective-permute-start.28 = (bf16[512,1792]{1,0:T(8,128)(2,1)}, bf16[512,1792]{1,0:T(8,128)(2,1)}, u32[]{:S(2)}, u32[]{:S(2)}) collective-permute-start(bf16[512,1792]{1,0:T(8,128)(2,1)} %slice.307), channel_id=1, source_target_pairs={{0,8},{8,0},{1,9},{9,1},{2,10},{10,2},{3,11},{11,3},{4,12},{12,4},... | collective-permute-start | bytes 5505032 | tf_op jit(solution)/shard_map/ppermute | solution.py:28
  809.7 48.1 %collective-permute-start.56 = (bf16[224,1216]{1,0:T(8,128)(2,1)}, bf16[224,1216]{1,0:T(8,128)(2,1)}, u32[]{:S(2)}, u32[]{:S(2)}) collective-permute-start(bf16[224,1216]{1,0:T(8,128)(2,1)} %fusion.32), channel_id=1, source_target_pairs={{0,0},{1,4},{2,8},{3,12},{4,1},{5,5},{6,9},{7,13},{8,2},{9,6},{10,... | collective-permute-start | bytes 1634312 | tf_op jit(solution)/shard_map/ppermute | solution.py:80
  824.1 92.9 %collective-permute-start.24 = (bf16[512,1792]{1,0:T(8,128)(2,1)}, bf16[512,1792]{1,0:T(8,128)(2,1)}, u32[]{:S(2)}, u32[]{:S(2)}) collective-permute-start(bf16[512,1792]{1,0:T(8,128)(2,1)} %slice.308), channel_id=1, source_target_pairs={{0,8},{8,0},{1,9},{9,1},{2,10},{10,2},{3,11},{11,3},{4,12},{12,4},... | collective-permute-start | bytes 5505032 | tf_op jit(solution)/shard_map/ppermute | solution.py:28
  831.6 30.4 %collective-permute-start.51 = (bf16[224,1216]{1,0:T(8,128)(2,1)}, bf16[224,1216]{1,0:T(8,128)(2,1)S(1)}, u32[]{:S(2)}, u32[]{:S(2)}) collective-permute-start(bf16[224,1216]{1,0:T(8,128)(2,1)} %fusion.35), channel_id=1, source_target_pairs={{0,0},{1,4},{2,8},{3,12},{4,1},{5,5},{6,9},{7,13},{8,2},{9,6},{10,... | collective-permute-start | bytes 1634312 | tf_op jit(solution)/shard_map/ppermute | solution.py:80
  948.6 161.7 %collective-permute-start.41 = (bf16[2,2,224,1792]{3,2,0,1:T(8,128)(2,1)}, bf16[2,2,224,1792]{3,2,0,1:T(8,128)(2,1)}, u32[]{:S(2)}, u32[]{:S(2)}) collective-permute-start(bf16[2,2,224,1792]{3,2,0,1:T(8,128)(2,1)} %bitcast.249), channel_id=1, source_target_pairs={{0,4},{4,0},{1,5},{5,1},{2,6},{6,2},{3,7},{7,3},{8,12},{12,8},{9,1... | collective-permute-start | bytes 9633800 | tf_op jit(solution)/shard_map/ppermute | solution.py:28
  957.7 156.2 %collective-permute-start.35 = (bf16[2,2,224,1792]{3,2,0,1:T(8,128)(2,1)}, bf16[2,2,224,1792]{3,2,0,1:T(8,128)(2,1)}, u32[]{:S(2)}, u32[]{:S(2)}) collective-permute-start(bf16[2,2,224,1792]{3,2,0,1:T(8,128)(2,1)} %bitcast.250), channel_id=1, source_target_pairs={{0,4},{4,0},{1,5},{5,1},{2,6},{6,2},{3,7},{7,3},{8,12},{12,8},{9,1... | collective-permute-start | bytes 9633800 | tf_op jit(solution)/shard_map/ppermute | solution.py:28
  1041.0 77.4 %collective-permute-start.29 = (bf16[2,2,224,1792]{3,2,0,1:T(8,128)(2,1)}, bf16[2,2,224,1792]{3,2,0,1:T(8,128)(2,1)}, u32[]{:S(2)}, u32[]{:S(2)}) collective-permute-start(bf16[2,2,224,1792]{3,2,0,1:T(8,128)(2,1)} %bitcast.251), channel_id=1, source_target_pairs={{0,4},{4,0},{1,5},{5,1},{2,6},{6,2},{3,7},{7,3},{8,12},{12,8},{9,1... | collective-permute-start | bytes 9633800 | tf_op jit(solution)/shard_map/ppermute | solution.py:28
  1113.0 38.1 %collective-permute-start.42 = (bf16[2,224,1792]{2,1,0:T(8,128)(2,1)S(1)}, bf16[2,224,1792]{2,1,0:T(8,128)(2,1)S(1)}, u32[]{:S(2)}, u32[]{:S(2)}) collective-permute-start(bf16[2,224,1792]{2,1,0:T(8,128)(2,1)S(1)} %fusion.26), channel_id=1, source_target_pairs={{0,8},{8,0},{1,9},{9,1},{2,10},{10,2},{3,11},{11,3},{4,12},{12,4},... | collective-permute-start | bytes 4816904 | tf_op jit(solution)/shard_map/ppermute | solution.py:28
  1117.5 68.1 %collective-permute-start.36 = (bf16[2,224,1792]{2,1,0:T(8,128)(2,1)S(1)}, bf16[2,224,1792]{2,1,0:T(8,128)(2,1)S(1)}, u32[]{:S(2)}, u32[]{:S(2)}) collective-permute-start(bf16[2,224,1792]{2,1,0:T(8,128)(2,1)S(1)} %fusion.25), channel_id=1, source_target_pairs={{0,8},{8,0},{1,9},{9,1},{2,10},{10,2},{3,11},{11,3},{4,12},{12,4},... | collective-permute-start | bytes 4816904 | tf_op jit(solution)/shard_map/ppermute | solution.py:28
  1121.9 95.5 %collective-permute-start.30 = (bf16[2,224,1792]{2,1,0:T(8,128)(2,1)S(1)}, bf16[2,224,1792]{2,1,0:T(8,128)(2,1)S(1)}, u32[]{:S(2)}, u32[]{:S(2)}) collective-permute-start(bf16[2,224,1792]{2,1,0:T(8,128)(2,1)S(1)} %fusion.24), channel_id=1, source_target_pairs={{0,8},{8,0},{1,9},{9,1},{2,10},{10,2},{3,11},{11,3},{4,12},{12,4},... | collective-permute-start | bytes 4816904 | tf_op jit(solution)/shard_map/ppermute | solution.py:28
  1151.5 67.4 %collective-permute-start.43 = (bf16[224,1792]{1,0:T(8,128)(2,1)S(1)}, bf16[224,1792]{1,0:T(8,128)(2,1)S(1)}, u32[]{:S(2)}, u32[]{:S(2)}) collective-permute-start(bf16[224,1792]{1,0:T(8,128)(2,1)S(1)} %fusion.38), channel_id=1, source_target_pairs={{0,16},{16,0},{1,17},{17,1},{2,18},{18,2},{3,19},{19,3},{4,20},{20... | collective-permute-start | bytes 2408456 | tf_op jit(solution)/shard_map/ppermute | solution.py:28
  1185.9 39.3 %collective-permute-start.37 = (bf16[224,1792]{1,0:T(8,128)(2,1)S(1)}, bf16[224,1792]{1,0:T(8,128)(2,1)S(1)}, u32[]{:S(2)}, u32[]{:S(2)}) collective-permute-start(bf16[224,1792]{1,0:T(8,128)(2,1)S(1)} %fusion.37), channel_id=1, source_target_pairs={{0,16},{16,0},{1,17},{17,1},{2,18},{18,2},{3,19},{19,3},{4,20},{20... | collective-permute-start | bytes 2408456 | tf_op jit(solution)/shard_map/ppermute | solution.py:28
  1217.8 17.4 %collective-permute-start.31 = (bf16[224,1792]{1,0:T(8,128)(2,1)S(1)}, bf16[224,1792]{1,0:T(8,128)(2,1)S(1)}, u32[]{:S(2)}, u32[]{:S(2)}) collective-permute-start(bf16[224,1792]{1,0:T(8,128)(2,1)S(1)} %fusion.36), channel_id=1, source_target_pairs={{0,16},{16,0},{1,17},{17,1},{2,18},{18,2},{3,19},{19,3},{4,20},{20... | collective-permute-start | bytes 2408456 | tf_op jit(solution)/shard_map/ppermute | solution.py:28
  1219.3 19.4 %collective-permute-start.44 = (bf16[224,448]{1,0:T(8,128)(2,1)S(1)}, bf16[224,448]{1,0:T(8,128)(2,1)S(1)}, u32[]{:S(2)}, u32[]{:S(2)}) collective-permute-start(bf16[224,448]{1,0:T(8,128)(2,1)S(1)} %get-tuple-element.89), channel_id=1, source_target_pairs={{0,3},{1,0},{2,1},{3,2},{4,7},{5,4},{6,5},{7,6},{8,11},{9,8},{10,9... | collective-permute-start | bytes 602120 | tf_op jit(solution)/shard_map/ppermute | solution.py:28
  1221.5 18.9 %collective-permute-start.45 = (bf16[224,448]{1,0:T(8,128)(2,1)S(1)}, bf16[224,448]{1,0:T(8,128)(2,1)S(1)}, u32[]{:S(2)}, u32[]{:S(2)}) collective-permute-start(bf16[224,448]{1,0:T(8,128)(2,1)S(1)} %get-tuple-element.91), channel_id=1, source_target_pairs={{0,2},{1,3},{2,0},{3,1},{4,6},{5,7},{6,4},{7,5},{8,10},{9,11},{10,... | collective-permute-start | bytes 602120 | tf_op jit(solution)/shard_map/ppermute | solution.py:28
  1222.4 30.2 %collective-permute-start.46 = (bf16[224,448]{1,0:T(8,128)(2,1)S(1)}, bf16[224,448]{1,0:T(8,128)(2,1)S(1)}, u32[]{:S(2)}, u32[]{:S(2)}) collective-permute-start(bf16[224,448]{1,0:T(8,128)(2,1)S(1)} %get-tuple-element.90), channel_id=1, source_target_pairs={{0,1},{1,2},{2,3},{3,0},{4,5},{5,6},{6,7},{7,4},{8,9},{9,10},{10,1... | collective-permute-start | bytes 602120 | tf_op jit(solution)/shard_map/ppermute | solution.py:28
  1225.7 32.0 %collective-permute-start.38 = (bf16[224,448]{1,0:T(8,128)(2,1)S(1)}, bf16[224,448]{1,0:T(8,128)(2,1)S(1)}, u32[]{:S(2)}, u32[]{:S(2)}) collective-permute-start(bf16[224,448]{1,0:T(8,128)(2,1)S(1)} %get-tuple-element.92), channel_id=1, source_target_pairs={{0,3},{1,0},{2,1},{3,2},{4,7},{5,4},{6,5},{7,6},{8,11},{9,8},{10,9... | collective-permute-start | bytes 602120 | tf_op jit(solution)/shard_map/ppermute | solution.py:28
  1235.2 28.5 %collective-permute-start.39 = (bf16[224,448]{1,0:T(8,128)(2,1)S(1)}, bf16[224,448]{1,0:T(8,128)(2,1)S(1)}, u32[]{:S(2)}, u32[]{:S(2)}) collective-permute-start(bf16[224,448]{1,0:T(8,128)(2,1)S(1)} %get-tuple-element.94), channel_id=1, source_target_pairs={{0,2},{1,3},{2,0},{3,1},{4,6},{5,7},{6,4},{7,5},{8,10},{9,11},{10,... | collective-permute-start | bytes 602120 | tf_op jit(solution)/shard_map/ppermute | solution.py:28
  1238.8 24.9 %collective-permute-start.40 = (bf16[224,448]{1,0:T(8,128)(2,1)S(1)}, bf16[224,448]{1,0:T(8,128)(2,1)S(1)}, u32[]{:S(2)}, u32[]{:S(2)}) collective-permute-start(bf16[224,448]{1,0:T(8,128)(2,1)S(1)} %get-tuple-element.93), channel_id=1, source_target_pairs={{0,1},{1,2},{2,3},{3,0},{4,5},{5,6},{6,7},{7,4},{8,9},{9,10},{10,1... | collective-permute-start | bytes 602120 | tf_op jit(solution)/shard_map/ppermute | solution.py:28
  1240.4 24.2 %collective-permute-start.32 = (bf16[224,448]{1,0:T(8,128)(2,1)S(1)}, bf16[224,448]{1,0:T(8,128)(2,1)S(1)}, u32[]{:S(2)}, u32[]{:S(2)}) collective-permute-start(bf16[224,448]{1,0:T(8,128)(2,1)S(1)} %get-tuple-element.95), channel_id=1, source_target_pairs={{0,3},{1,0},{2,1},{3,2},{4,7},{5,4},{6,5},{7,6},{8,11},{9,8},{10,9... | collective-permute-start | bytes 602120 | tf_op jit(solution)/shard_map/ppermute | solution.py:28
  1252.6 22.9 %collective-permute-start.33 = (bf16[224,448]{1,0:T(8,128)(2,1)S(1)}, bf16[224,448]{1,0:T(8,128)(2,1)S(1)}, u32[]{:S(2)}, u32[]{:S(2)}) collective-permute-start(bf16[224,448]{1,0:T(8,128)(2,1)S(1)} %get-tuple-element.97), channel_id=1, source_target_pairs={{0,2},{1,3},{2,0},{3,1},{4,6},{5,7},{6,4},{7,5},{8,10},{9,11},{10,... | collective-permute-start | bytes 602120 | tf_op jit(solution)/shard_map/ppermute | solution.py:28
  1257.6 19.4 %collective-permute-start.34 = (bf16[224,448]{1,0:T(8,128)(2,1)S(1)}, bf16[224,448]{1,0:T(8,128)(2,1)S(1)}, u32[]{:S(2)}, u32[]{:S(2)}) collective-permute-start(bf16[224,448]{1,0:T(8,128)(2,1)S(1)} %get-tuple-element.96), channel_id=1, source_target_pairs={{0,1},{1,2},{2,3},{3,0},{4,5},{5,6},{6,7},{7,4},{8,9},{9,10},{10,1... | collective-permute-start | bytes 602120 | tf_op jit(solution)/shard_map/ppermute | solution.py:28
  (77 other events, 1401.8 us)
Sparse Core Ops, SparseCore 0:
  25.0 139.0 all-gather.8
  203.0 103.5 all-gather.6
  384.2 80.8 all-gather.4

commit v2 on v1

v2 whole, which is shorter than its diff:
```python
import functools

import jax
import jax.numpy as jnp
from jax import lax
from jax.experimental import pallas as pl
from jax.experimental.pallas import tpu as pltpu
from jax.sharding import Mesh
from jax.sharding import PartitionSpec as P

BLOCK = 128
EPSILON = 1e-05
F32 = jnp.float32
BF16 = jnp.bfloat16
EVERY = ("a", "b", "c", "z")


def dot_nn(left, right):
    return lax.dot_general(left, right, (((1,), (0,)), ((), ())), preferred_element_type=F32)


def dot_nt(left, right):
    return lax.dot_general(left, right, (((1,), (1,)), ((), ())), preferred_element_type=F32)


def dot_tn(left, right):
    return lax.dot_general(left, right, (((0,), (0,)), ((), ())), preferred_element_type=F32)


def shift_by(value, axis, amount):
    size = lax.axis_size(axis)
    return lax.ppermute(value, axis, [(i, (i + amount) % size) for i in range(size)])


def pieces_of(value, axis):
    return [value] + [shift_by(value, axis, s) for s in range(1, lax.axis_size(axis))]


def near_pieces(value, axis):
    return shift_by(value, axis, 1), shift_by(value, axis, -1)


def far_pieces(value, near, axis):
    size = lax.axis_size(axis)
    pieces = [value] + [None] * (size - 1)
    pieces[1], pieces[size - 1] = near
    for s in range(2, size // 2 + 1):
        pieces[s] = shift_by(pieces[s - 1], axis, 1)
    for s in range(2, (size - 1) // 2 + 1):
        pieces[size - s] = shift_by(pieces[size - s + 1], axis, -1)
    return pieces


def phase(*values):
    return lax.optimization_barrier(values)


def after(value, *earlier):
    return lax.optimization_barrier((value, earlier))[0]


def in_order(pieces, axis, dim):
    size, index = len(pieces), lax.axis_index(axis)
    if size == 2:
        first = index == 0
        return jnp.stack(
            [jnp.where(first, pieces[0], pieces[1]), jnp.where(first, pieces[1], pieces[0])], axis=dim
        )
    return jnp.stack(
        [lax.select_n((index - j) % size, *pieces) for j in range(size)], axis=dim
    )


def parted(terms, axis, dim):
    size, index = lax.axis_size(axis), lax.axis_index(axis)

    def slices(i):
        return [lax.dynamic_index_in_dim(t, i, dim, keepdims=False) for t in terms]

    return slices(index) + [
        shift_by(joined(slices((index - s) % size)).astype(BF16), axis, -s) for s in range(1, size)
    ]


def joined(terms):
    total = terms[0].astype(F32)
    for value in terms[1:]:
        total = total + value.astype(F32)
    return total


def columns_home(terms):
    count = lax.axis_size("z")
    local = terms[0].shape[1] // count

    def columns(s):
        return joined([t[:, s * local : (s + 1) * local] for t in terms])

    return [columns(0)] + [shift_by(columns(s).astype(BF16), "z", -s) for s in range(1, count)]


def swapped(block, back=False):
    count, size = lax.axis_size("z"), lax.axis_size("b")
    moves = []
    for t in range(count):
        for z in range(count):
            team = (z % size) * 2 + z // size
            moves.append((t * count + z, team * count + t))
    return lax.ppermute(block, ("b", "c", "z"), [(j, i) if back else (i, j) for i, j in moves])


def partner(value, bit):
    count = lax.axis_size(EVERY)
    return lax.ppermute(value, EVERY, [(i, i ^ bit) for i in range(count)])


def exchange_order():
    bits = [1 << i for i in range(lax.axis_size(EVERY).bit_length() - 1)]
    core = lax.axis_size("z")
    return [b for b in bits[::-1] if b > core] + [b for b in bits if b < core] + [core]


def entry_of(difference):
    return sum(((difference & bit) // bit) << i for i, bit in enumerate(exchange_order()))


def told(value, bits):
    for bit in bits:
        value = jnp.concatenate([value, partner(value, bit)], axis=0)
    return value


def middle_kernel(steps, *refs):
    near_hidden, far_hidden, near_cot, far_cot, w_gate, w_up, w_down = refs[:7]
    activated, grads, near_back, far_back, near_out, far_out = refs[-6:]
    units = w_down.shape[1]
    near = pl.program_id(0) < steps
    hidden = jnp.where(near, near_hidden[...], far_hidden[...])
    cot = jnp.where(near, near_cot[...], far_cot[...])
    gate = dot_nn(hidden, w_gate[...])
    up = dot_nn(hidden, w_up[...])
    grad = dot_nn(cot, w_down[...])
    sigmoid = 1.0 / (1.0 + jnp.exp(-gate))
    silu = gate * sigmoid
    active = (silu * up).astype(BF16)
    to_gate = (grad * up * (sigmoid * (1.0 + gate * (1.0 - sigmoid)))).astype(BF16)
    to_up = (grad * silu).astype(BF16)
    activated[...] = active
    grads[:, :units] = to_gate
    grads[:, units:] = to_up
    back = (dot_nt(to_gate, w_gate[...]) + dot_nt(to_up, w_up[...])).astype(BF16)
    out = dot_nt(active, w_down[...]).astype(BF16)

    @pl.when(near)
    def _():
        near_back[...] = back
        near_out[...] = out

    @pl.when(jnp.logical_not(near))
    def _():
        far_back[...] = back
        far_out[...] = out


def middle(part, parts, hidden, cot, w_gate, w_up, w_down, held):
    rows, width = hidden[0].shape
    units = w_down.shape[1]
    tile = min(rows, 256)
    steps = rows // tile
    near = pl.BlockSpec((tile, width), lambda i: (jnp.minimum(i, steps - 1), 0))
    far = pl.BlockSpec((tile, width), lambda i: (jnp.maximum(i - steps, 0), 0))
    weight = pl.BlockSpec((width, units), lambda i: (0, 0), pipeline_mode=pl.Buffered(1))
    results = [pl.BlockSpec((tile, n * units), lambda i: (part * 2 * steps + i, 0)) for n in (1, 2)]
    return pl.pallas_call(
        functools.partial(middle_kernel, steps),
        grid=(2 * steps,),
        in_specs=[near, far, near, far, weight, weight, weight]
        + [pl.BlockSpec(memory_space=pl.ANY)] * len(held),
        out_specs=results + [near, far] * 2,
        out_shape=[jax.ShapeDtypeStruct((parts * 2 * rows, n * units), BF16) for n in (1, 2)]
        + [jax.ShapeDtypeStruct((rows, width), BF16)] * 4,
        input_output_aliases={7 + i: i for i in range(len(held))},
        compiler_params=pltpu.CompilerParams(vmem_limit_bytes=58 * 2**20),
        cost_estimate=pl.CostEstimate(
            flops=24 * rows * width * units,
            bytes_accessed=2 * (8 * rows * width + 3 * width * units + 6 * rows * units),
            transcendentals=2 * rows * units,
        ),
        name="middle",
    )(*hidden, *cot, w_gate, w_up, w_down, *held)


def gradient_kernel(*refs, count, extra):
    side, tokens, right, result = refs[0], refs[1 : 1 + count], refs[1 + count], refs[-1]
    del side
    rows = tokens[0].shape[0]
    total = refs[2 + count][...].astype(F32) if extra else None
    for i in range(count):
        term = lax.dot_general(
            tokens[i][...], right[i * rows : (i + 1) * rows, :], (((0,), (0,)), ((), ())), preferred_element_type=F32
        )
        total = term if total is None else total + term
    result[...] = total.astype(BF16)


def gradient_half(side, tokens, right, units, column=0, extra=()):
    rows, width = tokens[0].shape
    count, half = len(tokens), width // 2
    tile = 256 if units % 256 == 0 else 128
    steps = units // tile
    out = pl.BlockSpec((half, tile), lambda j, side: (0, j))
    return pl.pallas_call(
        functools.partial(gradient_kernel, count=count, extra=len(extra)),
        grid_spec=pltpu.PrefetchScalarGridSpec(
            num_scalar_prefetch=1,
            grid=(steps,),
            in_specs=[
                pl.BlockSpec((rows, half), lambda j, side: (0, side[0]), pipeline_mode=pl.Buffered(1))
            ]
            * count
            + [pl.BlockSpec((count * rows, tile), lambda j, side: (0, column * steps + j))]
            + [out] * len(extra),
            out_specs=out,
        ),
        out_shape=jax.ShapeDtypeStruct((half, units), BF16),
        compiler_params=pltpu.CompilerParams(vmem_limit_bytes=40 * 2**20),
        cost_estimate=pl.CostEstimate(
            flops=2 * count * rows * half * units,
            bytes_accessed=2 * (count * rows * (half + units) + half * units),
            transcendentals=0,
        ),
        name="gradient_half",
    )(side.reshape(1).astype(jnp.int32), *tokens, right, *extra)


def split_kernel(core, left, right, kept, leaving):
    total = lax.dot_general(left[...], right[...], (((0,), (0,)), ((), ())), preferred_element_type=F32)
    groups, _, rows, _ = (kept.shape[0], 2, *kept.shape[1:])
    total = total.astype(BF16).reshape(groups, 2, rows, -1)
    first = core[0] == 0
    kept[...] = jnp.where(first, total[:, 0], total[:, 1])
    leaving[...] = jnp.where(first, total[:, 1], total[:, 0])


def split_gradient(core, left, right, groups):
    count, width = left.shape
    columns = right.shape[1]
    tile = 256
    rows = width // (2 * groups)
    out = pl.BlockSpec((groups, rows, tile), lambda j, core: (0, 0, j))
    return pl.pallas_call(
        split_kernel,
        grid_spec=pltpu.PrefetchScalarGridSpec(
            num_scalar_prefetch=1,
            grid=(columns // tile,),
            in_specs=[
                pl.BlockSpec((count, width), lambda j, core: (0, 0), pipeline_mode=pl.Buffered(1)),
                pl.BlockSpec((count, tile), lambda j, core: (0, j)),
            ],
            out_specs=[out, out],
        ),
        out_shape=[jax.ShapeDtypeStruct((groups, rows, columns), BF16)] * 2,
        compiler_params=pltpu.CompilerParams(vmem_limit_bytes=40 * 2**20),
        cost_estimate=pl.CostEstimate(
            flops=2 * count * width * columns,
            bytes_accessed=2 * (count * (width + columns) + width * columns),
            transcendentals=0,
        ),
        name="split_gradient",
    )(core.reshape(1).astype(jnp.int32), left, right)


def per_device(
    tokens,
    lengths,
    permutation,
    cotangent,
    norm1_gain,
    mixer_in,
    mixer_gate,
    conv_kernel,
    mixer_out,
    norm2_gain,
    ffn_gate,
    ffn_up,
    ffn_down,
):
    micro, length, width = tokens.shape
    count_b, count_z = lax.axis_size("b"), lax.axis_size("z")
    ia, ib, ic, iz = (lax.axis_index(n) for n in EVERY)
    place = ((ia * count_b + ib) * 2 + ic) * count_z + iz
    per_block = BLOCK // length
    blocks = permutation.shape[1]
    local = conv_kernel.shape[1]
    rows = micro * length

    dealt = lax.dynamic_slice_in_dim(permutation, place // per_block, 1, axis=1)[:, 0]
    own = dealt * per_block + place % per_block
    spots = jnp.arange(blocks, dtype=jnp.int32)

    def holder(piece):
        at = jnp.sum(jnp.where(permutation == (piece // per_block)[:, None], spots[None, :], 0), axis=1)
        return at * per_block + piece % per_block

    before = holder(jnp.maximum(own - 1, 0))
    last = blocks * per_block - 1
    behind = holder(jnp.minimum(own + 1, last))
    order = jnp.arange(lengths.shape[1], dtype=jnp.int32)
    offsets = jnp.sum(jnp.where(order[None, None, :] < order[None, :, None], lengths[:, None, :], 0), axis=2)
    position = own[:, None] * length + jnp.arange(length, dtype=jnp.int32)[None, :]
    is_start = jnp.any(position[:, :, None] == offsets[:, None, :], axis=2)
    was_start = jnp.any(position[:, :, None] - 1 == offsets[:, None, :], axis=2)
    keep_one = jnp.where(is_start, 0.0, 1.0).astype(F32)[:, :, None]
    keep_two = jnp.where(is_start | was_start, 0.0, 1.0).astype(F32)[:, :, None]

    units = -(-ffn_gate.shape[1] // 128) * 128
    spare = ((0, 0), (0, units - ffn_gate.shape[1]))

    def rows_of(pieces):
        return lax.all_gather(jnp.concatenate(pieces, axis=1), ("a", "b", "c"), axis=0, tiled=True)

    def told_at_once(value):
        return lax.all_gather(lax.all_gather(value, "z", axis=0), ("a", "b", "c"), axis=0)

    bits = exchange_order()
    hops = [tuple(bits[:-3]), *((b,) for b in bits[-3:])]
    tails = told(tokens[:, length - 2 :, :].reshape(1, micro * 2, width), hops[0])
    z_in = pieces_of(mixer_in, "z")
    taps = pieces_of(conv_kernel, "z")
    z_in, tails, taps, mixer_gate, ffn_gate_later, mixer_out = phase(
        z_in, tails, taps, mixer_gate, ffn_gate, mixer_out
    )
    w_in = rows_of(z_in)
    z_gate = pieces_of(mixer_gate, "z")
    swap_g = swapped(jnp.pad(ffn_gate_later, spare))
    tails = told(tails, hops[1])
    z_gate, swap_g, tails, mixer_out, ffn_up_later, ffn_down, cotangent_later = phase(
        z_gate, swap_g, tails, mixer_out, ffn_up, ffn_down, cotangent
    )
    w_gate = rows_of(z_gate)
    z_out = pieces_of(mixer_out, "z")
    near_g = near_pieces(swap_g, "z")
    tails = told(tails, hops[2])
    z_out, near_g, tails, cotangent_later, ffn_up_later, ffn_down, w_in = phase(
        z_out, near_g, tails, cotangent_later, ffn_up_later, ffn_down, w_in
    )
    w_out = rows_of(z_out)
    z_g = far_pieces(swap_g, near_g, "z")
    swap_u, swap_d = swapped(jnp.pad(ffn_up_later, spare)), swapped(jnp.pad(ffn_down, spare))
    tails = told(tails, hops[3])
    z_g, swap_u, swap_d, cotangent_later, tails, w_gate = phase(z_g, swap_u, swap_d, cotangent_later, tails, w_gate)
    y_g = pieces_of(in_order(z_g, "z", 0), "a")
    z_u = pieces_of(swap_u, "z")
    y_d = pieces_of(swap_d, "a")
    far_cotangent = pieces_of(cotangent_later.reshape(rows, width), "b")
    kernel = jnp.concatenate(taps, axis=1)

    tail_in = jnp.concatenate(
        [
            lax.dynamic_slice(tails, (entry_of(before[m] ^ place), 2 * m, 0), (1, 2, width))[0]
            for m in range(micro)
        ]
    ).astype(F32)
    local_in = tokens.reshape(rows, width).astype(F32)
    local_cot = cotangent.reshape(rows, width).astype(F32)
    scale_one = lax.rsqrt(jnp.mean(local_in * local_in, axis=1, keepdims=True) + EPSILON)
    normed_one = local_in * scale_one
    hidden_one = (normed_one * norm1_gain).astype(BF16)
    tail_scale = lax.rsqrt(jnp.mean(tail_in * tail_in, axis=1, keepdims=True) + EPSILON)
    tail_hidden = (tail_in * tail_scale * norm1_gain).astype(BF16)
    channels = kernel.shape[1]
    signal = dot_nn(hidden_one, w_in).reshape(micro, length, channels)
    tail_signal = dot_nn(tail_hidden, w_in).reshape(micro, 2, channels)
    gating = dot_nn(hidden_one, w_gate).reshape(micro, length, channels)
    extended = jnp.concatenate([tail_signal, signal], axis=1)
    shift_one = keep_one * extended[:, 1 : length + 1, :]
    shift_two = keep_two * extended[:, 0:length, :]
    mixed = kernel[0] * signal + kernel[1] * shift_one + kernel[2] * shift_two
    product = (mixed * gating).astype(BF16).reshape(rows, channels)
    residual = local_in + dot_nt(product, w_out)

    scale_two = lax.rsqrt(jnp.mean(residual * residual, axis=1, keepdims=True) + EPSILON)
    normed_two = residual * scale_two
    hidden_own = (normed_two * norm2_gain).astype(BF16)

    y_g, z_u, y_d, far_cotangent, hidden_own = phase(y_g, z_u, y_d, far_cotangent, hidden_own)
    half_d = in_order(y_d, "a", 0)
    near_d = near_pieces(half_d, "z")
    y_u = pieces_of(in_order(z_u, "z", 0), "a")
    ffn_g = in_order(y_g, "a", 0).reshape(-1, units)

    def with_core(pieces):
        return [v for piece in pieces for v in (piece, shift_by(piece, "c", 1))]

    cot_parts = with_core(far_cotangent)
    hidden_parts = with_core([hidden_own])
    far_hidden = pieces_of(hidden_own, "b")[1:]
    near_d, y_u, half_d, ffn_g, cot_parts, hidden_parts, far_hidden = phase(
        near_d, y_u, half_d, ffn_g, cot_parts, hidden_parts, far_hidden
    )
    ffn_d = in_order(far_pieces(half_d, near_d, "z"), "z", 1).reshape(-1, units)
    ffn_u = in_order(y_u, "a", 0).reshape(-1, units)
    hidden_parts = hidden_parts + with_core(far_hidden)
    held, backs, outs = (), [], []
    for s in range(count_b):
        pair = slice(2 * s, 2 * s + 2)
        *held, near_back, far_back, near_out, far_out = middle(
            s, count_b, hidden_parts[pair], cot_parts[pair], ffn_g, ffn_u, ffn_d, held
        )
        backs.append((near_back, shift_by(far_back, "c", 1)))
        outs.append((near_out, shift_by(far_out, "c", 1)))
    activated, grads = held

    other = 1 - ia

    def to_owners(sums):
        return [(near.astype(F32) + far.astype(F32)).astype(BF16) for near, far in sums[1:]]

    def passed(values):
        return [shift_by(v, "b", -1 - i) for i, v in enumerate(values)]

    leaving_gate = gradient_half(other, hidden_parts, grads, units)
    leaving_gate, backs, outs, hidden_parts, cot_parts = phase(leaving_gate, backs, outs, hidden_parts, cot_parts)
    come_gate, came_back = shift_by(leaving_gate, "a", 1), passed(to_owners(backs))
    leaving_up = gradient_half(other, hidden_parts, grads, units, 1)
    leaving_down = gradient_half(other, cot_parts, activated, units)
    stay_gate = gradient_half(ia, hidden_parts, grads, units)
    stay_up = gradient_half(ia, hidden_parts, grads, units, 1)
    stay_down = gradient_half(ia, cot_parts, activated, units)
    leaving_out = to_owners(outs)
    come_gate, came_back, leaving_up, leaving_down, stay_gate, stay_up, stay_down, outs, leaving_out = phase(
        come_gate, came_back, leaving_up, leaving_down, stay_gate, stay_up, stay_down, outs, leaving_out
    )
    come_up, came_out = shift_by(leaving_up, "a", 1), passed(leaving_out)

    def over_z(stay, come):
        return lax.psum_scatter(joined([stay, come]).astype(BF16), "z", scatter_dimension=0, tiled=True)

    grad_hidden_two = joined([*backs[0], *came_back])

    grad_gain_two = jnp.sum(grad_hidden_two * normed_two, axis=0)
    grad_norm_two = grad_hidden_two * norm2_gain
    inner_two = jnp.mean(grad_norm_two * normed_two, axis=1, keepdims=True)
    grad_residual = local_cot + scale_two * (grad_norm_two - normed_two * inner_two)
    grad_branch = grad_residual.astype(BF16)
    grad_product = dot_nn(grad_branch, w_out).reshape(micro, length, channels)
    def over_c(split):
        kept, leaving = split
        shape = (2, count_b, *kept.shape[1:])
        return [kept.reshape(shape), shift_by(leaving, "c", 1).reshape(shape)]

    def split(left, right):
        return split_gradient(ic, left, right, 2 * count_b)

    out_split = split(grad_branch, product)
    grad_mixed = grad_product * gating
    grad_gating = (grad_product * mixed).astype(BF16).reshape(rows, channels)
    grad_kernel = jnp.stack(
        [
            jnp.sum(grad_mixed * signal, axis=(0, 1)),
            jnp.sum(grad_mixed * shift_one, axis=(0, 1)),
            jnp.sum(grad_mixed * shift_two, axis=(0, 1)),
        ]
    )
    into_one = kernel[1] * (keep_one * grad_mixed)
    into_two = kernel[2] * (keep_two * grad_mixed)
    leaving = jnp.stack([into_two[:, 0], into_one[:, 0] + into_two[:, 1]], axis=1)
    blocked = leaving.reshape(micro, 2, count_z, local)

    def turned(value, dim):
        picks = [
            lax.dynamic_index_in_dim(value, (iz - j) % count_z, dim, keepdims=False) for j in range(count_z)
        ]
        return jnp.concatenate(picks, axis=-1)

    blocked = turned(blocked, 2).reshape(micro * 2, channels).astype(BF16)
    gate_split = split(hidden_one, grad_gating)
    blocked, come_up, came_out, out_split, gate_split, grad_mixed, leaving_down = phase(
        blocked, come_up, came_out, out_split, gate_split, grad_mixed, leaving_down
    )
    everyone = told_at_once(blocked)
    out_c, gate_c = over_c(out_split), over_c(gate_split)
    everyone, out_c, gate_c, grad_mixed, leaving_down, come_gate, come_up = phase(
        everyone, out_c, gate_c, grad_mixed, leaving_down, come_gate, come_up
    )

    def over_z(stay, come):
        return lax.psum_scatter(joined([stay, come]).astype(BF16), "z", scatter_dimension=0, tiled=True)

    come_down = shift_by(leaving_down, "a", 1)
    out_b = parted(out_c, "b", 1)
    scattered_gate, scattered_up = over_z(stay_gate, come_gate), over_z(stay_up, come_up)
    into_one = kernel[1] * (keep_one * grad_mixed)
    into_two = kernel[2] * (keep_two * grad_mixed)
    arrived = jnp.stack(
        [
            lax.dynamic_slice(
                everyone, (behind[m] // count_z, behind[m] % count_z, 2 * m, 0), (1, 1, 2, channels)
            )[0, 0]
            for m in range(micro)
        ]
    )
    arrived = turned(arrived.reshape(micro, 2, count_z, local), 2).astype(F32)
    arrived = jnp.where((own == last)[:, None, None], 0.0, arrived)
    from_one = jnp.concatenate([into_one[:, 1:], arrived[:, 1:]], axis=1)
    from_two = jnp.concatenate([into_two[:, 2:], arrived[:, :1], jnp.zeros_like(arrived[:, :1])], axis=1)
    grad_signal = (kernel[0] * grad_mixed + from_one + from_two).astype(BF16).reshape(rows, channels)
    in_split = split(hidden_one, grad_signal)
    grad_hidden_one = dot_nt(grad_signal, w_in) + dot_nt(grad_gating, w_gate)
    grad_gain_one = jnp.sum(grad_hidden_one * normed_one, axis=0)
    grad_norm_one = grad_hidden_one * norm1_gain
    inner_one = jnp.mean(grad_norm_one * normed_one, axis=1, keepdims=True)
    input_grad = grad_residual + scale_one * (grad_norm_one - normed_one * inner_one)
    come_down, out_b, in_split, gate_c, input_grad, scattered_gate, grad_gain_one, outs = phase(
        come_down, out_b, in_split, gate_c, input_grad, scattered_gate, grad_gain_one, outs
    )
    in_c = over_c(in_split)
    gate_b = parted(gate_c, "b", 1)
    out_a = parted(out_b, "a", 0)
    gate_home = swapped(scattered_gate, True)
    scattered_down = over_z(stay_down, come_down)
    output = (joined([*outs[0], *came_out]) + residual).astype(BF16)
    in_c, gate_b, out_a, gate_home, scattered_up, output = phase(
        in_c, gate_b, out_a, gate_home, scattered_up, output
    )
    in_b = parted(in_c, "b", 1)
    gate_a = parted(gate_b, "a", 0)
    out_z = columns_home(out_a)
    up_home = swapped(scattered_up, True)
    in_b, gate_a, out_z, up_home, scattered_down = phase(in_b, gate_a, out_z, up_home, scattered_down)
    in_a = parted(in_b, "a", 0)
    gate_z = columns_home(gate_a)
    down_home = swapped(scattered_down, True)
    small = jnp.concatenate(
        [grad_gain_one[None], grad_gain_two[None], turned(grad_kernel.reshape(3, count_z, local), 1)]
    )
    small = lax.all_gather(after(small, scattered_down), EVERY, axis=0)
    in_a, gate_z, down_home = phase(in_a, gate_z, down_home)
    in_z = columns_home(in_a)
    share = width // (4 * count_b * count_z)
    gains = lax.dynamic_slice_in_dim(small[:, :2], place * share, share, axis=2)
    tap_grads = lax.dynamic_slice_in_dim(
        small[:, 2:], (iz * 4 * count_b + place // count_z) * share, share, axis=2
    )
    gains, tap_grads = jnp.sum(gains, axis=0), jnp.sum(tap_grads, axis=0)
    grad_out, grad_gate_w, grad_in_w = (joined(t) for t in (out_z, gate_z, in_z))
    hidden_units = ffn_gate.shape[1]
    grad_ffg, grad_ffu, grad_down = (g[:, :hidden_units].astype(F32) for g in (gate_home, up_home, down_home))

    return (
        output.reshape(micro, length, width),
        input_grad.reshape(micro, length, width),
        gains[0],
        grad_in_w,
        grad_gate_w,
        tap_grads,
        grad_out,
        gains[1],
        grad_ffg,
        grad_ffu,
        grad_down,
    )


def solution(mesh):
    row, col = mesh.shape["row"], mesh.shape["col"]
    fine = Mesh(mesh.devices.reshape(2, row // 4, 2, col), EVERY)
    by_rows = ("a", "b", "c")
    matrix = P(by_rows, "z")
    token = P(None, EVERY, None)
    return jax.shard_map(
        per_device,
        mesh=fine,
        in_specs=(
            token,
            P(),
            P(),
            token,
            P(),
            matrix,
            matrix,
            P(None, "z"),
            matrix,
            P(),
            matrix,
            matrix,
            matrix,
        ),
        out_specs=(
            token,
            token,
            P(EVERY),
            matrix,
            matrix,
            P(None, ("z", *by_rows)),
            matrix,
            P(EVERY),
            matrix,
            matrix,
            matrix,
        ),
        check_vma=False,
    )
```

time: 1300 us -> 975 us (0.75)
  blocking collectives: 188 us -> 24.1 us
  matrix products: 199 us -> 51 us
  Pallas kernels: 0 us -> 145 us
  waiting for transfers between devices: 514 us -> 422 us
  starting transfers between devices: 161 us -> 118 us
  local copies, waits for them, and re-layouts: 96.9 us -> 61 us
  other arithmetic: 95 us -> 112 us
    ppermute x56 -> x57, waiting for transfers between devices: 483 us -> 274 us  [shift_by(): lax.ppermute(value, axis, [(i, (i + amount) % size) for i in range(size)])]
    pallas_call x0 -> x11, Pallas kernels: none -> 145 us  [the longest x2 78.9 us: middle(): pl.pallas_call(functools.partial(middle_kernel, steps), grid=(2 * steps,)...]
    all_gather x2, blocking collectives: 145 us -> 24.1 us  [the longest x1 13.3 us: told_at_once(): lax.all_gather(value, 'z', axis=0)]
    ppermute x6 -> x11, waiting for transfers between devices: 30.7 us -> 117 us  [the longest x6 73.4 us: swapped(): lax.ppermute(block, ('b', 'c', 'z'), [(j, i) if back else (i, j) for i, j...]
    dot_general x6 -> x0, matrix products: 55.8 us -> none  [dot_tn(): lax.dot_general(left, right, (((0,), (0,)), ((), ())), preferred_element_...]
    dot_general x5 -> x3, matrix products: 69.2 us -> 23.2 us  [dot_nt(): lax.dot_general(left, right, (((1,), (1,)), ((), ())), preferred_element_...]
    dot_general x6 -> x4, matrix products: 73.5 us -> 27.9 us  [dot_nn(): lax.dot_general(left, right, (((1,), (0,)), ((), ())), preferred_element_...]
    unnamed x1 -> x0, blocking collectives: 43.7 us -> none
  transfers between devices with their start and end apart: 65 -> 75, of which waited for: 28 -> 32; matrix products, arithmetic and copies ran while one was open for 23% -> 18% of each run, Pallas kernels for 0% -> 15%
where the time goes in v2:
time: 975 us; the launch traced here: 963 us
  waiting for transfers between devices  422 us (43%)
  Pallas kernels  145 us (15%)
  starting transfers between devices  118 us (12%)
  other arithmetic  112 us (11%)
  local copies, waits for them, and re-layouts  61 us (6%)
  matrix products  51 us (5%)
  between operations  28.8 us (3%)
  blocking collectives  24.1 us (2%)
    ppermute x57, waiting for transfers between devices, shift_by(): lax.ppermute(value, axis, [(i, (i + amount) % size) for i in range(size)])  274 us
    ppermute x57, starting transfers between devices, shift_by(): lax.ppermute(value, axis, [(i, (i + amount) % size) for i in range(size)])  99.4 us
    pallas_call x2, Pallas kernels, middle(): pl.pallas_call(functools.partial(middle_kernel, steps), grid=(2 * steps,)...  78.9 us
    ppermute x6, waiting for transfers between devices, swapped(): lax.ppermute(block, ('b', 'c', 'z'), [(j, i) if back else (i, j) for i, j...  73.4 us
    pallas_call x6, Pallas kernels, gradient_half(): pl.pallas_call(functools.partial(gradient_kernel, count=count, extra=len(...  48.8 us
    ppermute x5, waiting for transfers between devices, partner(): return lax.ppermute(value, EVERY, [(i, i ^ bit) for i in range(count)])  43.1 us
    dot_general x4, matrix products, dot_nn(): lax.dot_general(left, right, (((1,), (0,)), ((), ())), preferred_element_...  27.9 us
    dot_general x3, matrix products, dot_nt(): lax.dot_general(left, right, (((1,), (1,)), ((), ())), preferred_element_...  23.2 us
  transfers between devices with their start and end apart: 75, of which 32 were waited for; matrix products, arithmetic and copies ran while one was open for 18% of the time, Pallas kernels for 15%

profile of v2, /device:TPU:30, one launch (start us, length us, event | category | flops | bytes accessed | tf_op | source)
XLA Modules:
  0.0 962.7 jit_solution(1483723295935040669)
XLA Ops:
  20.7 14.7 %collective-permute-done.6 = f32[3,448]{1,0:T(4,128)S(1)} collective-permute-done((f32[3,448]{1,0:T(4,128)}, f32[3,448]{1,0:T(4,128)S(1)}, u32[]{:S(2)}, u32[]{:S(2)}) %collective-permute-start.6) | collective-permute-done | bytes 5408 | tf_op jit(solution)/shard_map/ppermute | solution.py:32
  44.9 10.5 %collective-permute-done.12 = bf16[4,8,1792]{2,1,0:T(8,128)(2,1)S(1)} collective-permute-done((bf16[4,8,1792]{2,1,0:T(8,128)(2,1)S(1)}, bf16[4,8,1792]{2,1,0:T(8,128)(2,1)S(1)}, u32[]{:S(2)}, u32[]{:S(2)}) %collective-permute-start.12) | collective-permute-done | bytes 114720 | tf_op jit(solution)/shard_map/ppermute | solution.py:114
  55.4 6.5 collective-permute-done.10
  62.0 23.6 %collective-permute-done.9 = bf16[224,448]{1,0:T(8,128)(2,1)S(1)} collective-permute-done((bf16[224,448]{1,0:T(8,128)(2,1)S(1)}, bf16[224,448]{1,0:T(8,128)(2,1)S(1)}, u32[]{:S(2)}, u32[]{:S(2)}) %collective-permute-start.9) | collective-permute-done | bytes 200736 | tf_op jit(solution)/shard_map/ppermute | solution.py:32
  94.4 29.3 %collective-permute-done.18 = bf16[8,8,1792]{2,1,0:T(8,128)(2,1)S(1)} collective-permute-done((bf16[8,8,1792]{2,1,0:T(8,128)(2,1)S(1)}, bf16[8,8,1792]{2,1,0:T(8,128)(2,1)S(1)}, u32[]{:S(2)}, u32[]{:S(2)}) %collective-permute-start.18) | collective-permute-done | bytes 229408 | tf_op jit(solution)/shard_map/ppermute | solution.py:114
  123.7 11.6 %collective-permute-start.15 = (bf16[224,448]{1,0:T(8,128)(2,1)S(1)}, bf16[224,448]{1,0:T(8,128)(2,1)S(1)}, u32[]{:S(2)}, u32[]{:S(2)}) collective-permute-start(bf16[224,448]{1,0:T(8,128)(2,1)S(1)} %copy-done.60), channel_id=1, source_target_pairs={{0,3},{1,0},{2,1},{3,2},{4,7},{5,4},{6,5},{7,6},{8,11},{9,8},{10,9... | collective-permute-start | bytes 602120 | tf_op jit(solution)/shard_map/ppermute | solution.py:32
  138.4 5.6 collective-permute-done.15
  166.8 8.2 fusion.2
  175.1 23.7 %collective-permute-done.20 = bf16[224,1280]{1,0:T(8,128)(2,1)} collective-permute-done((bf16[224,1280]{1,0:T(8,128)(2,1)S(1)}, bf16[224,1280]{1,0:T(8,128)(2,1)}, u32[]{:S(2)}, u32[]{:S(2)}) %collective-permute-start.20) | collective-permute-done | bytes 573472 | tf_op jit(solution)/shard_map/ppermute | solution.py:109
  198.9 12.3 %collective-permute-done.21 = bf16[224,1280]{1,0:T(8,128)(2,1)} collective-permute-done((bf16[224,1280]{1,0:T(8,128)(2,1)S(1)}, bf16[224,1280]{1,0:T(8,128)(2,1)}, u32[]{:S(2)}, u32[]{:S(2)}) %collective-permute-start.21) | collective-permute-done | bytes 573472 | tf_op jit(solution)/shard_map/ppermute | solution.py:109
  211.1 14.6 %collective-permute-start.25 = (bf16[224,1280]{1,0:T(8,128)(2,1)}, bf16[224,1280]{1,0:T(8,128)(2,1)}, u32[]{:S(2)}, u32[]{:S(2)}) collective-permute-start(bf16[224,1280]{1,0:T(8,128)(2,1)} %collective-permute-done.20), channel_id=1, source_target_pairs={{0,2},{1,3},{2,0},{3,1},{4,6},{5,7},{6,4},{7,5},{8,10},{9,11},{10,... | collective-permute-start | bytes 1720328 | tf_op jit(solution)/shard_map/ppermute | solution.py:32
  226.5 3.9 fusion.35
  234.2 5.3 collective-permute-start.28
  239.6 9.4 multiply_convert_fusion.2
  248.9 7.5 multiply_reduce_fusion.5
  258.5 17.1 %collective-permute-done.25 = bf16[224,1280]{1,0:T(8,128)(2,1)} collective-permute-done((bf16[224,1280]{1,0:T(8,128)(2,1)}, bf16[224,1280]{1,0:T(8,128)(2,1)}, u32[]{:S(2)}, u32[]{:S(2)}) %collective-permute-start.25) | collective-permute-done | bytes 573472 | tf_op jit(solution)/shard_map/ppermute | solution.py:32
  275.6 21.6 %collective-permute-done.27 = bf16[224,1280]{1,0:T(8,128)(2,1)S(1)} collective-permute-done((bf16[224,1280]{1,0:T(8,128)(2,1)}, bf16[224,1280]{1,0:T(8,128)(2,1)S(1)}, u32[]{:S(2)}, u32[]{:S(2)}) %collective-permute-start.27) | collective-permute-done | bytes 573472 | tf_op jit(solution)/shard_map/ppermute | solution.py:32
  299.0 3.6 collective-permute-start.29
  305.6 22.7 %collective-permute-done.29 = bf16[2,224,1280]{2,1,0:T(8,128)(2,1)S(1)} collective-permute-done((bf16[2,224,1280]{2,1,0:T(8,128)(2,1)S(1)}, bf16[2,224,1280]{2,1,0:T(8,128)(2,1)S(1)}, u32[]{:S(2)}, u32[]{:S(2)}) %collective-permute-start.29) | collective-permute-done | bytes 1146912 | tf_op jit(solution)/shard_map/ppermute | solution.py:32
  328.3 22.3 %collective-permute-done.30 = bf16[2,224,1280]{2,1,0:T(8,128)(2,1)S(1)} collective-permute-done((bf16[2,224,1280]{2,1,0:T(8,128)(2,1)S(1)}, bf16[2,224,1280]{2,1,0:T(8,128)(2,1)S(1)}, u32[]{:S(2)}, u32[]{:S(2)}) %collective-permute-start.30) | collective-permute-done | bytes 1146912 | tf_op jit(solution)/shard_map/ppermute | solution.py:32
  350.6 8.9 collective-permute-start.35
  364.7 34.5 %collective-permute-done.35.refs_0_.refs_3_ = bf16[512,1792]{1,0:T(8,128)(2,1)} collective-permute-done((bf16[512,1792]{1,0:T(8,128)(2,1)S(1)}, bf16[512,1792]{1,0:T(8,128)(2,1)}, u32[]{:S(2)}, u32[]{:S(2)}) %collective-permute-start.35) | collective-permute-done | bytes 1835040 | tf_op jit(solution)/shard_map/ppermute | solution.py:32
  403.6 21.6 %collective-permute-done.37 = bf16[2,224,1280]{2,1,0:T(8,128)(2,1)S(1)} collective-permute-done((bf16[2,224,1280]{2,1,0:T(8,128)(2,1)S(1)}, bf16[2,224,1280]{2,1,0:T(8,128)(2,1)S(1)}, u32[]{:S(2)}, u32[]{:S(2)}) %collective-permute-start.37) | collective-permute-done | bytes 1146912 | tf_op jit(solution)/shard_map/ppermute | solution.py:32
  428.7 39.4 %middle.2 = (bf16[2048,1280]{1,0:T(8,128)(2,1)}, bf16[2048,2560]{1,0:T(8,128)(2,1)}, bf16[512,1792]{1,0:T(8,128)(2,1)}, bf16[512,1792]{1,0:T(8,128)(2,1)}, bf16[...) custom-call(bf16[512,1792]{1,0:T(8,128)(2,1)} %copy-done, bf16[512,1792]{1,0:T(8,128)(2,1)} %copy-done.2, ...), custom_call_target="tpu_custom_call" | custom-call | flops 28185722880 | bytes 36306944 | tf_op jit(solution)/shard_map/middle/pallas_call | solution.py:174
  469.8 39.5 %middle.3 = (bf16[2048,1280]{1,0:T(8,128)(2,1)}, bf16[2048,2560]{1,0:T(8,128)(2,1)}, bf16[512,1792]{1,0:T(8,128)(2,1)}, bf16[512,1792]{1,0:T(8,128)(2,1)}, bf16[...) custom-call(bf16[512,1792]{1,0:T(8,128)(2,1)} %collective-permute-done.35.refs_0_.re, ...), custom_call_target="tpu_custom_call", output_to_operand_aliasing={{0}: (7, {}), {1}: (8, {})} | custom-call | flops 28185722880 | bytes 36306944 | tf_op jit(solution)/shard_map/middle/pallas_call | solution.py:174
  514.8 7.7 gradient_half.6
  527.7 7.6 gradient_half.10
  536.8 8.2 gradient_half.9
  546.5 7.6 gradient_half.11
  555.5 8.8 gradient_half.8
  564.3 8.8 gradient_half.7
  578.8 3.9 multiply_reduce_fusion.3
  582.7 4.9 fusion.59
  588.7 6.4 fusion.63
  595.1 3.6 multiply_reduce_fusion.1
  602.8 6.2 split_gradient.3
  610.8 6.0 split_gradient.4
  618.6 10.4 %collective-permute-done.45 = bf16[512,1792]{1,0:T(8,128)(2,1)} collective-permute-done((bf16[512,1792]{1,0:T(8,128)(2,1)}, bf16[512,1792]{1,0:T(8,128)(2,1)}, u32[]{:S(2)}, u32[]{:S(2)}) %collective-permute-start.45) | collective-permute-done | bytes 1835040 | tf_op jit(solution)/shard_map/ppermute | solution.py:32
  628.9 9.6 collective-permute-done.44
  650.0 13.3 %all-gather = bf16[32,1792]{1,0:T(8,128)(2,1)S(1)} all-gather(bf16[8,1792]{1,0:T(8,128)(2,1)S(1)} %concatenate.80), channel_id=2, replica_groups=mesh['a'=2,'b'=2,'c'=2,'z'=4] {'z'}, dimensions={0}, use_global_device_ids=true | all-gather | bytes 143360 | tf_op jit(solution)/shard_map/all_gather | solution.py:323
  663.3 10.8 %all-gather.1 = bf16[32,8,1792]{2,1,0:T(8,128)(2,1)} all-gather(bf16[4,8,1792]{2,1,0:T(8,128)(2,1)S(1)} %bitcast.218), channel_id=3, replica_groups=mesh['a'=2,'b'=2,'c'=2,'z'=4] {'a','b','c'}, dimensions={0}, use_global_device_ids=true | all-gather | bytes 1032192 | tf_op jit(solution)/shard_map/all_gather | solution.py:323
  677.7 8.9 fusion.64
  693.8 4.7 fusion.6
  701.0 3.7 add_convert_fusion.1
  705.1 5.2 fusion.10
  710.9 6.8 fusion.20
  721.9 5.4 split_gradient.5
  731.7 13.2 %collective-permute-done.48 = bf16[896,1280]{1,0:T(8,128)(2,1)} collective-permute-done((bf16[896,1280]{1,0:T(8,128)(2,1)}, bf16[896,1280]{1,0:T(8,128)(2,1)}, u32[]{:S(2)}, u32[]{:S(2)}) %collective-permute-start.48) | collective-permute-done | bytes 2293792 | tf_op jit(solution)/shard_map/ppermute | solution.py:32
  768.5 4.2 add_convert_fusion.3
  772.7 13.2 %reduce-scatter.6.cloned.1.call-done = bf16[224,1280]{1,0:T(8,128)(2,1)} async-done(((bf16[896,1280]{1,0:T(8,128)(2,1)}), bf16[224,1280]{1,0:T(8,128)(2,1)}) %reduce-scatter.6.cloned.1.call-update) | async-done | bytes 573456 | tf_op jit(solution)/shard_map/reduce_scatter | solution.py:488
  785.9 4.1 collective-permute-done.53
  790.0 5.1 collective-permute-done.51
  795.1 4.2 add_convert_fusion.18
  819.8 4.1 collective-permute-start.58
  825.9 8.7 collective-permute-done.57
  834.6 17.8 %collective-permute-done.58 = bf16[224,448]{1,0:T(8,128)(2,1)} collective-permute-done((bf16[224,448]{1,0:T(8,128)(2,1)S(1)}, bf16[224,448]{1,0:T(8,128)(2,1)}, u32[]{:S(2)}, u32[]{:S(2)}) %collective-permute-start.58) | collective-permute-done | bytes 200736 | tf_op jit(solution)/shard_map/ppermute | solution.py:32
  852.4 11.3 %collective-permute-done.59 = bf16[224,1280]{1,0:T(8,128)(2,1)} collective-permute-done((bf16[224,1280]{1,0:T(8,128)(2,1)S(1)}, bf16[224,1280]{1,0:T(8,128)(2,1)}, u32[]{:S(2)}, u32[]{:S(2)}) %collective-permute-start.59) | collective-permute-done | bytes 573472 | tf_op jit(solution)/shard_map/ppermute | solution.py:109
  863.9 4.2 add_convert_fusion.15
  868.1 4.1 collective-permute-start.62
  884.9 3.8 collective-permute-done.62
  888.7 21.9 %collective-permute-done.64 = bf16[224,1280]{1,0:T(8,128)(2,1)} collective-permute-done((bf16[224,1280]{1,0:T(8,128)(2,1)}, bf16[224,1280]{1,0:T(8,128)(2,1)}, u32[]{:S(2)}, u32[]{:S(2)}) %collective-permute-start.64) | collective-permute-done | bytes 573472 | tf_op jit(solution)/shard_map/ppermute | solution.py:109
  913.0 3.7 collective-permute-start.67
  924.3 6.1 collective-permute-done.66
  932.3 18.6 %all-gather.15.cloned.1.call-done = f32[32,5,1792]{2,1,0:T(8,128)} async-done(((f32[1,5,1792]{2,1,0:T(8,128)}), f32[32,5,1792]{2,1,0:T(8,128)}) %all-gather.15.cloned.1.call-update) | async-done | bytes 1146896 | tf_op jit(solution)/shard_map/all_gather | solution.py:537
  (400 shorter events, 209.1 us)
Async XLA Ops:
  7.2 138.3 %all-gather.9.cloned.1.call-start = ((), (), s32[]{:S(2)}) async-start(), calls=%async_computation.3 | async-start | bytes 7225344 | tf_op jit(solution)/shard_map/all_gather | solution.py:320
  13.0 22.5 %collective-permute-start = (bf16[224,448]{1,0:T(8,128)(2,1)}, bf16[224,448]{1,0:T(8,128)(2,1)S(1)}, u32[]{:S(2)}, u32[]{:S(2)}) collective-permute-start(bf16[224,448]{1,0:T(8,128)(2,1)} %param.18), channel_id=1, source_target_pairs={{0,1},{1,2},{2,3},{3,0},{4,5},{5,6},{6,7},{7,4},{8,9},{9,10},{10,1... | collective-permute-start | bytes 602120 | tf_op jit(solution)/shard_map/ppermute | solution.py:32
  14.6 20.9 %collective-permute-start.1 = (bf16[224,448]{1,0:T(8,128)(2,1)}, bf16[224,448]{1,0:T(8,128)(2,1)S(1)}, u32[]{:S(2)}, u32[]{:S(2)}) collective-permute-start(bf16[224,448]{1,0:T(8,128)(2,1)} %param.18), channel_id=1, source_target_pairs={{0,2},{1,3},{2,0},{3,1},{4,6},{5,7},{6,4},{7,5},{8,10},{9,11},{10,... | collective-permute-start | bytes 602120 | tf_op jit(solution)/shard_map/ppermute | solution.py:32
  16.3 19.2 %collective-permute-start.2 = (bf16[224,448]{1,0:T(8,128)(2,1)}, bf16[224,448]{1,0:T(8,128)(2,1)S(1)}, u32[]{:S(2)}, u32[]{:S(2)}) collective-permute-start(bf16[224,448]{1,0:T(8,128)(2,1)} %param.18), channel_id=1, source_target_pairs={{0,3},{1,0},{2,1},{3,2},{4,7},{5,4},{6,5},{7,6},{8,11},{9,8},{10,9... | collective-permute-start | bytes 602120 | tf_op jit(solution)/shard_map/ppermute | solution.py:32
  16.8 18.7 %collective-permute-start.6 = (f32[3,448]{1,0:T(4,128)}, f32[3,448]{1,0:T(4,128)S(1)}, u32[]{:S(2)}, u32[]{:S(2)}) collective-permute-start(f32[3,448]{1,0:T(4,128)} %param.20), channel_id=1, source_target_pairs={{0,2},{1,3},{2,0},{3,1},{4,6},{5,7},{6,4},{7,5},{8,10},{9,11},{10,... | collective-permute-start | bytes 16136 | tf_op jit(solution)/shard_map/ppermute | solution.py:32
  37.6 173.6 %all-gather.11.cloned.1.call-start = ((), (), s32[]{:S(2)}) async-start(), calls=%async_computation.4 | async-start | bytes 7225344 | tf_op jit(solution)/shard_map/all_gather | solution.py:320
  37.7 48.6 %collective-permute-start.11 = (bf16[224,1280]{1,0:T(8,128)(2,1)S(1)}, bf16[224,1280]{1,0:T(8,128)(2,1)S(1)}, u32[]{:S(2)}, u32[]{:S(2)}) collective-permute-start(bf16[224,1280]{1,0:T(8,128)(2,1)S(1)} %pad.10), channel_id=1, source_target_pairs={{0,0},{1,8},{2,4},{3,12},{4,1},{5,9},{6,5},{7,13},{8,2},{9,10},{10... | collective-permute-start | bytes 1720328 | tf_op jit(solution)/shard_map/ppermute | solution.py:109
  40.2 21.8 %collective-permute-start.10 = (bf16[224,448]{1,0:T(8,128)(2,1)S(1)}, bf16[224,448]{1,0:T(8,128)(2,1)S(1)}, u32[]{:S(2)}, u32[]{:S(2)}) collective-permute-start(bf16[224,448]{1,0:T(8,128)(2,1)S(1)} %copy-done.59), channel_id=1, source_target_pairs={{0,3},{1,0},{2,1},{3,2},{4,7},{5,4},{6,5},{7,6},{8,11},{9,8},{10,9... | collective-permute-start | bytes 602120 | tf_op jit(solution)/shard_map/ppermute | solution.py:32
  41.8 20.2 %collective-permute-start.8 = (bf16[224,448]{1,0:T(8,128)(2,1)S(1)}, bf16[224,448]{1,0:T(8,128)(2,1)S(1)}, u32[]{:S(2)}, u32[]{:S(2)}) collective-permute-start(bf16[224,448]{1,0:T(8,128)(2,1)S(1)} %copy-done.59), channel_id=1, source_target_pairs={{0,1},{1,2},{2,3},{3,0},{4,5},{5,6},{6,7},{7,4},{8,9},{9,10},{10,1... | collective-permute-start | bytes 602120 | tf_op jit(solution)/shard_map/ppermute | solution.py:32
  44.0 41.6 %collective-permute-start.9 = (bf16[224,448]{1,0:T(8,128)(2,1)S(1)}, bf16[224,448]{1,0:T(8,128)(2,1)S(1)}, u32[]{:S(2)}, u32[]{:S(2)}) collective-permute-start(bf16[224,448]{1,0:T(8,128)(2,1)S(1)} %copy-done.59), channel_id=1, source_target_pairs={{0,2},{1,3},{2,0},{3,1},{4,6},{5,7},{6,4},{7,5},{8,10},{9,11},{10,... | collective-permute-start | bytes 602120 | tf_op jit(solution)/shard_map/ppermute | solution.py:32
  88.4 160.6 %all-gather.13.cloned.1.call-start = ((), (), s32[]{:S(2)}) async-start(), calls=%async_computation.5 | async-start | bytes 7225344 | tf_op jit(solution)/shard_map/all_gather | solution.py:320
  88.4 55.5 %collective-permute-start.16 = (bf16[224,1280]{1,0:T(8,128)(2,1)S(1)}, bf16[224,1280]{1,0:T(8,128)(2,1)S(1)}, u32[]{:S(2)}, u32[]{:S(2)}) collective-permute-start(bf16[224,1280]{1,0:T(8,128)(2,1)S(1)} %collective-permute-done.11), channel_id=1, source_target_pairs={{0,1},{1,2},{2,3},{3,0},{4,5},{5,6},{6,7},{7,4},{8,9},{9,10},{10,1... | collective-permute-start | bytes 1720328 | tf_op jit(solution)/shard_map/ppermute | solution.py:32
  88.5 57.0 %collective-permute-start.17 = (bf16[224,1280]{1,0:T(8,128)(2,1)S(1)}, bf16[224,1280]{1,0:T(8,128)(2,1)}, u32[]{:S(2)}, u32[]{:S(2)}) collective-permute-start(bf16[224,1280]{1,0:T(8,128)(2,1)S(1)} %collective-permute-done.11), channel_id=1, source_target_pairs={{0,3},{1,0},{2,1},{3,2},{4,7},{5,4},{6,5},{7,6},{8,11},{9,8},{10,9... | collective-permute-start | bytes 1720328 | tf_op jit(solution)/shard_map/ppermute | solution.py:32
  90.5 33.2 %collective-permute-start.18 = (bf16[8,8,1792]{2,1,0:T(8,128)(2,1)S(1)}, bf16[8,8,1792]{2,1,0:T(8,128)(2,1)S(1)}, u32[]{:S(2)}, u32[]{:S(2)}) collective-permute-start(bf16[8,8,1792]{2,1,0:T(8,128)(2,1)S(1)} %pad_maximum_fusion.9), channel_id=1, source_target_pairs={{0,2},{1,3},{2,0},{3,1},{4,6},{5,7},{6,4},{7,5},{8,10},{9,11},{10,... | collective-permute-start | bytes 688136 | tf_op jit(solution)/shard_map/ppermute | solution.py:114
  90.5 44.8 %collective-permute-start.13 = (bf16[224,448]{1,0:T(8,128)(2,1)S(1)}, bf16[224,448]{1,0:T(8,128)(2,1)S(1)}, u32[]{:S(2)}, u32[]{:S(2)}) collective-permute-start(bf16[224,448]{1,0:T(8,128)(2,1)S(1)} %copy-done.60), channel_id=1, source_target_pairs={{0,1},{1,2},{2,3},{3,0},{4,5},{5,6},{6,7},{7,4},{8,9},{9,10},{10,1... | collective-permute-start | bytes 602120 | tf_op jit(solution)/shard_map/ppermute | solution.py:32
  92.9 45.5 %collective-permute-start.14 = (bf16[224,448]{1,0:T(8,128)(2,1)S(1)}, bf16[224,448]{1,0:T(8,128)(2,1)S(1)}, u32[]{:S(2)}, u32[]{:S(2)}) collective-permute-start(bf16[224,448]{1,0:T(8,128)(2,1)S(1)} %copy-done.60), channel_id=1, source_target_pairs={{0,2},{1,3},{2,0},{3,1},{4,6},{5,7},{6,4},{7,5},{8,10},{9,11},{10,... | collective-permute-start | bytes 602120 | tf_op jit(solution)/shard_map/ppermute | solution.py:32
  123.7 20.3 %collective-permute-start.15 = (bf16[224,448]{1,0:T(8,128)(2,1)S(1)}, bf16[224,448]{1,0:T(8,128)(2,1)S(1)}, u32[]{:S(2)}, u32[]{:S(2)}) collective-permute-start(bf16[224,448]{1,0:T(8,128)(2,1)S(1)} %copy-done.60), channel_id=1, source_target_pairs={{0,3},{1,0},{2,1},{3,2},{4,7},{5,4},{6,5},{7,6},{8,11},{9,8},{10,9... | collective-permute-start | bytes 602120 | tf_op jit(solution)/shard_map/ppermute | solution.py:32
  147.6 597.4 %reduce-scatter.4.cloned.1.call-start = ((), (), s32[]{:S(2)}) async-start(), calls=%async_computation.6 | async-start | bytes 2867200 | tf_op jit(solution)/shard_map/reduce_scatter | solution.py:488
  154.6 20.4 %collective-permute-start.22 = (bf16[16,8,1792]{2,1,0:T(8,128)(2,1)S(1)}, bf16[16,8,1792]{2,1,0:T(8,128)(2,1)S(1)}, u32[]{:S(2)}, u32[]{:S(2)}) collective-permute-start(bf16[16,8,1792]{2,1,0:T(8,128)(2,1)S(1)} %pad_maximum_fusion.8), channel_id=1, source_target_pairs={{0,4},{1,5},{2,6},{3,7},{4,0},{5,1},{6,2},{7,3},{8,12},{9,13},{10,... | collective-permute-start | bytes 1376264 | tf_op jit(solution)/shard_map/ppermute | solution.py:114
  155.8 43.0 %collective-permute-start.20 = (bf16[224,1280]{1,0:T(8,128)(2,1)S(1)}, bf16[224,1280]{1,0:T(8,128)(2,1)}, u32[]{:S(2)}, u32[]{:S(2)}) collective-permute-start(bf16[224,1280]{1,0:T(8,128)(2,1)S(1)} %pad.11), channel_id=1, source_target_pairs={{0,0},{1,8},{2,4},{3,12},{4,1},{5,9},{6,5},{7,13},{8,2},{9,10},{10... | collective-permute-start | bytes 1720328 | tf_op jit(solution)/shard_map/ppermute | solution.py:109
  160.2 51.0 %collective-permute-start.21 = (bf16[224,1280]{1,0:T(8,128)(2,1)S(1)}, bf16[224,1280]{1,0:T(8,128)(2,1)}, u32[]{:S(2)}, u32[]{:S(2)}) collective-permute-start(bf16[224,1280]{1,0:T(8,128)(2,1)S(1)} %pad.12), channel_id=1, source_target_pairs={{0,0},{1,8},{2,4},{3,12},{4,1},{5,9},{6,5},{7,13},{8,2},{9,10},{10... | collective-permute-start | bytes 1720328 | tf_op jit(solution)/shard_map/ppermute | solution.py:109
  163.5 47.7 %collective-permute-start.19 = (bf16[224,1280]{1,0:T(8,128)(2,1)}, bf16[224,1280]{1,0:T(8,128)(2,1)}, u32[]{:S(2)}, u32[]{:S(2)}) collective-permute-start(bf16[224,1280]{1,0:T(8,128)(2,1)} %copy-done.56), channel_id=1, source_target_pairs={{0,1},{1,2},{2,3},{3,0},{4,5},{5,6},{6,7},{7,4},{8,9},{9,10},{10,1... | collective-permute-start | bytes 1720328 | tf_op jit(solution)/shard_map/ppermute | solution.py:32
  211.1 45.3 %collective-permute-start.24 = (bf16[224,1280]{1,0:T(8,128)(2,1)}, bf16[224,1280]{1,0:T(8,128)(2,1)S(1)}, u32[]{:S(2)}, u32[]{:S(2)}) collective-permute-start(bf16[224,1280]{1,0:T(8,128)(2,1)} %collective-permute-done.20), channel_id=1, source_target_pairs={{0,1},{1,2},{2,3},{3,0},{4,5},{5,6},{6,7},{7,4},{8,9},{9,10},{10,1... | collective-permute-start | bytes 1720328 | tf_op jit(solution)/shard_map/ppermute | solution.py:32
  211.1 64.5 %collective-permute-start.25 = (bf16[224,1280]{1,0:T(8,128)(2,1)}, bf16[224,1280]{1,0:T(8,128)(2,1)}, u32[]{:S(2)}, u32[]{:S(2)}) collective-permute-start(bf16[224,1280]{1,0:T(8,128)(2,1)} %collective-permute-done.20), channel_id=1, source_target_pairs={{0,2},{1,3},{2,0},{3,1},{4,6},{5,7},{6,4},{7,5},{8,10},{9,11},{10,... | collective-permute-start | bytes 1720328 | tf_op jit(solution)/shard_map/ppermute | solution.py:32
  225.8 49.8 %collective-permute-start.26 = (bf16[224,1280]{1,0:T(8,128)(2,1)}, bf16[224,1280]{1,0:T(8,128)(2,1)}, u32[]{:S(2)}, u32[]{:S(2)}) collective-permute-start(bf16[224,1280]{1,0:T(8,128)(2,1)} %collective-permute-done.20), channel_id=1, source_target_pairs={{0,3},{1,0},{2,1},{3,2},{4,7},{5,4},{6,5},{7,6},{8,11},{9,8},{10,9... | collective-permute-start | bytes 1720328 | tf_op jit(solution)/shard_map/ppermute | solution.py:32
  233.7 63.5 %collective-permute-start.23 = (bf16[4,224,1280]{2,1,0:T(8,128)(2,1)}, bf16[4,224,1280]{2,1,0:T(8,128)(2,1)}, u32[]{:S(2)}, u32[]{:S(2)}) collective-permute-start(bf16[4,224,1280]{2,1,0:T(8,128)(2,1)} %pad_maximum_fusion.4), channel_id=1, source_target_pairs={{0,16},{16,0},{1,17},{17,1},{2,18},{18,2},{3,19},{19,3},{4,20},{20... | collective-permute-start | bytes 6881288 | tf_op jit(solution)/shard_map/ppermute | solution.py:32
  234.2 63.0 %collective-permute-start.28 = (bf16[512,1792]{1,0:T(8,128)(2,1)}, bf16[512,1792]{1,0:T(8,128)(2,1)S(1)}, u32[]{:S(2)}, u32[]{:S(2)}) collective-permute-start(bf16[512,1792]{1,0:T(8,128)(2,1)} %bitcast.18.refs_2_.refs_1_), channel_id=1, source_target_pairs={{0,8},{8,0},{1,9},{9,1},{2,10},{10,2},{3,11},{11,3},{4,12},{12,4},... | collective-permute-start | bytes 5505032 | tf_op jit(solution)/shard_map/ppermute | solution.py:32
  256.5 40.7 %collective-permute-start.27 = (bf16[224,1280]{1,0:T(8,128)(2,1)}, bf16[224,1280]{1,0:T(8,128)(2,1)S(1)}, u32[]{:S(2)}, u32[]{:S(2)}) collective-permute-start(bf16[224,1280]{1,0:T(8,128)(2,1)} %collective-permute-done.21), channel_id=1, source_target_pairs={{0,16},{16,0},{1,17},{17,1},{2,18},{18,2},{3,19},{19,3},{4,20},{20... | collective-permute-start | bytes 1720328 | tf_op jit(solution)/shard_map/ppermute | solution.py:32
  299.0 29.3 %collective-permute-start.29 = (bf16[2,224,1280]{2,1,0:T(8,128)(2,1)S(1)}, bf16[2,224,1280]{2,1,0:T(8,128)(2,1)S(1)}, u32[]{:S(2)}, u32[]{:S(2)}) collective-permute-start(bf16[2,224,1280]{2,1,0:T(8,128)(2,1)S(1)} %pad_maximum_fusion.6), channel_id=1, source_target_pairs={{0,1},{1,2},{2,3},{3,0},{4,5},{5,6},{6,7},{7,4},{8,9},{9,10},{10,1... | collective-permute-start | bytes 3440648 | tf_op jit(solution)/shard_map/ppermute | solution.py:32
  302.6 48.0 %collective-permute-start.30 = (bf16[2,224,1280]{2,1,0:T(8,128)(2,1)S(1)}, bf16[2,224,1280]{2,1,0:T(8,128)(2,1)S(1)}, u32[]{:S(2)}, u32[]{:S(2)}) collective-permute-start(bf16[2,224,1280]{2,1,0:T(8,128)(2,1)S(1)} %pad_maximum_fusion.6), channel_id=1, source_target_pairs={{0,3},{1,0},{2,1},{3,2},{4,7},{5,4},{6,5},{7,6},{8,11},{9,8},{10,9... | collective-permute-start | bytes 3440648 | tf_op jit(solution)/shard_map/ppermute | solution.py:32
  304.5 94.6 %collective-permute-start.31 = (bf16[4,224,1280]{2,1,0:T(8,128)(2,1)S(1)}, bf16[4,224,1280]{2,1,0:T(8,128)(2,1)S(1)}, u32[]{:S(2)}, u32[]{:S(2)}) collective-permute-start(bf16[4,224,1280]{2,1,0:T(8,128)(2,1)S(1)} %pad_maximum_fusion.5), channel_id=1, source_target_pairs={{0,16},{16,0},{1,17},{17,1},{2,18},{18,2},{3,19},{19,3},{4,20},{20... | collective-permute-start | bytes 6881288 | tf_op jit(solution)/shard_map/ppermute | solution.py:32
  305.1 59.5 %collective-permute-start.32 = (bf16[512,1792]{1,0:T(8,128)(2,1)}, bf16[512,1792]{1,0:T(8,128)(2,1)S(1)}, u32[]{:S(2)}, u32[]{:S(2)}) collective-permute-start(bf16[512,1792]{1,0:T(8,128)(2,1)} %bitcast.18.refs_2_.refs_1_), channel_id=1, source_target_pairs={{0,4},{4,0},{1,5},{5,1},{2,6},{6,2},{3,7},{7,3},{8,12},{12,8},{9,1... | collective-permute-start | bytes 5505032 | tf_op jit(solution)/shard_map/ppermute | solution.py:32
  305.1 59.5 %collective-permute-start.33 = (bf16[512,1792]{1,0:T(8,128)(2,1)S(1)}, bf16[512,1792]{1,0:T(8,128)(2,1)S(1)}, u32[]{:S(2)}, u32[]{:S(2)}) collective-permute-start(bf16[512,1792]{1,0:T(8,128)(2,1)S(1)} %collective-permute-done.28.refs_2_.refs_3_), channel_id=1, source_target_pairs={{0,4},{4,0},{1,5},{5,1},{2,6},{6,2},{3,7},{7,3},{8,12},{12,8},{9,1... | collective-permute-start | bytes 5505032 | tf_op jit(solution)/shard_map/ppermute | solution.py:32
  328.3 36.4 %collective-permute-start.34 = (bf16[512,1792]{1,0:T(8,128)(2,1)S(1)}, bf16[512,1792]{1,0:T(8,128)(2,1)S(1)}, u32[]{:S(2)}, u32[]{:S(2)}) collective-permute-start(bf16[512,1792]{1,0:T(8,128)(2,1)S(1)} %multiply_convert_fusion.1.refs_0_.refs_1_), channel_id=1, source_target_pairs={{0,4},{4,0},{1,5},{5,1},{2,6},{6,2},{3,7},{7,3},{8,12},{12,8},{9,1... | collective-permute-start | bytes 5505032 | tf_op jit(solution)/shard_map/ppermute | solution.py:32
  350.6 48.5 %collective-permute-start.35 = (bf16[512,1792]{1,0:T(8,128)(2,1)S(1)}, bf16[512,1792]{1,0:T(8,128)(2,1)}, u32[]{:S(2)}, u32[]{:S(2)}) collective-permute-start(bf16[512,1792]{1,0:T(8,128)(2,1)S(1)} %multiply_convert_fusion.1.refs_0_.refs_1_), channel_id=1, source_target_pairs={{0,8},{8,0},{1,9},{9,1},{2,10},{10,2},{3,11},{11,3},{4,12},{12,4},... | collective-permute-start | bytes 5505032 | tf_op jit(solution)/shard_map/ppermute | solution.py:32
  399.1 26.0 %collective-permute-start.37 = (bf16[2,224,1280]{2,1,0:T(8,128)(2,1)S(1)}, bf16[2,224,1280]{2,1,0:T(8,128)(2,1)S(1)}, u32[]{:S(2)}, u32[]{:S(2)}) collective-permute-start(bf16[2,224,1280]{2,1,0:T(8,128)(2,1)S(1)} %collective-permute-done.29), channel_id=1, source_target_pairs={{0,1},{1,2},{2,3},{3,0},{4,5},{5,6},{6,7},{7,4},{8,9},{9,10},{10,1... | collective-permute-start | bytes 3440648 | tf_op jit(solution)/shard_map/ppermute | solution.py:32
  400.8 67.8 %collective-permute-start.36 = (bf16[512,1792]{1,0:T(8,128)(2,1)}, bf16[512,1792]{1,0:T(8,128)(2,1)S(1)}, u32[]{:S(2)}, u32[]{:S(2)}) collective-permute-start(bf16[512,1792]{1,0:T(8,128)(2,1)} %collective-permute-done.35.refs_0_.refs_3_), channel_id=1, source_target_pairs={{0,4},{4,0},{1,5},{5,1},{2,6},{6,2},{3,7},{7,3},{8,12},{12,8},{9,1... | collective-permute-start | bytes 5505032 | tf_op jit(solution)/shard_map/ppermute | solution.py:32
  468.0 54.5 %collective-permute-start.38 = (bf16[512,1792]{1,0:T(8,128)(2,1)}, bf16[512,1792]{1,0:T(8,128)(2,1)}, u32[]{:S(2)}, u32[]{:S(2)}) collective-permute-start(bf16[512,1792]{1,0:T(8,128)(2,1)} %get-tuple-element.258), channel_id=1, source_target_pairs={{0,4},{4,0},{1,5},{5,1},{2,6},{6,2},{3,7},{7,3},{8,12},{12,8},{9,1... | collective-permute-start | bytes 5505032 | tf_op jit(solution)/shard_map/ppermute | solution.py:32
  468.1 54.4 %collective-permute-start.40 = (bf16[512,1792]{1,0:T(8,128)(2,1)}, bf16[512,1792]{1,0:T(8,128)(2,1)}, u32[]{:S(2)}, u32[]{:S(2)}) collective-permute-start(bf16[512,1792]{1,0:T(8,128)(2,1)} %get-tuple-element.262), channel_id=1, source_target_pairs={{0,4},{4,0},{1,5},{5,1},{2,6},{6,2},{3,7},{7,3},{8,12},{12,8},{9,1... | collective-permute-start | bytes 5505032 | tf_op jit(solution)/shard_map/ppermute | solution.py:32
  525.8 50.8 %collective-permute-start.43 = (bf16[512,1792]{1,0:T(8,128)(2,1)}, bf16[512,1792]{1,0:T(8,128)(2,1)S(1)}, u32[]{:S(2)}, u32[]{:S(2)}) collective-permute-start(bf16[512,1792]{1,0:T(8,128)(2,1)} %add_convert_fusion.5), channel_id=1, source_target_pairs={{0,8},{8,0},{1,9},{9,1},{2,10},{10,2},{3,11},{11,3},{4,12},{12,4},... | collective-permute-start | bytes 5505032 | tf_op jit(solution)/shard_map/ppermute | solution.py:32
  527.2 51.5 %collective-permute-start.42 = (bf16[896,1280]{1,0:T(8,128)(2,1)S(1)}, bf16[896,1280]{1,0:T(8,128)(2,1)S(1)}, u32[]{:S(2)}, u32[]{:S(2)}) collective-permute-start(bf16[896,1280]{1,0:T(8,128)(2,1)S(1)} %gradient_half.6), channel_id=1, source_target_pairs={{0,16},{16,0},{1,17},{17,1},{2,18},{18,2},{3,19},{19,3},{4,20},{20... | collective-permute-start | bytes 6881288 | tf_op jit(solution)/shard_map/ppermute | solution.py:32
  587.6 51.0 %collective-permute-start.44 = (bf16[896,1280]{1,0:T(8,128)(2,1)}, bf16[896,1280]{1,0:T(8,128)(2,1)}, u32[]{:S(2)}, u32[]{:S(2)}) collective-permute-start(bf16[896,1280]{1,0:T(8,128)(2,1)} %gradient_half.7), channel_id=1, source_target_pairs={{0,16},{16,0},{1,17},{17,1},{2,18},{18,2},{3,19},{19,3},{4,20},{20... | collective-permute-start | bytes 6881288 | tf_op jit(solution)/shard_map/ppermute | solution.py:32
  588.1 40.9 %collective-permute-start.45 = (bf16[512,1792]{1,0:T(8,128)(2,1)}, bf16[512,1792]{1,0:T(8,128)(2,1)}, u32[]{:S(2)}, u32[]{:S(2)}) collective-permute-start(bf16[512,1792]{1,0:T(8,128)(2,1)} %add_convert_fusion.4), channel_id=1, source_target_pairs={{0,8},{8,0},{1,9},{9,1},{2,10},{10,2},{3,11},{11,3},{4,12},{12,4},... | collective-permute-start | bytes 5505032 | tf_op jit(solution)/shard_map/ppermute | solution.py:32
  638.6 35.5 %collective-permute-start.46 = (bf16[4,224,1792]{2,1,0:T(8,128)(2,1)}, bf16[4,224,1792]{2,1,0:T(8,128)(2,1)}, u32[]{:S(2)}, u32[]{:S(2)}) collective-permute-start(bf16[4,224,1792]{2,1,0:T(8,128)(2,1)} %get-tuple-element.293), channel_id=1, source_target_pairs={{0,4},{4,0},{1,5},{5,1},{2,6},{6,2},{3,7},{7,3},{8,12},{12,8},{9,1... | collective-permute-start | bytes 9633800 | tf_op jit(solution)/shard_map/ppermute | solution.py:32
  638.6 35.5 %collective-permute-start.47 = (bf16[4,224,1792]{2,1,0:T(8,128)(2,1)}, bf16[4,224,1792]{2,1,0:T(8,128)(2,1)}, u32[]{:S(2)}, u32[]{:S(2)}) collective-permute-start(bf16[4,224,1792]{2,1,0:T(8,128)(2,1)} %get-tuple-element.295), channel_id=1, source_target_pairs={{0,4},{4,0},{1,5},{5,1},{2,6},{6,2},{3,7},{7,3},{8,12},{12,8},{9,1... | collective-permute-start | bytes 9633800 | tf_op jit(solution)/shard_map/ppermute | solution.py:32
  677.7 108.2 %reduce-scatter.6.cloned.1.call-start = ((), (), s32[]{:S(2)}) async-start(), calls=%async_computation.7 | async-start | bytes 2867200 | tf_op jit(solution)/shard_map/reduce_scatter | solution.py:488
  691.4 40.3 %collective-permute-start.49 = (bf16[2,224,1792]{2,1,0:T(8,128)(2,1)}, bf16[2,224,1792]{2,1,0:T(8,128)(2,1)}, u32[]{:S(2)}, u32[]{:S(2)}) collective-permute-start(bf16[2,224,1792]{2,1,0:T(8,128)(2,1)} %fusion.24), channel_id=1, source_target_pairs={{0,8},{8,0},{1,9},{9,1},{2,10},{10,2},{3,11},{11,3},{4,12},{12,4},... | collective-permute-start | bytes 4816904 | tf_op jit(solution)/shard_map/ppermute | solution.py:32
  692.9 52.1 %collective-permute-start.48 = (bf16[896,1280]{1,0:T(8,128)(2,1)}, bf16[896,1280]{1,0:T(8,128)(2,1)}, u32[]{:S(2)}, u32[]{:S(2)}) collective-permute-start(bf16[896,1280]{1,0:T(8,128)(2,1)} %gradient_half.8), channel_id=1, source_target_pairs={{0,16},{16,0},{1,17},{17,1},{2,18},{18,2},{3,19},{19,3},{4,20},{20... | collective-permute-start | bytes 6881288 | tf_op jit(solution)/shard_map/ppermute | solution.py:32
  704.8 159.1 %reduce-scatter.8.cloned.1.call-start = ((), (), s32[]{:S(2)}) async-start(), calls=%async_computation.8 | async-start | bytes 2867200 | tf_op jit(solution)/shard_map/reduce_scatter | solution.py:488
  748.1 47.0 %collective-permute-start.51 = (bf16[2,224,1792]{2,1,0:T(8,128)(2,1)}, bf16[2,224,1792]{2,1,0:T(8,128)(2,1)}, u32[]{:S(2)}, u32[]{:S(2)}) collective-permute-start(bf16[2,224,1792]{2,1,0:T(8,128)(2,1)} %fusion.25), channel_id=1, source_target_pairs={{0,8},{8,0},{1,9},{9,1},{2,10},{10,2},{3,11},{11,3},{4,12},{12,4},... | collective-permute-start | bytes 4816904 | tf_op jit(solution)/shard_map/ppermute | solution.py:32
  748.7 46.4 %collective-permute-start.50 = (bf16[4,224,1792]{2,1,0:T(8,128)(2,1)}, bf16[4,224,1792]{2,1,0:T(8,128)(2,1)}, u32[]{:S(2)}, u32[]{:S(2)}) collective-permute-start(bf16[4,224,1792]{2,1,0:T(8,128)(2,1)} %copy-done.22), channel_id=1, source_target_pairs={{0,4},{4,0},{1,5},{5,1},{2,6},{6,2},{3,7},{7,3},{8,12},{12,8},{9,1... | collective-permute-start | bytes 9633800 | tf_op jit(solution)/shard_map/ppermute | solution.py:32
  752.3 198.6 %all-gather.15.cloned.1.call-start = ((), (), s32[]{:S(2)}) async-start(), calls=%async_computation.9 | async-start | bytes 1892352 | tf_op jit(solution)/shard_map/all_gather | solution.py:537
  760.0 30.0 %collective-permute-start.52 = (bf16[224,1792]{1,0:T(8,128)(2,1)}, bf16[224,1792]{1,0:T(8,128)(2,1)}, u32[]{:S(2)}, u32[]{:S(2)}) collective-permute-start(bf16[224,1792]{1,0:T(8,128)(2,1)} %fusion.29), channel_id=1, source_target_pairs={{0,16},{16,0},{1,17},{17,1},{2,18},{18,2},{3,19},{19,3},{4,20},{20... | collective-permute-start | bytes 2408456 | tf_op jit(solution)/shard_map/ppermute | solution.py:32
  761.4 28.6 %collective-permute-start.53 = (bf16[224,1280]{1,0:T(8,128)(2,1)}, bf16[224,1280]{1,0:T(8,128)(2,1)}, u32[]{:S(2)}, u32[]{:S(2)}) collective-permute-start(bf16[224,1280]{1,0:T(8,128)(2,1)} %reduce-scatter.4.cloned.1.call-done), channel_id=1, source_target_pairs={{0,0},{8,1},{4,2},{12,3},{1,4},{9,5},{5,6},{13,7},{2,8},{10,9},{6,... | collective-permute-start | bytes 1720328 | tf_op jit(solution)/shard_map/ppermute | solution.py:109
  799.3 20.4 %collective-permute-start.56 = (bf16[224,448]{1,0:T(8,128)(2,1)S(1)}, bf16[224,448]{1,0:T(8,128)(2,1)S(1)}, u32[]{:S(2)}, u32[]{:S(2)}) collective-permute-start(bf16[224,448]{1,0:T(8,128)(2,1)S(1)} %get-tuple-element.407), channel_id=1, source_target_pairs={{0,3},{1,0},{2,1},{3,2},{4,7},{5,4},{6,5},{7,6},{8,11},{9,8},{10,9... | collective-permute-start | bytes 602120 | tf_op jit(solution)/shard_map/ppermute | solution.py:32
  802.4 32.2 %collective-permute-start.57 = (bf16[224,448]{1,0:T(8,128)(2,1)S(1)}, bf16[224,448]{1,0:T(8,128)(2,1)}, u32[]{:S(2)}, u32[]{:S(2)}) collective-permute-start(bf16[224,448]{1,0:T(8,128)(2,1)S(1)} %get-tuple-element.406), channel_id=1, source_target_pairs={{0,2},{1,3},{2,0},{3,1},{4,6},{5,7},{6,4},{7,5},{8,10},{9,11},{10,... | collective-permute-start | bytes 602120 | tf_op jit(solution)/shard_map/ppermute | solution.py:32
  807.6 56.3 %collective-permute-start.54 = (bf16[2,224,1792]{2,1,0:T(8,128)(2,1)}, bf16[2,224,1792]{2,1,0:T(8,128)(2,1)}, u32[]{:S(2)}, u32[]{:S(2)}) collective-permute-start(bf16[2,224,1792]{2,1,0:T(8,128)(2,1)} %fusion.26), channel_id=1, source_target_pairs={{0,8},{8,0},{1,9},{9,1},{2,10},{10,2},{3,11},{11,3},{4,12},{12,4},... | collective-permute-start | bytes 4816904 | tf_op jit(solution)/shard_map/ppermute | solution.py:32
  811.8 51.9 %collective-permute-start.55 = (bf16[224,1792]{1,0:T(8,128)(2,1)S(1)}, bf16[224,1792]{1,0:T(8,128)(2,1)}, u32[]{:S(2)}, u32[]{:S(2)}) collective-permute-start(bf16[224,1792]{1,0:T(8,128)(2,1)S(1)} %fusion.30), channel_id=1, source_target_pairs={{0,16},{16,0},{1,17},{17,1},{2,18},{18,2},{3,19},{19,3},{4,20},{20... | collective-permute-start | bytes 2408456 | tf_op jit(solution)/shard_map/ppermute | solution.py:32
  812.5 51.2 %collective-permute-start.59 = (bf16[224,1280]{1,0:T(8,128)(2,1)S(1)}, bf16[224,1280]{1,0:T(8,128)(2,1)}, u32[]{:S(2)}, u32[]{:S(2)}) collective-permute-start(bf16[224,1280]{1,0:T(8,128)(2,1)S(1)} %copy-done.73), channel_id=1, source_target_pairs={{0,0},{8,1},{4,2},{12,3},{1,4},{9,5},{5,6},{13,7},{2,8},{10,9},{6,... | collective-permute-start | bytes 1720328 | tf_op jit(solution)/shard_map/ppermute | solution.py:109
  819.8 32.6 %collective-permute-start.58 = (bf16[224,448]{1,0:T(8,128)(2,1)S(1)}, bf16[224,448]{1,0:T(8,128)(2,1)}, u32[]{:S(2)}, u32[]{:S(2)}) collective-permute-start(bf16[224,448]{1,0:T(8,128)(2,1)S(1)} %get-tuple-element.405), channel_id=1, source_target_pairs={{0,1},{1,2},{2,3},{3,0},{4,5},{5,6},{6,7},{7,4},{8,9},{9,10},{10,1... | collective-permute-start | bytes 602120 | tf_op jit(solution)/shard_map/ppermute | solution.py:32
  868.1 20.5 %collective-permute-start.62 = (bf16[224,448]{1,0:T(8,128)(2,1)}, bf16[224,448]{1,0:T(8,128)(2,1)}, u32[]{:S(2)}, u32[]{:S(2)}) collective-permute-start(bf16[224,448]{1,0:T(8,128)(2,1)} %get-tuple-element.402), channel_id=1, source_target_pairs={{0,2},{1,3},{2,0},{3,1},{4,6},{5,7},{6,4},{7,5},{8,10},{9,11},{10,... | collective-permute-start | bytes 602120 | tf_op jit(solution)/shard_map/ppermute | solution.py:32
  875.2 35.4 %collective-permute-start.60 = (bf16[224,1792]{1,0:T(8,128)(2,1)}, bf16[224,1792]{1,0:T(8,128)(2,1)}, u32[]{:S(2)}, u32[]{:S(2)}) collective-permute-start(bf16[224,1792]{1,0:T(8,128)(2,1)} %fusion.31), channel_id=1, source_target_pairs={{0,16},{16,0},{1,17},{17,1},{2,18},{18,2},{3,19},{19,3},{4,20},{20... | collective-permute-start | bytes 2408456 | tf_op jit(solution)/shard_map/ppermute | solution.py:32
  875.8 34.8 %collective-permute-start.64 = (bf16[224,1280]{1,0:T(8,128)(2,1)}, bf16[224,1280]{1,0:T(8,128)(2,1)}, u32[]{:S(2)}, u32[]{:S(2)}) collective-permute-start(bf16[224,1280]{1,0:T(8,128)(2,1)} %reduce-scatter.8.cloned.1.call-done), channel_id=1, source_target_pairs={{0,0},{8,1},{4,2},{12,3},{1,4},{9,5},{5,6},{13,7},{2,8},{10,9},{6,... | collective-permute-start | bytes 1720328 | tf_op jit(solution)/shard_map/ppermute | solution.py:109
  912.9 17.5 %collective-permute-start.66 = (bf16[224,448]{1,0:T(8,128)(2,1)S(1)}, bf16[224,448]{1,0:T(8,128)(2,1)S(1)}, u32[]{:S(2)}, u32[]{:S(2)}) collective-permute-start(bf16[224,448]{1,0:T(8,128)(2,1)S(1)} %get-tuple-element.400), channel_id=1, source_target_pairs={{0,2},{1,3},{2,0},{3,1},{4,6},{5,7},{6,4},{7,5},{8,10},{9,11},{10,... | collective-permute-start | bytes 602120 | tf_op jit(solution)/shard_map/ppermute | solution.py:32
  (86 other events, 1299.7 us)
Sparse Core Ops, SparseCore 0:
  37.7 53.6 all-gather.8
  93.9 46.0 all-gather.10
  147.7 67.9 all-gather.12
  677.8 46.3 reduce-scatter.3
  726.5 59.3 reduce-scatter.5
  788.0 75.7 reduce-scatter.7
  879.5 71.3 all-gather.14

commit v3 on v2

--- a/solution.py
+++ b/solution.py
@@ -99,14 +99,14 @@
     return [columns(0)] + [shift_by(columns(s).astype(BF16), "z", -s) for s in range(1, count)]
 
 
-def swapped(block, back=False):
+def home(block):
     count, size = lax.axis_size("z"), lax.axis_size("b")
     moves = []
     for t in range(count):
         for z in range(count):
             team = (z % size) * 2 + z // size
-            moves.append((t * count + z, team * count + t))
-    return lax.ppermute(block, ("b", "c", "z"), [(j, i) if back else (i, j) for i, j in moves])
+            moves.append((team * count + t, t * count + z))
+    return lax.ppermute(block, ("b", "c", "z"), moves)
 
 
 def partner(value, bit):
@@ -117,7 +117,7 @@
 def exchange_order():
     bits = [1 << i for i in range(lax.axis_size(EVERY).bit_length() - 1)]
     core = lax.axis_size("z")
-    return [b for b in bits[::-1] if b > core] + [b for b in bits if b < core] + [core]
+    return [b for b in bits if b < core] + [b for b in bits[::-1] if b > core] + [core]
 
 
 def entry_of(difference):
@@ -130,26 +130,33 @@
     return value
 
 
-def middle_kernel(steps, *refs):
-    near_hidden, far_hidden, near_cot, far_cot, w_gate, w_up, w_down = refs[:7]
-    activated, grads, near_back, far_back, near_out, far_out = refs[-6:]
+def first_kernel(steps, *refs):
+    near_hidden, far_hidden, w_gate, w_up = refs[:4]
+    gates, ups, activated = refs[-3:]
+    near = pl.program_id(0) < steps
+    hidden = jnp.where(near, near_hidden[...], far_hidden[...])
+    gate = dot_nn(hidden, w_gate[...])
+    up = dot_nn(hidden, w_up[...])
+    gates[...] = gate.astype(BF16)
+    ups[...] = up.astype(BF16)
+    activated[...] = (gate * (1.0 / (1.0 + jnp.exp(-gate))) * up).astype(BF16)
+
+
+def second_kernel(steps, *refs):
+    near_cot, far_cot, gates, ups, activated, w_gate, w_up, w_down = refs[:8]
+    grads, near_back, far_back, near_out, far_out = refs[-5:]
     units = w_down.shape[1]
     near = pl.program_id(0) < steps
-    hidden = jnp.where(near, near_hidden[...], far_hidden[...])
     cot = jnp.where(near, near_cot[...], far_cot[...])
-    gate = dot_nn(hidden, w_gate[...])
-    up = dot_nn(hidden, w_up[...])
     grad = dot_nn(cot, w_down[...])
+    gate, up = gates[...].astype(F32), ups[...].astype(F32)
     sigmoid = 1.0 / (1.0 + jnp.exp(-gate))
-    silu = gate * sigmoid
-    active = (silu * up).astype(BF16)
     to_gate = (grad * up * (sigmoid * (1.0 + gate * (1.0 - sigmoid)))).astype(BF16)
-    to_up = (grad * silu).astype(BF16)
-    activated[...] = active
+    to_up = (grad * (gate * sigmoid)).astype(BF16)
     grads[:, :units] = to_gate
     grads[:, units:] = to_up
     back = (dot_nt(to_gate, w_gate[...]) + dot_nt(to_up, w_up[...])).astype(BF16)
-    out = dot_nt(active, w_down[...]).astype(BF16)
+    out = dot_nt(activated[...], w_down[...]).astype(BF16)
 
     @pl.when(near)
     def _():
@@ -162,32 +169,40 @@
         far_out[...] = out
 
 
-def middle(part, parts, hidden, cot, w_gate, w_up, w_down, held):
-    rows, width = hidden[0].shape
-    units = w_down.shape[1]
+def feed_forward(second, part, parts, tokens, whole, weights, held):
+    rows, width = tokens[0].shape
+    units = weights[0].shape[1]
     tile = min(rows, 256)
     steps = rows // tile
     near = pl.BlockSpec((tile, width), lambda i: (jnp.minimum(i, steps - 1), 0))
     far = pl.BlockSpec((tile, width), lambda i: (jnp.maximum(i - steps, 0), 0))
     weight = pl.BlockSpec((width, units), lambda i: (0, 0), pipeline_mode=pl.Buffered(1))
-    results = [pl.BlockSpec((tile, n * units), lambda i: (part * 2 * steps + i, 0)) for n in (1, 2)]
+
+    def of_whole(columns):
+        return pl.BlockSpec((tile, columns), lambda i: (part * 2 * steps + i, 0))
+
+    kept = (2 * units,) if second else (units,) * 3
+    first_held = 2 + len(whole) + len(weights)
+    products = 8 if second else 4
     return pl.pallas_call(
-        functools.partial(middle_kernel, steps),
+        functools.partial(second_kernel if second else first_kernel, steps),
         grid=(2 * steps,),
-        in_specs=[near, far, near, far, weight, weight, weight]
+        in_specs=[near, far]
+        + [of_whole(units)] * len(whole)
+        + [weight] * len(weights)
         + [pl.BlockSpec(memory_space=pl.ANY)] * len(held),
-        out_specs=results + [near, far] * 2,
-        out_shape=[jax.ShapeDtypeStruct((parts * 2 * rows, n * units), BF16) for n in (1, 2)]
-        + [jax.ShapeDtypeStruct((rows, width), BF16)] * 4,
-        input_output_aliases={7 + i: i for i in range(len(held))},
+        out_specs=[of_whole(n) for n in kept] + ([near, far] * 2 if second else []),
+        out_shape=[jax.ShapeDtypeStruct((parts * 2 * rows, n), BF16) for n in kept]
+        + [jax.ShapeDtypeStruct((rows, width), BF16)] * (4 if second else 0),
+        input_output_aliases={first_held + i: i for i in range(len(held))},
         compiler_params=pltpu.CompilerParams(vmem_limit_bytes=58 * 2**20),
         cost_estimate=pl.CostEstimate(
-            flops=24 * rows * width * units,
-            bytes_accessed=2 * (8 * rows * width + 3 * width * units + 6 * rows * units),
+            flops=2 * products * 2 * rows * width * units,
+            bytes_accessed=2 * (2 * rows * width + len(weights) * width * units + 10 * rows * units),
             transcendentals=2 * rows * units,
         ),
-        name="middle",
-    )(*hidden, *cot, w_gate, w_up, w_down, *held)
+        name="second_half" if second else "first_half",
+    )(*tokens, *whole, *weights, *held)
 
 
 def gradient_kernel(*refs, count, extra):
@@ -322,45 +337,73 @@
     def told_at_once(value):
         return lax.all_gather(lax.all_gather(value, "z", axis=0), ("a", "b", "c"), axis=0)
 
+    def in_plane(value):
+        value = value.reshape(2, count_b, *value.shape[1:])
+        mine = lax.dynamic_index_in_dim(value, ic, 0, keepdims=False)
+        far = shift_by(lax.dynamic_index_in_dim(value, 1 - ic, 0, keepdims=False), "c", 1)
+        value = in_order([mine, far], "c", 1)
+        pieces = [lax.dynamic_index_in_dim(value, ib, 0, keepdims=False)]
+        for s in range(1, count_b):
+            leaving = lax.dynamic_index_in_dim(value, (ib + s) % count_b, 0, keepdims=False)
+            pieces.append(shift_by(leaving, "b", s))
+        return pieces
+
+    def plane_rows(pieces):
+        value = in_order(pieces, "b", 0)
+        return value.reshape(-1, *value.shape[2:])
+
     bits = exchange_order()
-    hops = [tuple(bits[:-3]), *((b,) for b in bits[-3:])]
-    tails = told(tokens[:, length - 2 :, :].reshape(1, micro * 2, width), hops[0])
+    tap_count = conv_kernel.size
+    told_rows = jnp.concatenate(
+        [
+            tokens[:, length - 2 :, :].reshape(micro * 2, width).astype(F32),
+            jnp.pad(conv_kernel.reshape(1, tap_count), ((0, 0), (0, width - tap_count))),
+        ]
+    )[None]
+    pad_g, pad_u, pad_d = (jnp.pad(w, spare) for w in (ffn_gate, ffn_up, ffn_down))
     z_in = pieces_of(mixer_in, "z")
-    taps = pieces_of(conv_kernel, "z")
-    z_in, tails, taps, mixer_gate, ffn_gate_later, mixer_out = phase(
-        z_in, tails, taps, mixer_gate, ffn_gate, mixer_out
+    told_rows = told(told_rows, bits[:-3])
+    far_cotangent = pieces_of(cotangent.reshape(rows, width), "b")
+    z_in, told_rows, far_cotangent, mixer_gate, mixer_out, pad_g = phase(
+        z_in, told_rows, far_cotangent, mixer_gate, mixer_out, pad_g
     )
     w_in = rows_of(z_in)
     z_gate = pieces_of(mixer_gate, "z")
-    swap_g = swapped(jnp.pad(ffn_gate_later, spare))
-    tails = told(tails, hops[1])
-    z_gate, swap_g, tails, mixer_out, ffn_up_later, ffn_down, cotangent_later = phase(
-        z_gate, swap_g, tails, mixer_out, ffn_up, ffn_down, cotangent
-    )
+    near_g = near_pieces(pad_g, "z")
+    z_gate, near_g, told_rows, mixer_out, pad_u, pad_d = phase(z_gate, near_g, told_rows, mixer_out, pad_u, pad_d)
     w_gate = rows_of(z_gate)
     z_out = pieces_of(mixer_out, "z")
-    near_g = near_pieces(swap_g, "z")
-    tails = told(tails, hops[2])
-    z_out, near_g, tails, cotangent_later, ffn_up_later, ffn_down, w_in = phase(
-        z_out, near_g, tails, cotangent_later, ffn_up_later, ffn_down, w_in
-    )
+    z_g = far_pieces(pad_g, near_g, "z")
+    told_rows = told(told_rows, bits[-3:-2])
+    z_out, z_g, told_rows, pad_u, pad_d, w_in = phase(z_out, z_g, told_rows, pad_u, pad_d, w_in)
     w_out = rows_of(z_out)
-    z_g = far_pieces(swap_g, near_g, "z")
-    swap_u, swap_d = swapped(jnp.pad(ffn_up_later, spare)), swapped(jnp.pad(ffn_down, spare))
-    tails = told(tails, hops[3])
-    z_g, swap_u, swap_d, cotangent_later, tails, w_gate = phase(z_g, swap_u, swap_d, cotangent_later, tails, w_gate)
-    y_g = pieces_of(in_order(z_g, "z", 0), "a")
-    z_u = pieces_of(swap_u, "z")
-    y_d = pieces_of(swap_d, "a")
-    far_cotangent = pieces_of(cotangent_later.reshape(rows, width), "b")
-    kernel = jnp.concatenate(taps, axis=1)
+    plane_g = in_plane(in_order(z_g, "z", 0))
+    z_u = pieces_of(pad_u, "z")
+    told_rows = told(told_rows, bits[-2:])
+    plane_g, z_u, told_rows, pad_d, w_gate = phase(plane_g, z_u, told_rows, pad_d, w_gate)
+    y_g = pieces_of(plane_rows(plane_g), "a")
+    plane_u = in_plane(in_order(z_u, "z", 0))
+    z_d = pieces_of(pad_d, "z")
+    kernel = jnp.concatenate(
+        [
+            lax.dynamic_slice(
+                told_rows, (entry_of(place ^ (place - iz + (iz - s) % count_z)), micro * 2, 0), (1, 1, tap_count)
+            ).reshape(3, local)
+            for s in range(count_z)
+        ],
+        axis=1,
+    )
+    y_g, plane_u, z_d, w_out = phase(y_g, plane_u, z_d, w_out)
+    y_u = pieces_of(plane_rows(plane_u), "a")
+    plane_d = in_plane(in_order(z_d, "z", 0))
+    ffn_g = in_order(y_g, "a", 0).reshape(-1, units)
 
     tail_in = jnp.concatenate(
         [
-            lax.dynamic_slice(tails, (entry_of(before[m] ^ place), 2 * m, 0), (1, 2, width))[0]
+            lax.dynamic_slice(told_rows, (entry_of(before[m] ^ place), 2 * m, 0), (1, 2, width))[0]
             for m in range(micro)
         ]
-    ).astype(F32)
+    )
     local_in = tokens.reshape(rows, width).astype(F32)
     local_cot = cotangent.reshape(rows, width).astype(F32)
     scale_one = lax.rsqrt(jnp.mean(local_in * local_in, axis=1, keepdims=True) + EPSILON)
@@ -383,35 +426,36 @@
     normed_two = residual * scale_two
     hidden_own = (normed_two * norm2_gain).astype(BF16)
 
-    y_g, z_u, y_d, far_cotangent, hidden_own = phase(y_g, z_u, y_d, far_cotangent, hidden_own)
-    half_d = in_order(y_d, "a", 0)
-    near_d = near_pieces(half_d, "z")
-    y_u = pieces_of(in_order(z_u, "z", 0), "a")
-    ffn_g = in_order(y_g, "a", 0).reshape(-1, units)
 
     def with_core(pieces):
         return [v for piece in pieces for v in (piece, shift_by(piece, "c", 1))]
 
+    plane_d, y_u, ffn_g, hidden_own = phase(plane_d, y_u, ffn_g, hidden_own)
+    y_d = pieces_of(plane_rows(plane_d), "a")
+    ffn_u = in_order(y_u, "a", 0).reshape(-1, units)
+    far_hidden = pieces_of(hidden_own, "b")[1:]
+    hidden_parts = with_core([hidden_own])
+    kept = feed_forward(False, 0, count_b, hidden_parts, (), (ffn_g, ffn_u), ())
+    y_d, far_hidden, kept = phase(y_d, far_hidden, kept)
+    hidden_parts = hidden_parts + with_core(far_hidden)
+    for s in range(1, count_b):
+        kept = feed_forward(False, s, count_b, hidden_parts[2 * s : 2 * s + 2], (), (ffn_g, ffn_u), kept)
+    gates, ups, activated = kept
+    ffn_d = in_order(y_d, "a", 0).reshape(-1, units)
     cot_parts = with_core(far_cotangent)
-    hidden_parts = with_core([hidden_own])
-    far_hidden = pieces_of(hidden_own, "b")[1:]
-    near_d, y_u, half_d, ffn_g, cot_parts, hidden_parts, far_hidden = phase(
-        near_d, y_u, half_d, ffn_g, cot_parts, hidden_parts, far_hidden
-    )
-    ffn_d = in_order(far_pieces(half_d, near_d, "z"), "z", 1).reshape(-1, units)
-    ffn_u = in_order(y_u, "a", 0).reshape(-1, units)
-    hidden_parts = hidden_parts + with_core(far_hidden)
+    other = 1 - ia
+    leaving_down = gradient_half(other, cot_parts, activated, units)
+    leaving_down, cot_parts, hidden_parts = phase(leaving_down, cot_parts, hidden_parts)
+    come_down = shift_by(leaving_down, "a", 1)
     held, backs, outs = (), [], []
     for s in range(count_b):
-        pair = slice(2 * s, 2 * s + 2)
-        *held, near_back, far_back, near_out, far_out = middle(
-            s, count_b, hidden_parts[pair], cot_parts[pair], ffn_g, ffn_u, ffn_d, held
+        pair = cot_parts[2 * s : 2 * s + 2]
+        *held, near_back, far_back, near_out, far_out = feed_forward(
+            True, s, count_b, pair, (gates, ups, activated), (ffn_g, ffn_u, ffn_d), held
         )
         backs.append((near_back, shift_by(far_back, "c", 1)))
         outs.append((near_out, shift_by(far_out, "c", 1)))
-    activated, grads = held
-
-    other = 1 - ia
+    grads = held[0]
 
     def to_owners(sums):
         return [(near.astype(F32) + far.astype(F32)).astype(BF16) for near, far in sums[1:]]
@@ -419,23 +463,24 @@
     def passed(values):
         return [shift_by(v, "b", -1 - i) for i, v in enumerate(values)]
 
+    def over_z(stay, come):
+        return lax.psum_scatter(joined([stay, come]).astype(BF16), "z", scatter_dimension=0, tiled=True)
+
     leaving_gate = gradient_half(other, hidden_parts, grads, units)
-    leaving_gate, backs, outs, hidden_parts, cot_parts = phase(leaving_gate, backs, outs, hidden_parts, cot_parts)
+    leaving_gate, come_down, backs, outs, hidden_parts, cot_parts = phase(
+        leaving_gate, come_down, backs, outs, hidden_parts, cot_parts
+    )
     come_gate, came_back = shift_by(leaving_gate, "a", 1), passed(to_owners(backs))
     leaving_up = gradient_half(other, hidden_parts, grads, units, 1)
-    leaving_down = gradient_half(other, cot_parts, activated, units)
+    stay_down = gradient_half(ia, cot_parts, activated, units)
     stay_gate = gradient_half(ia, hidden_parts, grads, units)
     stay_up = gradient_half(ia, hidden_parts, grads, units, 1)
-    stay_down = gradient_half(ia, cot_parts, activated, units)
     leaving_out = to_owners(outs)
-    come_gate, came_back, leaving_up, leaving_down, stay_gate, stay_up, stay_down, outs, leaving_out = phase(
-        come_gate, came_back, leaving_up, leaving_down, stay_gate, stay_up, stay_down, outs, leaving_out
+    come_gate, came_back, leaving_up, stay_down, stay_gate, stay_up, outs, leaving_out = phase(
+        come_gate, came_back, leaving_up, stay_down, stay_gate, stay_up, outs, leaving_out
     )
     come_up, came_out = shift_by(leaving_up, "a", 1), passed(leaving_out)
-
-    def over_z(stay, come):
-        return lax.psum_scatter(joined([stay, come]).astype(BF16), "z", scatter_dimension=0, tiled=True)
-
+    scattered_down = over_z(stay_down, come_down)
     grad_hidden_two = joined([*backs[0], *came_back])
 
     grad_gain_two = jnp.sum(grad_hidden_two * normed_two, axis=0)
@@ -475,21 +520,18 @@
 
     blocked = turned(blocked, 2).reshape(micro * 2, channels).astype(BF16)
     gate_split = split(hidden_one, grad_gating)
-    blocked, come_up, came_out, out_split, gate_split, grad_mixed, leaving_down = phase(
-        blocked, come_up, came_out, out_split, gate_split, grad_mixed, leaving_down
+    from_gating = dot_nt(grad_gating, w_gate)
+    blocked, come_up, came_out, out_split, gate_split, grad_mixed, from_gating = phase(
+        blocked, come_up, came_out, out_split, gate_split, grad_mixed, from_gating
     )
     everyone = told_at_once(blocked)
+    scattered_gate = over_z(stay_gate, come_gate)
     out_c, gate_c = over_c(out_split), over_c(gate_split)
-    everyone, out_c, gate_c, grad_mixed, leaving_down, come_gate, come_up = phase(
-        everyone, out_c, gate_c, grad_mixed, leaving_down, come_gate, come_up
-    )
-
-    def over_z(stay, come):
-        return lax.psum_scatter(joined([stay, come]).astype(BF16), "z", scatter_dimension=0, tiled=True)
-
-    come_down = shift_by(leaving_down, "a", 1)
+    everyone, out_c, gate_c, grad_mixed, scattered_down = phase(everyone, out_c, gate_c, grad_mixed, scattered_down)
     out_b = parted(out_c, "b", 1)
-    scattered_gate, scattered_up = over_z(stay_gate, come_gate), over_z(stay_up, come_up)
+    gate_a = parted(gate_c, "a", 0)
+    down_home = home(scattered_down)
+    scattered_up = over_z(stay_up, come_up)
     into_one = kernel[1] * (keep_one * grad_mixed)
     into_two = kernel[2] * (keep_two * grad_mixed)
     arrived = jnp.stack(
@@ -506,44 +548,42 @@
     from_two = jnp.concatenate([into_two[:, 2:], arrived[:, :1], jnp.zeros_like(arrived[:, :1])], axis=1)
     grad_signal = (kernel[0] * grad_mixed + from_one + from_two).astype(BF16).reshape(rows, channels)
     in_split = split(hidden_one, grad_signal)
-    grad_hidden_one = dot_nt(grad_signal, w_in) + dot_nt(grad_gating, w_gate)
+    grad_hidden_one = dot_nt(grad_signal, w_in) + from_gating
     grad_gain_one = jnp.sum(grad_hidden_one * normed_one, axis=0)
     grad_norm_one = grad_hidden_one * norm1_gain
     inner_one = jnp.mean(grad_norm_one * normed_one, axis=1, keepdims=True)
     input_grad = grad_residual + scale_one * (grad_norm_one - normed_one * inner_one)
-    come_down, out_b, in_split, gate_c, input_grad, scattered_gate, grad_gain_one, outs = phase(
-        come_down, out_b, in_split, gate_c, input_grad, scattered_gate, grad_gain_one, outs
+    out_b, gate_a, in_split, input_grad, down_home, grad_gain_one, outs, scattered_gate = phase(
+        out_b, gate_a, in_split, input_grad, down_home, grad_gain_one, outs, scattered_gate
     )
     in_c = over_c(in_split)
-    gate_b = parted(gate_c, "b", 1)
+    middle = channels // 2
+    in_a = parted([t[..., :middle] for t in in_c], "a", 0)
+    in_b = parted([t[..., middle:] for t in in_c], "b", 1)
+    gate_b = parted(gate_a, "b", 0)
     out_a = parted(out_b, "a", 0)
-    gate_home = swapped(scattered_gate, True)
-    scattered_down = over_z(stay_down, come_down)
+    gate_home = home(scattered_gate)
     output = (joined([*outs[0], *came_out]) + residual).astype(BF16)
-    in_c, gate_b, out_a, gate_home, scattered_up, output = phase(
-        in_c, gate_b, out_a, gate_home, scattered_up, output
-    )
-    in_b = parted(in_c, "b", 1)
-    gate_a = parted(gate_b, "a", 0)
-    out_z = columns_home(out_a)
-    up_home = swapped(scattered_up, True)
-    in_b, gate_a, out_z, up_home, scattered_down = phase(in_b, gate_a, out_z, up_home, scattered_down)
-    in_a = parted(in_b, "a", 0)
-    gate_z = columns_home(gate_a)
-    down_home = swapped(scattered_down, True)
     small = jnp.concatenate(
         [grad_gain_one[None], grad_gain_two[None], turned(grad_kernel.reshape(3, count_z, local), 1)]
     )
-    small = lax.all_gather(after(small, scattered_down), EVERY, axis=0)
-    in_a, gate_z, down_home = phase(in_a, gate_z, down_home)
-    in_z = columns_home(in_a)
+    small = lax.all_gather(small, EVERY, axis=0)
+    in_a, in_b, gate_b, out_a, gate_home, scattered_up, output = phase(
+        in_a, in_b, gate_b, out_a, gate_home, scattered_up, output
+    )
+    in_a, in_b = parted(in_a, "b", 0), parted(in_b, "a", 0)
+    up_home = home(scattered_up)
+    two_z = columns_home([jnp.concatenate([joined(out_a), joined(gate_b)], axis=0)])
+    in_a, in_b, two_z, small, up_home = phase(in_a, in_b, two_z, small, up_home)
+    in_z = columns_home([jnp.concatenate([joined(in_a), joined(in_b)], axis=1)])
     share = width // (4 * count_b * count_z)
     gains = lax.dynamic_slice_in_dim(small[:, :2], place * share, share, axis=2)
     tap_grads = lax.dynamic_slice_in_dim(
         small[:, 2:], (iz * 4 * count_b + place // count_z) * share, share, axis=2
     )
     gains, tap_grads = jnp.sum(gains, axis=0), jnp.sum(tap_grads, axis=0)
-    grad_out, grad_gate_w, grad_in_w = (joined(t) for t in (out_z, gate_z, in_z))
+    grad_out, grad_gate_w = jnp.split(joined(two_z), 2)
+    grad_in_w = joined(in_z)
     hidden_units = ffn_gate.shape[1]
     grad_ffg, grad_ffu, grad_down = (g[:, :hidden_units].astype(F32) for g in (gate_home, up_home, down_home))
 

time: 975 us -> 878 us (0.901)
  waiting for transfers between devices: 422 us -> 347 us
  starting transfers between devices: 118 us -> 68 us
  Pallas kernels: 145 us -> 160 us
  matrix products: 51 us -> 38.9 us
  local copies, waits for them, and re-layouts: 61 us -> 72.3 us
    ppermute x6 -> x3, waiting for transfers between devices: 73.4 us -> 23 us  [home(): return lax.ppermute(block, ('b', 'c', 'z'), moves)]
    ppermute x57 -> x59, starting transfers between devices: 99.4 us -> 59.1 us  [shift_by(): lax.ppermute(value, axis, [(i, (i + amount) % size) for i in range(size)])]
    all_gather x1, waiting for transfers between devices: 18.6 us -> 0.01 us  [per_device(): small = lax.all_gather(small, EVERY, axis=0)]
    reduce_scatter x3, waiting for transfers between devices: 13.3 us -> 0.01 us  [over_z(): lax.psum_scatter(joined([stay, come]).astype(BF16), 'z', scatter_dimensio...]
    ppermute x57 -> x59, waiting for transfers between devices: 274 us -> 287 us  [shift_by(): lax.ppermute(value, axis, [(i, (i + amount) % size) for i in range(size)])]
    pallas_call x2 -> x4, Pallas kernels: 78.9 us -> 91.6 us  [feed_forward(): pl.pallas_call(functools.partial(second_kernel if second else first_kerne...]
    another operation x6 -> x15, other arithmetic: 9.59 us -> 21.9 us  [in_order(): jnp.stack([jnp.where(first, pieces[0], pieces[1]), jnp.where(first, piece...]
    unnamed x157 -> x225, local copies, waits for them, and re-layouts: 18.1 us -> 21.4 us
  transfers between devices with their start and end apart: 75 -> 74, of which waited for: 32 -> 31; matrix products, arithmetic and copies ran while one was open for 18% -> 23% of each run, Pallas kernels for 15% -> 17%
where the time goes in v3:
time: 878 us; the launch traced here: 862 us
  waiting for transfers between devices  347 us (40%)
  Pallas kernels  160 us (18%)
  other arithmetic  120 us (14%)
  local copies, waits for them, and re-layouts  72.3 us (8%)
  starting transfers between devices  68 us (8%)
  matrix products  38.9 us (4%)
  between operations  29.5 us (3%)
  blocking collectives  27.1 us (3%)
    ppermute x59, waiting for transfers between devices, shift_by(): lax.ppermute(value, axis, [(i, (i + amount) % size) for i in range(size)])  287 us
    pallas_call x4, Pallas kernels, feed_forward(): pl.pallas_call(functools.partial(second_kernel if second else first_kerne...  91.6 us
    ppermute x59, starting transfers between devices, shift_by(): lax.ppermute(value, axis, [(i, (i + amount) % size) for i in range(size)])  59.1 us
    pallas_call x6, Pallas kernels, gradient_half(): pl.pallas_call(functools.partial(gradient_kernel, count=count, extra=len(...  49 us
    ppermute x5, waiting for transfers between devices, partner(): return lax.ppermute(value, EVERY, [(i, i ^ bit) for i in range(count)])  36.6 us
    ppermute x3, waiting for transfers between devices, home(): return lax.ppermute(block, ('b', 'c', 'z'), moves)  23 us
    squeeze x18, local copies, waits for them, and re-layouts, slices(): return [lax.dynamic_index_in_dim(t, i, dim, keepdims=False) for t in terms]  22.4 us
    dot_general x4, matrix products, dot_nn(): lax.dot_general(left, right, (((1,), (0,)), ((), ())), preferred_element_...  21.9 us
  transfers between devices with their start and end apart: 74, of which 31 were waited for; matrix products, arithmetic and copies ran while one was open for 23% of the time, Pallas kernels for 17%

profile of v3, /device:TPU:30, one launch (start us, length us, event | category | flops | bytes accessed | tf_op | source)
XLA Modules:
  0.0 861.7 jit_solution(12984373944461680560)
XLA Ops:
  10.1 4.3 collective-permute-done.3
  20.6 15.8 %collective-permute-done.4 = f32[2,9,1792]{2,1,0:T(8,128)S(1)} collective-permute-done((f32[2,9,1792]{2,1,0:T(8,128)S(1)}, f32[2,9,1792]{2,1,0:T(8,128)S(1)}, u32[]{:S(2)}, u32[]{:S(2)}) %collective-permute-start.4) | collective-permute-done | bytes 129056 | tf_op jit(solution)/shard_map/ppermute | solution.py:114
  36.4 9.7 %collective-permute-done.1 = bf16[224,448]{1,0:T(8,128)(2,1)S(1)} collective-permute-done((bf16[224,448]{1,0:T(8,128)(2,1)}, bf16[224,448]{1,0:T(8,128)(2,1)S(1)}, u32[]{:S(2)}, u32[]{:S(2)}) %collective-permute-start.1) | collective-permute-done | bytes 200736 | tf_op jit(solution)/shard_map/ppermute | solution.py:32
  46.1 3.1 collective-permute-done.5.refs_3_.refs_0_
  60.1 23.3 %collective-permute-done.6 = bf16[224,448]{1,0:T(8,128)(2,1)S(1)} collective-permute-done((bf16[224,448]{1,0:T(8,128)(2,1)}, bf16[224,448]{1,0:T(8,128)(2,1)S(1)}, u32[]{:S(2)}, u32[]{:S(2)}) %collective-permute-start.6) | collective-permute-done | bytes 200736 | tf_op jit(solution)/shard_map/ppermute | solution.py:32
  83.3 13.9 %collective-permute-done.7 = bf16[224,448]{1,0:T(8,128)(2,1)S(1)} collective-permute-done((bf16[224,448]{1,0:T(8,128)(2,1)}, bf16[224,448]{1,0:T(8,128)(2,1)S(1)}, u32[]{:S(2)}, u32[]{:S(2)}) %collective-permute-start.7) | collective-permute-done | bytes 200736 | tf_op jit(solution)/shard_map/ppermute | solution.py:32
  104.4 6.6 collective-permute-done.15
  111.1 7.8 collective-permute-done.11
  118.9 15.5 %collective-permute-done.12 = bf16[224,448]{1,0:T(8,128)(2,1)S(1)} collective-permute-done((bf16[224,448]{1,0:T(8,128)(2,1)}, bf16[224,448]{1,0:T(8,128)(2,1)S(1)}, u32[]{:S(2)}, u32[]{:S(2)}) %collective-permute-start.12) | collective-permute-done | bytes 200736 | tf_op jit(solution)/shard_map/ppermute | solution.py:32
  150.0 9.8 %collective-permute-done.21 = f32[8,9,1792]{2,0,1:T(8,128)S(1)} collective-permute-done((f32[8,9,1792]{2,0,1:T(8,128)S(1)}, f32[8,9,1792]{2,0,1:T(8,128)S(1)}, u32[]{:S(2)}, u32[]{:S(2)}) %collective-permute-start.21) | collective-permute-done | bytes 516128 | tf_op jit(solution)/shard_map/ppermute | solution.py:114
  163.8 5.4 fusion.2
  170.8 26.6 %collective-permute-done.19 = bf16[224,1280]{1,0:T(8,128)(2,1)} collective-permute-done((bf16[224,1280]{1,0:T(8,128)(2,1)}, bf16[224,1280]{1,0:T(8,128)(2,1)}, u32[]{:S(2)}, u32[]{:S(2)}) %collective-permute-start.19) | collective-permute-done | bytes 573472 | tf_op jit(solution)/shard_map/ppermute | solution.py:32
  197.4 7.3 collective-permute-done.17
  222.1 9.0 %multiply_convert_fusion.2 = (bf16[4,128,1792]{2,1,0:T(8,128)(2,1)S(1)}, f32[4,128,1792]{2,1,0:T(8,128)}, f32[4,128,1792]{2,1,0:T(8,128)}) fusion(f32[4,128,1792]{2,1,0:T(8,128)S(1)} %copy-done.46, f32[4,2,1792]{2,1,0:T(2,128)S(1)} %reshape.354, f32[4,128]{1,0:T(4,128)S(1)} %get-tuple-element.479, f32[1792]{0:T(1024)S(1)} %get-tuple-element.386, ...), kind=kOutput, calls=%fused_computation.57 | convolution fusion | flops 3302096896 | bytes 21194752 | tf_op jit(solution)/shard_map/dot_general | solution.py:19
  231.1 25.1 %collective-permute-done.27 = bf16[224,1280]{1,0:T(8,128)(2,1)} collective-permute-done((bf16[224,1280]{1,0:T(8,128)(2,1)}, bf16[224,1280]{1,0:T(8,128)(2,1)}, u32[]{:S(2)}, u32[]{:S(2)}) %collective-permute-start.27) | collective-permute-done | bytes 573472 | tf_op jit(solution)/shard_map/ppermute | solution.py:32
  256.3 11.1 %collective-permute-done.23 = bf16[4,224,1280]{2,1,0:T(8,128)(2,1)} collective-permute-done((bf16[4,224,1280]{2,1,0:T(8,128)(2,1)}, bf16[4,224,1280]{2,1,0:T(8,128)(2,1)}, u32[]{:S(2)}, u32[]{:S(2)}) %collective-permute-start.23) | collective-permute-done | bytes 2293792 | tf_op jit(solution)/shard_map/ppermute | solution.py:32
  273.0 3.7 multiply_reduce_fusion.5
  276.6 4.0 select_bitcast_fusion.5
  285.4 23.1 %collective-permute-done.32 = bf16[2,224,1280]{2,1,0:T(8,128)(2,1)S(1)} collective-permute-done((bf16[2,224,1280]{2,1,0:T(8,128)(2,1)S(1)}, bf16[2,224,1280]{2,1,0:T(8,128)(2,1)S(1)}, u32[]{:S(2)}, u32[]{:S(2)}) %collective-permute-start.32) | collective-permute-done | bytes 1146912 | tf_op jit(solution)/shard_map/ppermute | solution.py:32
  308.5 15.3 %collective-permute-done.33 = bf16[4,224,1280]{2,1,0:T(8,128)(2,1)S(1)} collective-permute-done((bf16[4,224,1280]{2,1,0:T(8,128)(2,1)S(1)}, bf16[4,224,1280]{2,1,0:T(8,128)(2,1)S(1)}, u32[]{:S(2)}, u32[]{:S(2)}) %collective-permute-start.33) | collective-permute-done | bytes 2293792 | tf_op jit(solution)/shard_map/ppermute | solution.py:32
  330.9 15.6 %first_half.2 = (bf16[2048,1280]{1,0:T(8,128)(2,1)}, bf16[2048,1280]{1,0:T(8,128)(2,1)}, bf16[2048,1280]{1,0:T(8,128)(2,1)}) custom-call(bf16[512,1792]{1,0:T(8,128)(2,1)} %copy-done, bf16[512,1792]{1,0:T(8,128)(2,1)} %copy-done.2, bf16[1792,1280]{1,0:T(8,128)(2,1)} %bitcast.311, bf16[1792,1280]{1,0:T(8,128)(2,1)} %bitcast.315), custom_call_target="tpu_custom_call" | custom-call | flops 18790481920 | bytes 25952256 | tf_op jit(solution)/shard_map/first_half/pallas_call | solution.py:187
  346.4 18.9 %collective-permute-done.35.refs_0_.refs_3_ = bf16[512,1792]{1,0:T(8,128)(2,1)} collective-permute-done((bf16[512,1792]{1,0:T(8,128)(2,1)S(1)}, bf16[512,1792]{1,0:T(8,128)(2,1)}, u32[]{:S(2)}, u32[]{:S(2)}) %collective-permute-start.35) | collective-permute-done | bytes 1835040 | tf_op jit(solution)/shard_map/ppermute | solution.py:32
  365.4 12.7 %collective-permute-done.34 = bf16[4,224,1280]{2,1,0:T(8,128)(2,1)} collective-permute-done((bf16[4,224,1280]{2,1,0:T(8,128)(2,1)S(1)}, bf16[4,224,1280]{2,1,0:T(8,128)(2,1)}, u32[]{:S(2)}, u32[]{:S(2)}) %collective-permute-start.34) | collective-permute-done | bytes 2293792 | tf_op jit(solution)/shard_map/ppermute | solution.py:32
  385.9 16.0 %first_half.3 = (bf16[2048,1280]{1,0:T(8,128)(2,1)}, bf16[2048,1280]{1,0:T(8,128)(2,1)}, bf16[2048,1280]{1,0:T(8,128)(2,1)}) custom-call(bf16[512,1792]{1,0:T(8,128)(2,1)} %collective-permute-done.35.refs_0_.refs_3_, bf16[512,1792]{1,0:T(8,128)(2,1)} %copy-done.4, ...), custom_call_target="tpu_custom_call", output_to_operand_aliasing={{0}: (4, {}), {1}: (5, {}), {2}: (6, {})} | custom-call | flops 18790481920 | bytes 25952256 | tf_op jit(solution)/shard_map/first_half/pallas_call | solution.py:187
  403.5 9.0 %gradient_half.6 = bf16[896,1280]{1,0:T(8,128)(2,1)} custom-call(s32[1]{0:T(128)} %bitcast.35.refs_0_, bf16[512,1792]{1,0:T(8,128)(2,1)S(1)} %bitcast.289, bf16[512,1792]{1,0:T(8,128)(2,1)} %collective-permute-done.29.refs_2_.refs_1_, bf16[512,1792]{1,0:T(8,128)(2,1)S(1)} %copy-done.23, bf16[512,1792]{1,0:T(8,128)(2,1)} %collective-permute-done.30.refs_4_.refs_1_, ...), custom_call_target="tpu_custom_call" | custom-call | flops 4697620480 | bytes 11206656 | tf_op jit(solution)/shard_map/gradient_half/pallas_call | solution.py:227
  413.0 29.9 %second_half.2 = (bf16[2048,2560]{1,0:T(8,128)(2,1)}, bf16[512,1792]{1,0:T(8,128)(2,1)}, bf16[512,1792]{1,0:T(8,128)(2,1)}, bf16[512,1792]{1,0:T(8,128)(2,1)}, bf16[512,1792]{1,0:T(8,128)(2,1)}) custom-call(bf16[512,1792]{1,0:T(8,128)(2,1)} %bitcast.288, bf16[512,1792]{1,0:T(8,128)(2,1)} %collective-permute-done.29.refs_2_.refs_1_, ...), custom_call_target="tpu_custom_call" | custom-call | flops 37580963840 | bytes 30539776 | tf_op jit(solution)/shard_map/second_half/pallas_call | solution.py:187
  442.9 30.1 %second_half.3 = (bf16[2048,2560]{1,0:T(8,128)(2,1)}, bf16[512,1792]{1,0:T(8,128)(2,1)}, bf16[512,1792]{1,0:T(8,128)(2,1)}, bf16[512,1792]{1,0:T(8,128)(2,1)}, bf16[512,1792]{1,0:T(8,128)(2,1)}) custom-call(bf16[512,1792]{1,0:T(8,128)(2,1)} %copy-done.22, bf16[512,1792]{1,0:T(8,128)(2,1)} %collective-permute-done.30.refs_4_.refs_1_, ...), custom_call_target="tpu_custom_call", output_to_operand_aliasing={{0}: (8, {})} | custom-call | flops 37580963840 | bytes 30539776 | tf_op jit(solution)/shard_map/second_half/pallas_call | solution.py:187
  474.1 3.4 fusion.15.left
  479.0 7.7 gradient_half.7
  488.3 3.3 add_convert_fusion.5
  492.2 8.7 %gradient_half.8 = bf16[896,1280]{1,0:T(8,128)(2,1)} custom-call(s32[1]{0:T(128)} %bitcast.35.refs_0_, bf16[512,1792]{1,0:T(8,128)(2,1)S(1)} %copy-done.1, bf16[512,1792]{1,0:T(8,128)(2,1)S(1)} %copy-done.3, bf16[512,1792]{1,0:T(8,128)(2,1)} %collective-permute-done.35.refs_0_.refs_3_, bf16[512,1792]{1,0:T(8,128)(2,1)S(1)} %copy-done.5, ...), custom_call_target="tpu_custom_call" | custom-call | flops 4697620480 | bytes 11206656 | tf_op jit(solution)/shard_map/gradient_half/pallas_call | solution.py:227
  500.8 7.6 gradient_half.10
  509.8 7.7 gradient_half.11
  519.0 8.2 gradient_half.9
  527.2 3.2 add_convert_fusion.4
  530.4 3.1 collective-permute-done.44
  533.5 5.1 collective-permute-done.43
  540.7 3.6 add_convert_fusion.2
  545.0 5.2 multiply_reduce_fusion.3
  552.2 6.3 fusion.80
  558.6 6.5 fusion.89
  565.1 3.4 multiply_reduce_fusion.1
  572.7 6.6 split_gradient.3
  581.0 6.2 split_gradient.4
  587.3 5.4 fusion.90
  605.1 3.7 add_convert_fusion
  608.8 14.8 %all-gather = bf16[32,1792]{1,0:T(8,128)(2,1)S(1)} all-gather(bf16[8,1792]{1,0:T(8,128)(2,1)S(1)} %concatenate.88), channel_id=2, replica_groups=mesh['a'=2,'b'=2,'c'=2,'z'=4] {'z'}, dimensions={0}, use_global_device_ids=true | all-gather | bytes 143360 | tf_op jit(solution)/shard_map/all_gather | solution.py:338
  623.6 12.3 %all-gather.1 = bf16[32,8,1792]{2,1,0:T(8,128)(2,1)} all-gather(bf16[4,8,1792]{2,1,0:T(8,128)(2,1)S(1)} %bitcast.324), channel_id=3, replica_groups=mesh['a'=2,'b'=2,'c'=2,'z'=4] {'a','b','c'}, dimensions={0}, use_global_device_ids=true | all-gather | bytes 1032192 | tf_op jit(solution)/shard_map/all_gather | solution.py:338
  635.9 3.2 fusion.25
  640.1 3.0 fusion.26
  645.5 4.7 fusion.7
  655.0 5.2 fusion.10
  660.3 6.4 split_gradient.5
  666.7 7.9 fusion.20
  674.6 3.5 dynamic-slice_bitcast_fusion.2
  683.5 20.8 %collective-permute-done.51 = bf16[224,1280]{1,0:T(8,128)(2,1)} collective-permute-done((bf16[224,1280]{1,0:T(8,128)(2,1)}, bf16[224,1280]{1,0:T(8,128)(2,1)}, u32[]{:S(2)}, u32[]{:S(2)}) %collective-permute-start.51) | collective-permute-done | bytes 573472 | tf_op jit(solution)/shard_map/ppermute | solution.py:109
  719.9 4.2 add_convert_fusion.3
  729.9 3.0 collective-permute-start.54
  738.1 7.8 collective-permute-done.53
  745.9 10.7 %collective-permute-done.54 = bf16[2,224,896]{2,1,0:T(8,128)(2,1)} collective-permute-done((bf16[2,224,896]{2,1,0:T(8,128)(2,1)}, bf16[2,224,896]{2,1,0:T(8,128)(2,1)}, u32[]{:S(2)}, u32[]{:S(2)}) %collective-permute-start.54) | collective-permute-done | bytes 802848 | tf_op jit(solution)/shard_map/ppermute | solution.py:32
  781.3 10.6 %collective-permute-done.58 = bf16[224,896]{1,0:T(8,128)(2,1)S(1)} collective-permute-done((bf16[224,896]{1,0:T(8,128)(2,1)S(1)}, bf16[224,896]{1,0:T(8,128)(2,1)S(1)}, u32[]{:S(2)}, u32[]{:S(2)}) %collective-permute-start.58) | collective-permute-done | bytes 401440 | tf_op jit(solution)/shard_map/ppermute | solution.py:32
  799.1 18.4 %collective-permute-done.61 = bf16[448,448]{1,0:T(8,128)(2,1)S(1)} collective-permute-done((bf16[448,448]{1,0:T(8,128)(2,1)}, bf16[448,448]{1,0:T(8,128)(2,1)S(1)}, u32[]{:S(2)}, u32[]{:S(2)}) %collective-permute-start.61) | collective-permute-done | bytes 401440 | tf_op jit(solution)/shard_map/ppermute | solution.py:32
  823.0 11.5 %collective-permute-start.66 = (bf16[224,448]{1,0:T(8,128)(2,1)S(1)}, bf16[224,448]{1,0:T(8,128)(2,1)S(1)}, u32[]{:S(2)}, u32[]{:S(2)}) collective-permute-start(bf16[224,448]{1,0:T(8,128)(2,1)S(1)} %get-tuple-element.456), channel_id=1, source_target_pairs={{0,1},{1,2},{2,3},{3,0},{4,5},{5,6},{6,7},{7,4},{8,9},{9,10},{10,1... | collective-permute-start | bytes 602120 | tf_op jit(solution)/shard_map/ppermute | solution.py:32
  840.6 13.1 %collective-permute-done.65 = bf16[224,448]{1,0:T(8,128)(2,1)S(1)} collective-permute-done((bf16[224,448]{1,0:T(8,128)(2,1)S(1)}, bf16[224,448]{1,0:T(8,128)(2,1)S(1)}, u32[]{:S(2)}, u32[]{:S(2)}) %collective-permute-start.65) | collective-permute-done | bytes 200736 | tf_op jit(solution)/shard_map/ppermute | solution.py:32
  (511 shorter events, 193.4 us)
Async XLA Ops:
  7.2 128.6 %all-gather.9.cloned.1.call-start = ((), (), s32[]{:S(2)}) async-start(), calls=%async_computation.3 | async-start | bytes 7225344 | tf_op jit(solution)/shard_map/all_gather | solution.py:335
  7.2 42.0 %collective-permute-start.5 = (bf16[512,1792]{1,0:T(8,128)(2,1)}, bf16[512,1792]{1,0:T(8,128)(2,1)S(1)}, u32[]{:S(2)}, u32[]{:S(2)}) collective-permute-start(bf16[512,1792]{1,0:T(8,128)(2,1)} %bitcast.286), channel_id=1, source_target_pairs={{0,8},{8,0},{1,9},{9,1},{2,10},{10,2},{3,11},{11,3},{4,12},{12,4},... | collective-permute-start | bytes 5505032 | tf_op jit(solution)/shard_map/ppermute | solution.py:32
  14.5 21.9 %collective-permute-start.4 = (f32[2,9,1792]{2,1,0:T(8,128)S(1)}, f32[2,9,1792]{2,1,0:T(8,128)S(1)}, u32[]{:S(2)}, u32[]{:S(2)}) collective-permute-start(f32[2,9,1792]{2,1,0:T(8,128)S(1)} %pad_maximum_fusion.15), channel_id=1, source_target_pairs={{0,2},{1,3},{2,0},{3,1},{4,6},{5,7},{6,4},{7,5},{8,10},{9,11},{10,... | collective-permute-start | bytes 387080 | tf_op jit(solution)/shard_map/ppermute | solution.py:114
  14.9 21.5 %collective-permute-start = (bf16[224,448]{1,0:T(8,128)(2,1)}, bf16[224,448]{1,0:T(8,128)(2,1)S(1)}, u32[]{:S(2)}, u32[]{:S(2)}) collective-permute-start(bf16[224,448]{1,0:T(8,128)(2,1)} %param.18), channel_id=1, source_target_pairs={{0,1},{1,2},{2,3},{3,0},{4,5},{5,6},{6,7},{7,4},{8,9},{9,10},{10,1... | collective-permute-start | bytes 602120 | tf_op jit(solution)/shard_map/ppermute | solution.py:32
  17.4 28.8 %collective-permute-start.1 = (bf16[224,448]{1,0:T(8,128)(2,1)}, bf16[224,448]{1,0:T(8,128)(2,1)S(1)}, u32[]{:S(2)}, u32[]{:S(2)}) collective-permute-start(bf16[224,448]{1,0:T(8,128)(2,1)} %param.18), channel_id=1, source_target_pairs={{0,2},{1,3},{2,0},{3,1},{4,6},{5,7},{6,4},{7,5},{8,10},{9,11},{10,... | collective-permute-start | bytes 602120 | tf_op jit(solution)/shard_map/ppermute | solution.py:32
  17.5 28.6 %collective-permute-start.2 = (bf16[224,448]{1,0:T(8,128)(2,1)}, bf16[224,448]{1,0:T(8,128)(2,1)}, u32[]{:S(2)}, u32[]{:S(2)}) collective-permute-start(bf16[224,448]{1,0:T(8,128)(2,1)} %param.18), channel_id=1, source_target_pairs={{0,3},{1,0},{2,1},{3,2},{4,7},{5,4},{6,5},{7,6},{8,11},{9,8},{10,9... | collective-permute-start | bytes 602120 | tf_op jit(solution)/shard_map/ppermute | solution.py:32
  51.5 145.9 %all-gather.11.cloned.1.call-start = ((), (), s32[]{:S(2)}) async-start(), calls=%async_computation.4 | async-start | bytes 7225344 | tf_op jit(solution)/shard_map/all_gather | solution.py:335
  51.5 45.7 %collective-permute-start.9 = (bf16[224,1280]{1,0:T(8,128)(2,1)S(1)}, bf16[224,1280]{1,0:T(8,128)(2,1)S(1)}, u32[]{:S(2)}, u32[]{:S(2)}) collective-permute-start(bf16[224,1280]{1,0:T(8,128)(2,1)S(1)} %pad.15), channel_id=1, source_target_pairs={{0,1},{1,2},{2,3},{3,0},{4,5},{5,6},{6,7},{7,4},{8,9},{9,10},{10,1... | collective-permute-start | bytes 1720328 | tf_op jit(solution)/shard_map/ppermute | solution.py:32
  51.8 46.2 %collective-permute-start.10 = (bf16[224,1280]{1,0:T(8,128)(2,1)S(1)}, bf16[224,1280]{1,0:T(8,128)(2,1)}, u32[]{:S(2)}, u32[]{:S(2)}) collective-permute-start(bf16[224,1280]{1,0:T(8,128)(2,1)S(1)} %pad.15), channel_id=1, source_target_pairs={{0,3},{1,0},{2,1},{3,2},{4,7},{5,4},{6,5},{7,6},{8,11},{9,8},{10,9... | collective-permute-start | bytes 1720328 | tf_op jit(solution)/shard_map/ppermute | solution.py:32
  53.6 29.7 %collective-permute-start.6 = (bf16[224,448]{1,0:T(8,128)(2,1)}, bf16[224,448]{1,0:T(8,128)(2,1)S(1)}, u32[]{:S(2)}, u32[]{:S(2)}) collective-permute-start(bf16[224,448]{1,0:T(8,128)(2,1)} %param.19), channel_id=1, source_target_pairs={{0,1},{1,2},{2,3},{3,0},{4,5},{5,6},{6,7},{7,4},{8,9},{9,10},{10,1... | collective-permute-start | bytes 602120 | tf_op jit(solution)/shard_map/ppermute | solution.py:32
  55.6 41.6 %collective-permute-start.7 = (bf16[224,448]{1,0:T(8,128)(2,1)}, bf16[224,448]{1,0:T(8,128)(2,1)S(1)}, u32[]{:S(2)}, u32[]{:S(2)}) collective-permute-start(bf16[224,448]{1,0:T(8,128)(2,1)} %param.19), channel_id=1, source_target_pairs={{0,2},{1,3},{2,0},{3,1},{4,6},{5,7},{6,4},{7,5},{8,10},{9,11},{10,... | collective-permute-start | bytes 602120 | tf_op jit(solution)/shard_map/ppermute | solution.py:32
  55.6 41.6 %collective-permute-start.8 = (bf16[224,448]{1,0:T(8,128)(2,1)}, bf16[224,448]{1,0:T(8,128)(2,1)S(1)}, u32[]{:S(2)}, u32[]{:S(2)}) collective-permute-start(bf16[224,448]{1,0:T(8,128)(2,1)} %param.19), channel_id=1, source_target_pairs={{0,3},{1,0},{2,1},{3,2},{4,7},{5,4},{6,5},{7,6},{8,11},{9,8},{10,9... | collective-permute-start | bytes 602120 | tf_op jit(solution)/shard_map/ppermute | solution.py:32
  100.3 167.1 %all-gather.13.cloned.1.call-start = ((), (), s32[]{:S(2)}) async-start(), calls=%async_computation.5 | async-start | bytes 7225344 | tf_op jit(solution)/shard_map/all_gather | solution.py:335
  100.3 35.5 %collective-permute-start.14 = (bf16[224,1280]{1,0:T(8,128)(2,1)S(1)}, bf16[224,1280]{1,0:T(8,128)(2,1)S(1)}, u32[]{:S(2)}, u32[]{:S(2)}) collective-permute-start(bf16[224,1280]{1,0:T(8,128)(2,1)S(1)} %collective-permute-done.9), channel_id=1, source_target_pairs={{0,1},{1,2},{2,3},{3,0},{4,5},{5,6},{6,7},{7,4},{8,9},{9,10},{10,1... | collective-permute-start | bytes 1720328 | tf_op jit(solution)/shard_map/ppermute | solution.py:32
  101.0 18.0 %collective-permute-start.11 = (bf16[224,448]{1,0:T(8,128)(2,1)}, bf16[224,448]{1,0:T(8,128)(2,1)S(1)}, u32[]{:S(2)}, u32[]{:S(2)}) collective-permute-start(bf16[224,448]{1,0:T(8,128)(2,1)} %param.21), channel_id=1, source_target_pairs={{0,1},{1,2},{2,3},{3,0},{4,5},{5,6},{6,7},{7,4},{8,9},{9,10},{10,1... | collective-permute-start | bytes 602120 | tf_op jit(solution)/shard_map/ppermute | solution.py:32
  103.6 30.9 %collective-permute-start.12 = (bf16[224,448]{1,0:T(8,128)(2,1)}, bf16[224,448]{1,0:T(8,128)(2,1)S(1)}, u32[]{:S(2)}, u32[]{:S(2)}) collective-permute-start(bf16[224,448]{1,0:T(8,128)(2,1)} %param.21), channel_id=1, source_target_pairs={{0,2},{1,3},{2,0},{3,1},{4,6},{5,7},{6,4},{7,5},{8,10},{9,11},{10,... | collective-permute-start | bytes 602120 | tf_op jit(solution)/shard_map/ppermute | solution.py:32
  104.4 30.1 %collective-permute-start.13 = (bf16[224,448]{1,0:T(8,128)(2,1)}, bf16[224,448]{1,0:T(8,128)(2,1)S(1)}, u32[]{:S(2)}, u32[]{:S(2)}) collective-permute-start(bf16[224,448]{1,0:T(8,128)(2,1)} %param.21), channel_id=1, source_target_pairs={{0,3},{1,0},{2,1},{3,2},{4,7},{5,4},{6,5},{7,6},{8,11},{9,8},{10,9... | collective-permute-start | bytes 602120 | tf_op jit(solution)/shard_map/ppermute | solution.py:32
  138.0 497.9 %reduce-scatter.4.cloned.1.call-start = ((), (), s32[]{:S(2)}) async-start(), calls=%async_computation.6 | async-start | bytes 2867200 | tf_op jit(solution)/shard_map/reduce_scatter | solution.py:467
  144.5 16.4 %collective-permute-start.16 = (bf16[2,224,1280]{2,1,0:T(8,128)(2,1)S(1)}, bf16[2,224,1280]{2,1,0:T(8,128)(2,1)S(1)}, u32[]{:S(2)}, u32[]{:S(2)}) collective-permute-start(bf16[2,224,1280]{2,1,0:T(8,128)(2,1)S(1)} %dynamic-slice_bitcast_fusion.6), channel_id=1, source_target_pairs={{0,4},{4,0},{1,5},{5,1},{2,6},{6,2},{3,7},{7,3},{8,12},{12,8},{9,1... | collective-permute-start | bytes 3440648 | tf_op jit(solution)/shard_map/ppermute | solution.py:32
  148.0 22.8 %collective-permute-start.18 = (bf16[224,1280]{1,0:T(8,128)(2,1)}, bf16[224,1280]{1,0:T(8,128)(2,1)}, u32[]{:S(2)}, u32[]{:S(2)}) collective-permute-start(bf16[224,1280]{1,0:T(8,128)(2,1)} %pad.16), channel_id=1, source_target_pairs={{0,1},{1,2},{2,3},{3,0},{4,5},{5,6},{6,7},{7,4},{8,9},{9,10},{10,1... | collective-permute-start | bytes 1720328 | tf_op jit(solution)/shard_map/ppermute | solution.py:32
  148.0 49.3 %collective-permute-start.19 = (bf16[224,1280]{1,0:T(8,128)(2,1)}, bf16[224,1280]{1,0:T(8,128)(2,1)}, u32[]{:S(2)}, u32[]{:S(2)}) collective-permute-start(bf16[224,1280]{1,0:T(8,128)(2,1)} %pad.16), channel_id=1, source_target_pairs={{0,2},{1,3},{2,0},{3,1},{4,6},{5,7},{6,4},{7,5},{8,10},{9,11},{10,... | collective-permute-start | bytes 1720328 | tf_op jit(solution)/shard_map/ppermute | solution.py:32
  148.1 49.3 %collective-permute-start.20 = (bf16[224,1280]{1,0:T(8,128)(2,1)}, bf16[224,1280]{1,0:T(8,128)(2,1)}, u32[]{:S(2)}, u32[]{:S(2)}) collective-permute-start(bf16[224,1280]{1,0:T(8,128)(2,1)} %pad.16), channel_id=1, source_target_pairs={{0,3},{1,0},{2,1},{3,2},{4,7},{5,4},{6,5},{7,6},{8,11},{9,8},{10,9... | collective-permute-start | bytes 1720328 | tf_op jit(solution)/shard_map/ppermute | solution.py:32
  162.3 42.3 %collective-permute-start.17 = (bf16[2,224,1280]{2,1,0:T(8,128)(2,1)}, bf16[2,224,1280]{2,1,0:T(8,128)(2,1)}, u32[]{:S(2)}, u32[]{:S(2)}) collective-permute-start(bf16[2,224,1280]{2,1,0:T(8,128)(2,1)} %get-tuple-element.436), channel_id=1, source_target_pairs={{0,8},{8,0},{1,9},{9,1},{2,10},{10,2},{3,11},{11,3},{4,12},{12,4},... | collective-permute-start | bytes 3440648 | tf_op jit(solution)/shard_map/ppermute | solution.py:32
  204.6 26.5 %collective-permute-start.26 = (bf16[224,1280]{1,0:T(8,128)(2,1)}, bf16[224,1280]{1,0:T(8,128)(2,1)}, u32[]{:S(2)}, u32[]{:S(2)}) collective-permute-start(bf16[224,1280]{1,0:T(8,128)(2,1)} %pad.17), channel_id=1, source_target_pairs={{0,1},{1,2},{2,3},{3,0},{4,5},{5,6},{6,7},{7,4},{8,9},{9,10},{10,1... | collective-permute-start | bytes 1720328 | tf_op jit(solution)/shard_map/ppermute | solution.py:32
  205.1 51.1 %collective-permute-start.27 = (bf16[224,1280]{1,0:T(8,128)(2,1)}, bf16[224,1280]{1,0:T(8,128)(2,1)}, u32[]{:S(2)}, u32[]{:S(2)}) collective-permute-start(bf16[224,1280]{1,0:T(8,128)(2,1)} %pad.17), channel_id=1, source_target_pairs={{0,2},{1,3},{2,0},{3,1},{4,6},{5,7},{6,4},{7,5},{8,10},{9,11},{10,... | collective-permute-start | bytes 1720328 | tf_op jit(solution)/shard_map/ppermute | solution.py:32
  206.6 49.7 %collective-permute-start.28 = (bf16[224,1280]{1,0:T(8,128)(2,1)}, bf16[224,1280]{1,0:T(8,128)(2,1)}, u32[]{:S(2)}, u32[]{:S(2)}) collective-permute-start(bf16[224,1280]{1,0:T(8,128)(2,1)} %pad.17), channel_id=1, source_target_pairs={{0,3},{1,0},{2,1},{3,2},{4,7},{5,4},{6,5},{7,6},{8,11},{9,8},{10,9... | collective-permute-start | bytes 1720328 | tf_op jit(solution)/shard_map/ppermute | solution.py:32
  215.4 52.0 %collective-permute-start.23 = (bf16[4,224,1280]{2,1,0:T(8,128)(2,1)}, bf16[4,224,1280]{2,1,0:T(8,128)(2,1)}, u32[]{:S(2)}, u32[]{:S(2)}) collective-permute-start(bf16[4,224,1280]{2,1,0:T(8,128)(2,1)} %bitcast.23), channel_id=1, source_target_pairs={{0,16},{16,0},{1,17},{17,1},{2,18},{18,2},{3,19},{19,3},{4,20},{20... | collective-permute-start | bytes 6881288 | tf_op jit(solution)/shard_map/ppermute | solution.py:32
  220.5 35.8 %collective-permute-start.25 = (bf16[2,224,1280]{2,1,0:T(8,128)(2,1)S(1)}, bf16[2,224,1280]{2,1,0:T(8,128)(2,1)}, u32[]{:S(2)}, u32[]{:S(2)}) collective-permute-start(bf16[2,224,1280]{2,1,0:T(8,128)(2,1)S(1)} %get-tuple-element.428), channel_id=1, source_target_pairs={{0,8},{8,0},{1,9},{9,1},{2,10},{10,2},{3,11},{11,3},{4,12},{12,4},... | collective-permute-start | bytes 3440648 | tf_op jit(solution)/shard_map/ppermute | solution.py:32
  271.6 52.2 %collective-permute-start.33 = (bf16[4,224,1280]{2,1,0:T(8,128)(2,1)S(1)}, bf16[4,224,1280]{2,1,0:T(8,128)(2,1)S(1)}, u32[]{:S(2)}, u32[]{:S(2)}) collective-permute-start(bf16[4,224,1280]{2,1,0:T(8,128)(2,1)S(1)} %bitcast.299), channel_id=1, source_target_pairs={{0,16},{16,0},{1,17},{17,1},{2,18},{18,2},{3,19},{19,3},{4,20},{20... | collective-permute-start | bytes 6881288 | tf_op jit(solution)/shard_map/ppermute | solution.py:32
  281.0 27.5 %collective-permute-start.32 = (bf16[2,224,1280]{2,1,0:T(8,128)(2,1)S(1)}, bf16[2,224,1280]{2,1,0:T(8,128)(2,1)S(1)}, u32[]{:S(2)}, u32[]{:S(2)}) collective-permute-start(bf16[2,224,1280]{2,1,0:T(8,128)(2,1)S(1)} %get-tuple-element.422), channel_id=1, source_target_pairs={{0,8},{8,0},{1,9},{9,1},{2,10},{10,2},{3,11},{11,3},{4,12},{12,4},... | collective-permute-start | bytes 3440648 | tf_op jit(solution)/shard_map/ppermute | solution.py:32
  323.8 41.6 %collective-permute-start.35 = (bf16[512,1792]{1,0:T(8,128)(2,1)S(1)}, bf16[512,1792]{1,0:T(8,128)(2,1)}, u32[]{:S(2)}, u32[]{:S(2)}) collective-permute-start(bf16[512,1792]{1,0:T(8,128)(2,1)S(1)} %multiply_convert_fusion.1.refs_0_.refs_1_), channel_id=1, source_target_pairs={{0,8},{8,0},{1,9},{9,1},{2,10},{10,2},{3,11},{11,3},{4,12},{12,4},... | collective-permute-start | bytes 5505032 | tf_op jit(solution)/shard_map/ppermute | solution.py:32
  325.7 52.4 %collective-permute-start.34 = (bf16[4,224,1280]{2,1,0:T(8,128)(2,1)S(1)}, bf16[4,224,1280]{2,1,0:T(8,128)(2,1)}, u32[]{:S(2)}, u32[]{:S(2)}) collective-permute-start(bf16[4,224,1280]{2,1,0:T(8,128)(2,1)S(1)} %bitcast.303), channel_id=1, source_target_pairs={{0,16},{16,0},{1,17},{17,1},{2,18},{18,2},{3,19},{19,3},{4,20},{20... | collective-permute-start | bytes 6881288 | tf_op jit(solution)/shard_map/ppermute | solution.py:32
  378.1 23.9 %collective-permute-start.29 = (bf16[512,1792]{1,0:T(8,128)(2,1)}, bf16[512,1792]{1,0:T(8,128)(2,1)}, u32[]{:S(2)}, u32[]{:S(2)}) collective-permute-start(bf16[512,1792]{1,0:T(8,128)(2,1)} %bitcast.287), channel_id=1, source_target_pairs={{0,4},{4,0},{1,5},{5,1},{2,6},{6,2},{3,7},{7,3},{8,12},{12,8},{9,1... | collective-permute-start | bytes 5505032 | tf_op jit(solution)/shard_map/ppermute | solution.py:32
  378.6 23.4 %collective-permute-start.30 = (bf16[512,1792]{1,0:T(8,128)(2,1)}, bf16[512,1792]{1,0:T(8,128)(2,1)}, u32[]{:S(2)}, u32[]{:S(2)}) collective-permute-start(bf16[512,1792]{1,0:T(8,128)(2,1)} %copy-done.22), channel_id=1, source_target_pairs={{0,4},{4,0},{1,5},{5,1},{2,6},{6,2},{3,7},{7,3},{8,12},{12,8},{9,1... | collective-permute-start | bytes 5505032 | tf_op jit(solution)/shard_map/ppermute | solution.py:32
  412.5 74.3 %collective-permute-start.38 = (bf16[896,1280]{1,0:T(8,128)(2,1)}, bf16[896,1280]{1,0:T(8,128)(2,1)}, u32[]{:S(2)}, u32[]{:S(2)}) collective-permute-start(bf16[896,1280]{1,0:T(8,128)(2,1)} %gradient_half.6), channel_id=1, source_target_pairs={{0,16},{16,0},{1,17},{17,1},{2,18},{18,2},{3,19},{19,3},{4,20},{20... | collective-permute-start | bytes 6881288 | tf_op jit(solution)/shard_map/ppermute | solution.py:32
  442.9 43.8 %collective-permute-start.39 = (bf16[512,1792]{1,0:T(8,128)(2,1)}, bf16[512,1792]{1,0:T(8,128)(2,1)}, u32[]{:S(2)}, u32[]{:S(2)}) collective-permute-start(bf16[512,1792]{1,0:T(8,128)(2,1)} %get-tuple-element.272), channel_id=1, source_target_pairs={{0,4},{4,0},{1,5},{5,1},{2,6},{6,2},{3,7},{7,3},{8,12},{12,8},{9,1... | collective-permute-start | bytes 5505032 | tf_op jit(solution)/shard_map/ppermute | solution.py:32
  473.0 13.7 %collective-permute-start.40 = (bf16[512,1792]{1,0:T(8,128)(2,1)}, bf16[512,1792]{1,0:T(8,128)(2,1)}, u32[]{:S(2)}, u32[]{:S(2)}) collective-permute-start(bf16[512,1792]{1,0:T(8,128)(2,1)} %get-tuple-element.274), channel_id=1, source_target_pairs={{0,4},{4,0},{1,5},{5,1},{2,6},{6,2},{3,7},{7,3},{8,12},{12,8},{9,1... | collective-permute-start | bytes 5505032 | tf_op jit(solution)/shard_map/ppermute | solution.py:32
  486.8 51.9 %collective-permute-start.43 = (bf16[896,1280]{1,0:T(8,128)(2,1)S(1)}, bf16[896,1280]{1,0:T(8,128)(2,1)S(1)}, u32[]{:S(2)}, u32[]{:S(2)}) collective-permute-start(bf16[896,1280]{1,0:T(8,128)(2,1)S(1)} %gradient_half.7), channel_id=1, source_target_pairs={{0,16},{16,0},{1,17},{17,1},{2,18},{18,2},{3,19},{19,3},{4,20},{20... | collective-permute-start | bytes 6881288 | tf_op jit(solution)/shard_map/ppermute | solution.py:32
  491.6 41.9 %collective-permute-start.44 = (bf16[512,1792]{1,0:T(8,128)(2,1)}, bf16[512,1792]{1,0:T(8,128)(2,1)S(1)}, u32[]{:S(2)}, u32[]{:S(2)}) collective-permute-start(bf16[512,1792]{1,0:T(8,128)(2,1)} %add_convert_fusion.5), channel_id=1, source_target_pairs={{0,8},{8,0},{1,9},{9,1},{2,10},{10,2},{3,11},{11,3},{4,12},{12,4},... | collective-permute-start | bytes 5505032 | tf_op jit(solution)/shard_map/ppermute | solution.py:32
  538.7 53.9 %collective-permute-start.45 = (bf16[896,1280]{1,0:T(8,128)(2,1)}, bf16[896,1280]{1,0:T(8,128)(2,1)}, u32[]{:S(2)}, u32[]{:S(2)}) collective-permute-start(bf16[896,1280]{1,0:T(8,128)(2,1)} %gradient_half.8), channel_id=1, source_target_pairs={{0,16},{16,0},{1,17},{17,1},{2,18},{18,2},{3,19},{19,3},{4,20},{20... | collective-permute-start | bytes 6881288 | tf_op jit(solution)/shard_map/ppermute | solution.py:32
  540.1 52.5 %collective-permute-start.46 = (bf16[512,1792]{1,0:T(8,128)(2,1)}, bf16[512,1792]{1,0:T(8,128)(2,1)}, u32[]{:S(2)}, u32[]{:S(2)}) collective-permute-start(bf16[512,1792]{1,0:T(8,128)(2,1)} %add_convert_fusion.4), channel_id=1, source_target_pairs={{0,8},{8,0},{1,9},{9,1},{2,10},{10,2},{3,11},{11,3},{4,12},{12,4},... | collective-permute-start | bytes 5505032 | tf_op jit(solution)/shard_map/ppermute | solution.py:32
  544.3 139.2 %reduce-scatter.6.cloned.1.call-start = ((), (), s32[]{:S(2)}) async-start(), calls=%async_computation.7 | async-start | bytes 2867200 | tf_op jit(solution)/shard_map/reduce_scatter | solution.py:467
  570.9 167.0 %reduce-scatter.8.cloned.1.call-start = ((), (), s32[]{:S(2)}) async-start(), calls=%async_computation.8 | async-start | bytes 2867200 | tf_op jit(solution)/shard_map/reduce_scatter | solution.py:467
  592.6 43.3 %collective-permute-start.47 = (bf16[4,224,1792]{2,1,0:T(8,128)(2,1)}, bf16[4,224,1792]{2,1,0:T(8,128)(2,1)}, u32[]{:S(2)}, u32[]{:S(2)}) collective-permute-start(bf16[4,224,1792]{2,1,0:T(8,128)(2,1)} %get-tuple-element.305), channel_id=1, source_target_pairs={{0,4},{4,0},{1,5},{5,1},{2,6},{6,2},{3,7},{7,3},{8,12},{12,8},{9,1... | collective-permute-start | bytes 9633800 | tf_op jit(solution)/shard_map/ppermute | solution.py:32
  592.7 43.2 %collective-permute-start.48 = (bf16[4,224,1792]{2,1,0:T(8,128)(2,1)}, bf16[4,224,1792]{2,1,0:T(8,128)(2,1)}, u32[]{:S(2)}, u32[]{:S(2)}) collective-permute-start(bf16[4,224,1792]{2,1,0:T(8,128)(2,1)} %get-tuple-element.307), channel_id=1, source_target_pairs={{0,4},{4,0},{1,5},{5,1},{2,6},{6,2},{3,7},{7,3},{8,12},{12,8},{9,1... | collective-permute-start | bytes 9633800 | tf_op jit(solution)/shard_map/ppermute | solution.py:32
  608.8 187.4 %all-gather.15.cloned.1.call-start = ((), (), s32[]{:S(2)}) async-start(), calls=%async_computation.9 | async-start | bytes 1892352 | tf_op jit(solution)/shard_map/all_gather | solution.py:570
  639.1 65.3 %collective-permute-start.49 = (bf16[2,224,1792]{2,1,0:T(8,128)(2,1)}, bf16[2,224,1792]{2,1,0:T(8,128)(2,1)}, u32[]{:S(2)}, u32[]{:S(2)}) collective-permute-start(bf16[2,224,1792]{2,1,0:T(8,128)(2,1)} %fusion.25), channel_id=1, source_target_pairs={{0,8},{8,0},{1,9},{9,1},{2,10},{10,2},{3,11},{11,3},{4,12},{12,4},... | collective-permute-start | bytes 4816904 | tf_op jit(solution)/shard_map/ppermute | solution.py:32
  643.1 61.3 %collective-permute-start.50 = (bf16[2,224,1792]{2,1,0:T(8,128)(2,1)}, bf16[2,224,1792]{2,1,0:T(8,128)(2,1)}, u32[]{:S(2)}, u32[]{:S(2)}) collective-permute-start(bf16[2,224,1792]{2,1,0:T(8,128)(2,1)} %fusion.26), channel_id=1, source_target_pairs={{0,16},{16,0},{1,17},{17,1},{2,18},{18,2},{3,19},{19,3},{4,20},{20... | collective-permute-start | bytes 4816904 | tf_op jit(solution)/shard_map/ppermute | solution.py:32
  653.1 51.3 %collective-permute-start.51 = (bf16[224,1280]{1,0:T(8,128)(2,1)}, bf16[224,1280]{1,0:T(8,128)(2,1)}, u32[]{:S(2)}, u32[]{:S(2)}) collective-permute-start(bf16[224,1280]{1,0:T(8,128)(2,1)} %reduce-scatter.4.cloned.1.call-done), channel_id=1, source_target_pairs={{0,0},{8,1},{4,2},{12,3},{1,4},{9,5},{5,6},{13,7},{2,8},{10,9},{6,... | collective-permute-start | bytes 1720328 | tf_op jit(solution)/shard_map/ppermute | solution.py:109
  704.3 19.7 %collective-permute-start.52 = (bf16[4,224,1792]{2,1,0:T(8,128)(2,1)}, bf16[4,224,1792]{2,1,0:T(8,128)(2,1)}, u32[]{:S(2)}, u32[]{:S(2)}) collective-permute-start(bf16[4,224,1792]{2,1,0:T(8,128)(2,1)} %get-tuple-element.326), channel_id=1, source_target_pairs={{0,4},{4,0},{1,5},{5,1},{2,6},{6,2},{3,7},{7,3},{8,12},{12,8},{9,1... | collective-permute-start | bytes 9633800 | tf_op jit(solution)/shard_map/ppermute | solution.py:32
  706.7 31.3 %collective-permute-start.55 = (bf16[224,1792]{1,0:T(8,128)(2,1)}, bf16[224,1792]{1,0:T(8,128)(2,1)}, u32[]{:S(2)}, u32[]{:S(2)}) collective-permute-start(bf16[224,1792]{1,0:T(8,128)(2,1)} %fusion.50), channel_id=1, source_target_pairs={{0,8},{8,0},{1,9},{9,1},{2,10},{10,2},{3,11},{11,3},{4,12},{12,4},... | collective-permute-start | bytes 2408456 | tf_op jit(solution)/shard_map/ppermute | solution.py:32
  709.3 28.8 %collective-permute-start.56 = (bf16[224,1792]{1,0:T(8,128)(2,1)}, bf16[224,1792]{1,0:T(8,128)(2,1)}, u32[]{:S(2)}, u32[]{:S(2)}) collective-permute-start(bf16[224,1792]{1,0:T(8,128)(2,1)} %fusion.51), channel_id=1, source_target_pairs={{0,16},{16,0},{1,17},{17,1},{2,18},{18,2},{3,19},{19,3},{4,20},{20... | collective-permute-start | bytes 2408456 | tf_op jit(solution)/shard_map/ppermute | solution.py:32
  710.2 27.7 %collective-permute-start.57 = (bf16[224,1280]{1,0:T(8,128)(2,1)}, bf16[224,1280]{1,0:T(8,128)(2,1)}, u32[]{:S(2)}, u32[]{:S(2)}) collective-permute-start(bf16[224,1280]{1,0:T(8,128)(2,1)} %reduce-scatter.6.cloned.1.call-done), channel_id=1, source_target_pairs={{0,0},{8,1},{4,2},{12,3},{1,4},{9,5},{5,6},{13,7},{2,8},{10,9},{6,... | collective-permute-start | bytes 1720328 | tf_op jit(solution)/shard_map/ppermute | solution.py:109
  727.3 18.5 %collective-permute-start.53 = (bf16[2,224,896]{2,1,0:T(8,128)(2,1)}, bf16[2,224,896]{2,1,0:T(8,128)(2,1)}, u32[]{:S(2)}, u32[]{:S(2)}) collective-permute-start(bf16[2,224,896]{2,1,0:T(8,128)(2,1)} %fusion.48), channel_id=1, source_target_pairs={{0,16},{16,0},{1,17},{17,1},{2,18},{18,2},{3,19},{19,3},{4,20},{20... | collective-permute-start | bytes 2408456 | tf_op jit(solution)/shard_map/ppermute | solution.py:32
  729.9 26.7 %collective-permute-start.54 = (bf16[2,224,896]{2,1,0:T(8,128)(2,1)}, bf16[2,224,896]{2,1,0:T(8,128)(2,1)}, u32[]{:S(2)}, u32[]{:S(2)}) collective-permute-start(bf16[2,224,896]{2,1,0:T(8,128)(2,1)} %fusion.49), channel_id=1, source_target_pairs={{0,8},{8,0},{1,9},{9,1},{2,10},{10,2},{3,11},{11,3},{4,12},{12,4},... | collective-permute-start | bytes 2408456 | tf_op jit(solution)/shard_map/ppermute | solution.py:32
  768.6 23.3 %collective-permute-start.58 = (bf16[224,896]{1,0:T(8,128)(2,1)S(1)}, bf16[224,896]{1,0:T(8,128)(2,1)S(1)}, u32[]{:S(2)}, u32[]{:S(2)}) collective-permute-start(bf16[224,896]{1,0:T(8,128)(2,1)S(1)} %fusion.54), channel_id=1, source_target_pairs={{0,8},{8,0},{1,9},{9,1},{2,10},{10,2},{3,11},{11,3},{4,12},{12,4},... | collective-permute-start | bytes 1204232 | tf_op jit(solution)/shard_map/ppermute | solution.py:32
  771.1 25.1 %collective-permute-start.59 = (bf16[224,896]{1,0:T(8,128)(2,1)}, bf16[224,896]{1,0:T(8,128)(2,1)}, u32[]{:S(2)}, u32[]{:S(2)}) collective-permute-start(bf16[224,896]{1,0:T(8,128)(2,1)} %fusion.55), channel_id=1, source_target_pairs={{0,16},{16,0},{1,17},{17,1},{2,18},{18,2},{3,19},{19,3},{4,20},{20... | collective-permute-start | bytes 1204232 | tf_op jit(solution)/shard_map/ppermute | solution.py:32
  772.1 47.6 %collective-permute-start.63 = (bf16[224,1280]{1,0:T(8,128)(2,1)}, bf16[224,1280]{1,0:T(8,128)(2,1)}, u32[]{:S(2)}, u32[]{:S(2)}) collective-permute-start(bf16[224,1280]{1,0:T(8,128)(2,1)} %reduce-scatter.8.cloned.1.call-done), channel_id=1, source_target_pairs={{0,0},{8,1},{4,2},{12,3},{1,4},{9,5},{5,6},{13,7},{2,8},{10,9},{6,... | collective-permute-start | bytes 1720328 | tf_op jit(solution)/shard_map/ppermute | solution.py:109
  778.8 20.3 %collective-permute-start.60 = (bf16[448,448]{1,0:T(8,128)(2,1)}, bf16[448,448]{1,0:T(8,128)(2,1)S(1)}, u32[]{:S(2)}, u32[]{:S(2)}) collective-permute-start(bf16[448,448]{1,0:T(8,128)(2,1)} %get-tuple-element.448), channel_id=1, source_target_pairs={{0,3},{1,0},{2,1},{3,2},{4,7},{5,4},{6,5},{7,6},{8,11},{9,8},{10,9... | collective-permute-start | bytes 1204232 | tf_op jit(solution)/shard_map/ppermute | solution.py:32
  780.3 37.2 %collective-permute-start.61 = (bf16[448,448]{1,0:T(8,128)(2,1)}, bf16[448,448]{1,0:T(8,128)(2,1)S(1)}, u32[]{:S(2)}, u32[]{:S(2)}) collective-permute-start(bf16[448,448]{1,0:T(8,128)(2,1)} %get-tuple-element.447), channel_id=1, source_target_pairs={{0,2},{1,3},{2,0},{3,1},{4,6},{5,7},{6,4},{7,5},{8,10},{9,11},{10,... | collective-permute-start | bytes 1204232 | tf_op jit(solution)/shard_map/ppermute | solution.py:32
  792.7 24.9 %collective-permute-start.62 = (bf16[448,448]{1,0:T(8,128)(2,1)}, bf16[448,448]{1,0:T(8,128)(2,1)S(1)}, u32[]{:S(2)}, u32[]{:S(2)}) collective-permute-start(bf16[448,448]{1,0:T(8,128)(2,1)} %get-tuple-element.446), channel_id=1, source_target_pairs={{0,1},{1,2},{2,3},{3,0},{4,5},{5,6},{6,7},{7,4},{8,9},{9,10},{10,1... | collective-permute-start | bytes 1204232 | tf_op jit(solution)/shard_map/ppermute | solution.py:32
  823.0 17.6 %collective-permute-start.66 = (bf16[224,448]{1,0:T(8,128)(2,1)S(1)}, bf16[224,448]{1,0:T(8,128)(2,1)S(1)}, u32[]{:S(2)}, u32[]{:S(2)}) collective-permute-start(bf16[224,448]{1,0:T(8,128)(2,1)S(1)} %get-tuple-element.456), channel_id=1, source_target_pairs={{0,1},{1,2},{2,3},{3,0},{4,5},{5,6},{6,7},{7,4},{8,9},{9,10},{10,1... | collective-permute-start | bytes 602120 | tf_op jit(solution)/shard_map/ppermute | solution.py:32
  834.5 19.2 %collective-permute-start.65 = (bf16[224,448]{1,0:T(8,128)(2,1)S(1)}, bf16[224,448]{1,0:T(8,128)(2,1)S(1)}, u32[]{:S(2)}, u32[]{:S(2)}) collective-permute-start(bf16[224,448]{1,0:T(8,128)(2,1)S(1)} %get-tuple-element.455), channel_id=1, source_target_pairs={{0,2},{1,3},{2,0},{3,1},{4,6},{5,7},{6,4},{7,5},{8,10},{9,11},{10,... | collective-permute-start | bytes 602120 | tf_op jit(solution)/shard_map/ppermute | solution.py:32
  834.9 18.8 %collective-permute-start.64 = (bf16[224,448]{1,0:T(8,128)(2,1)S(1)}, bf16[224,448]{1,0:T(8,128)(2,1)S(1)}, u32[]{:S(2)}, u32[]{:S(2)}) collective-permute-start(bf16[224,448]{1,0:T(8,128)(2,1)S(1)} %slice.255), channel_id=1, source_target_pairs={{0,3},{1,0},{2,1},{3,2},{4,7},{5,4},{6,5},{7,6},{8,11},{9,8},{10,9... | collective-permute-start | bytes 602120 | tf_op jit(solution)/shard_map/ppermute | solution.py:32
  (119 other events, 1337.8 us)
Sparse Core Ops, SparseCore 0:
  51.6 46.0 all-gather.8
  100.4 47.4 all-gather.10
  150.4 63.2 all-gather.12
  544.4 46.4 reduce-scatter.3
  593.1 48.1 reduce-scatter.5
  643.5 64.4 reduce-scatter.7
  713.7 61.8 all-gather.14
